TPU v7x, 512 devices: a whole 4x8x8 slice. The times are simulated.
512 devices in a mesh: gx: 4 (over x), gy: 128 (over z, y, core).
Axes of the slice: x: 4, y: 8, z: 8, core: 2. Of those that a mesh axis runs over, the one named last changes fastest.
Arguments:
- velocity: float32 [3, 1536, 32, 512], P(None, 'gy', None, 'gx'), may hold values from -6 to 6
- old_advection: float32 [3, 1536, 32, 512], P(None, 'gy', None, 'gx'), may hold values from -12 to 12
- lower_gap: float32 [1536], P('gy'), may hold values from 0.35 to 1.4
- upper_gap: float32 [1536], P('gy'), may hold values from 0.35 to 1.4, as said below
Outputs:
- new_velocity: float32 [3, 1536, 32, 512], P(None, 'gy', None, 'gx')
- advection: float32 [3, 1536, 32, 512], P(None, 'gy', None, 'gx')
Inputs may be any that keep to these rules, and one draw needn't show every extreme that they name: upper_gap of every point equals lower_gap of the next point.
All inputs are finite; a program needn't handle non-finite values.
Results may differ from a plain program's by a relative error of at most 0.0075.
Values sent between devices are 32-bit elements; how exact they have to be, the bound alone decides.
A program may use at most 128 MiB of HBM per device.

v0:
```python
import jax
import jax.numpy as jnp
from jax import lax
from jax.sharding import PartitionSpec as P

STIFF = 1024


STENCIL = (0.8, -0.2, 4.0 / 105.0, -1.0 / 280.0)
GAMMA = 5.0 / 12.0
ZETA = -17.0 / 60.0


def extended(array, sides, width, wrap):
    for axis, dim in sides:
        size, length = (lax.axis_size(axis), array.shape[dim])
        up = [(i, (i + 1) % size) for i in range(size if wrap else size - 1)]
        down = [(j, i) for i, j in up]
        last = lax.slice_in_dim(array, length - width, length, axis=dim)
        first = lax.slice_in_dim(array, 0, width, axis=dim)
        before = lax.ppermute(last, axis, up)
        after = lax.ppermute(first, axis, down)
        array = jnp.concatenate([before, array, after], axis=dim)
    return array


def prefix(value, axis, join, neutral, backward):
    count, mine = (lax.axis_size(axis), lax.axis_index(axis))
    pieces = jax.tree.map(lambda part: lax.all_gather(part, axis), value)
    if backward:
        pieces = jax.tree.map(lambda part: part[::-1], pieces)
        mine = count - 1 - mine
    total = jax.tree.map(
        lambda part, zero: jnp.full_like(part, 0) + jnp.asarray(zero, part.dtype), value, neutral
    )

    def turn(position, total):
        longer = join(total, jax.tree.map(lambda part: part[position], pieces))
        return jax.tree.map(lambda new, old: jnp.where(position < mine, new, old), longer, total)

    return lax.fori_loop(0, count - 1, turn, total)


def stream_slope(padded, planes):
    summed = STENCIL[0] * (padded[..., 5 : 5 + planes] - padded[..., 3 : 3 + planes])
    for offset in range(2, 5):
        summed = summed + STENCIL[offset - 1] * (
            padded[..., 4 + offset : 4 + offset + planes]
            - padded[..., 4 - offset : 4 - offset + planes]
        )
    return summed


def roll_slope(values, along_axis):
    summed = STENCIL[0] * (jnp.roll(values, -1, along_axis) - jnp.roll(values, 1, along_axis))
    for offset in range(2, 5):
        summed = summed + STENCIL[offset - 1] * (
            jnp.roll(values, -offset, along_axis) - jnp.roll(values, offset, along_axis)
        )
    return summed


def compose(earlier, latter):
    return (latter[0] * earlier[0], latter[1] + latter[0] * earlier[1])


def chain_ratio(earlier, latter):
    product = jnp.dot(latter, earlier, precision=lax.Precision.HIGHEST)
    return product / jnp.max(jnp.abs(product))


def ratio_matrix(cross_term, top_right, bottom_left):
    unit_entry = jnp.ones((), jnp.float32)
    return jnp.stack([jnp.stack([cross_term, top_right]), jnp.stack([bottom_left, unit_entry])])


def shards(velocity, old_advection, lower_gap, upper_gap):
    planes = velocity.shape[3]
    padded = extended(velocity, (("gx", 3),), 4, True)
    stream = stream_slope(padded, planes)
    spanwise = roll_slope(velocity, 2)
    rimmed = extended(velocity, (("gy", 1),), 1, False)
    gap_sum = lower_gap + upper_gap
    normal_slope = (rimmed[:, 2:] - rimmed[:, :-2]) / gap_sum[None, :, None, None]
    advection = -(
        velocity[0][None] * stream + velocity[1][None] * normal_slope + velocity[2][None] * spanwise
    )
    forcing = velocity + GAMMA * advection + ZETA * old_advection
    lower_coef = -2.0 * STIFF / (gap_sum * lower_gap)
    upper_coef = -2.0 * STIFF / (gap_sum * upper_gap)
    diagonal = 1.0 - lower_coef - upper_coef
    below_band = lower_coef.at[0].set(0.0)
    above_band = upper_coef.at[-1].set(0.0)
    rows_here = velocity.shape[1]
    line_values = forcing.reshape(3, rows_here, -1)
    solved = lax.linalg.tridiagonal_solve(
        jnp.stack([below_band] * 3),
        jnp.stack([diagonal] * 3),
        jnp.stack([above_band] * 3),
        line_values,
    )
    columns = jnp.zeros((rows_here, 2), jnp.float32)
    columns = columns.at[0, 0].set(lower_coef[0]).at[rows_here - 1, 1].set(upper_coef[-1])
    spikes = lax.linalg.tridiagonal_solve(below_band, diagonal, above_band, columns)
    left_spike = spikes[:, 0]
    right_spike = spikes[:, 1]
    left_first = left_spike[0]
    left_last = left_spike[-1]
    right_first = right_spike[0]
    right_last = right_spike[-1]
    cross_term = left_last * right_first - right_last * left_first
    unit_matrix = jnp.eye(2, dtype=jnp.float32)
    below_prefix = prefix(
        ratio_matrix(cross_term, right_last, -left_first), "gy", chain_ratio, unit_matrix, False
    )
    below_ratio = below_prefix[0, 1] / below_prefix[1, 1]
    first_solved = solved[:, 0]
    last_solved = solved[:, -1]
    lower_denom = 1.0 - left_first * below_ratio
    lower_step = (
        jnp.reshape(-left_last / lower_denom, (1, 1)),
        last_solved + left_last * below_ratio / lower_denom * first_solved,
    )
    identity_step = (jnp.ones((1, 1), jnp.float32), jnp.zeros_like(first_solved))
    below_offset = prefix(lower_step, "gy", compose, identity_step, False)[1]
    first_base = (first_solved - left_first * below_offset) / lower_denom
    first_slope = right_first / lower_denom
    upper_step = (jnp.reshape(-first_slope, (1, 1)), first_base)
    above_value = prefix(upper_step, "gy", compose, identity_step, True)[1]
    first_value = first_base - first_slope * above_value
    below_value = below_offset - below_ratio * first_value
    finished = (
        solved
        - below_value[:, None, :] * left_spike[None, :, None]
        - above_value[:, None, :] * right_spike[None, :, None]
    )
    return (finished.reshape(velocity.shape), advection)


def solution(mesh):
    return jax.shard_map(
        shards,
        mesh=mesh,
        in_specs=(P(None, "gy", None, "gx"), P(None, "gy", None, "gx"), P("gy"), P("gy")),
        out_specs=(P(None, "gy", None, "gx"), P(None, "gy", None, "gx")),
        check_vma=False,
    )
```

profile of v0, /device:TPU:6, one launch (start us, length us, event | category | flops | bytes accessed | tf_op | source)
XLA Modules:
  0.0 1278.0 jit_solution(14658627915192162866)
XLA Ops:
  10.0 3.6 collective-permute-start.3
  15.5 7.8 collective-permute-start.1
  23.7 1.9 collective-permute-start
  25.6 1.6 fusion.71
  27.2 1.6 fusion.73
  28.9 1.7 fusion.75
  30.6 1.7 fusion.77
  32.2 1.9 slice_bitcast_fusion.3
  63.1 7.1 subtract_divide_fusion.11
  71.5 1.9 multiply_subtract_fusion.10
  78.1 53.6 %all-gather.2 = f32[128,2,2]{2,1,0:T(2,128)S(1)} all-gather(f32[1,2,2]{2,1,0:T(2,128)S(1)} %maximum_bitcast_fusion), channel_id=2, replica_groups=mesh['gx'=4,'gy'=128] {'gy'}, dimensions={0}, use_global_device_ids=true | all-gather | bytes 2064 | tf_op jit(solution)/shard_map/all_gather | solution.py:29
  131.7 192.8 %while.45 = (s32[]{:T(128)}, f32[2,2]{1,0:T(2,128)S(1)}, s32[]{:T(128)}, f32[128,2,2]{2,1,0:T(2,128)S(1)}, s32[]{:T(128)}) while((s32[]{:T(128)}, f32[2,2]{1,0:T(2,128)S(1)}, s32[]{:T(128)}, f32[128,2,2]{2,1,0:T(2,128)S(1)}, s32[]{:T(128)}) %tuple.192), condition=%wide.region_2.3_spmd, body=%wide.region_0.2_spmd.sunk | while | flops 114 | bytes 2203 | solution.py:41
  350.9 5.0 multiply_add_fusion
  356.4 7.9 constant_dynamic-update-slice_fusion.10
  371.5 249.9 %all-reduce.3 = (f32[128]{0:T(128)S(1)}, f32[128]{0:T(128)S(1)}) all-reduce(f32[128]{0:T(128)S(1)} %dynamic-update-slice.8, f32[128]{0:T(128)S(1)} %dynamic-update-slice.9), channel_id=1, replica_groups=mesh['gx'=4,'gy'=128] {'gy'}, use_global_device_ids=true, to_apply=%add.1 | all-reduce | flops 256 | bytes 2048
  621.4 273.5 %while.46 = (s32[]{:T(128)}, f32[3,4096]{1,0:T(4,128)S(1)}, s32[]{:T(128)}, f32[128,3,4096]{2,1,0:T(4,128)}, f32[128,1,1]{0,2,1:T(1,128)S(1)}, /*index=5*/s32[]{:T(128)}, s32[]{:T(128)}) while((s32[]{:T(128)}, f32[3,4096]{1,0:T(4,128)S(1)}, s32[]{:T(128)}, f32[128,3,4096]{2,1,0:T(4,128)}, f32[128,1,1]{0,2,1:T(1,128)S(1)}, ...), condition=%wide.region_4.5_spmd.clone, body=%wide.region_3.4_spmd.clone.sunk | while | flops 49156 | bytes 147581 | solution.py:41
  622.0 1.6 fusion.89
  624.2 1.6 fusion.89
  626.3 1.6 fusion.89
  894.9 9.2 fusion.52
  904.8 7.9 subtract_bitcast_fusion.1
  912.7 71.5 %all-gather.9.cloned.1.call-done = f32[128,3,4096]{2,1,0:T(4,128)} async-done(((f32[1,3,4096]{2,1,0:T(4,128)}), f32[128,3,4096]{2,1,0:T(4,128)}) %all-gather.9.cloned.1.call-update) | async-done | bytes 6291472 | tf_op jit(solution)/shard_map/all_gather | solution.py:29
  984.2 9.8 reverse
  994.0 276.0 %while.47 = (s32[]{:T(128)}, f32[3,4096]{1,0:T(4,128)S(1)}, s32[]{:T(128)}, f32[128,3,4096]{2,1,0:T(4,128)}, f32[128,1,1]{0,2,1:T(1,128)S(1)}, /*index=5*/s32[]{:T(128)}, s32[]{:T(128)}) while((s32[]{:T(128)}, f32[3,4096]{1,0:T(4,128)S(1)}, s32[]{:T(128)}, f32[128,3,4096]{2,1,0:T(4,128)}, f32[128,1,1]{0,2,1:T(1,128)S(1)}, ...), condition=%wide.region_6.7_spmd.clone, body=%wide.region_5.6_spmd.clone.sunk | while | flops 49156 | bytes 147581 | solution.py:41
  (846 shorter events, 755.7 us)
Async XLA Ops:
  7.2 28.4 %copy-start = (f32[3,12,32,128]{3,2,1,0:T(8,128)S(1)}, f32[3,12,32,128]{3,2,1,0:T(8,128)}, u32[]{:S(2)}) copy-start(f32[3,12,32,128]{3,2,1,0:T(8,128)} %param.18) | copy-start | bytes 1769476
  7.2 31.6 %copy-start.11 = (f32[12]{0:T(128)S(1)}, f32[12]{0:T(128)}, u32[]{:S(2)}) copy-start(f32[12]{0:T(128)} %param.21) | copy-start | bytes 148
  7.2 31.6 %copy-start.10 = (f32[12]{0:T(128)S(1)}, f32[12]{0:T(128)}, u32[]{:S(2)}) copy-start(f32[12]{0:T(128)} %param.20) | copy-start | bytes 148
  7.2 614.2 %all-gather.7.cloned.1.call-start = ((), (), s32[]{:S(2)}) async-start(), calls=%async_computation | async-start | bytes 8454144 | tf_op jit(solution)/shard_map/all_gather | solution.py:29
  8.8 342.2 %collective-permute-start.2 = (f32[3,1,32,128]{3,2,1,0:T(8,128)}, f32[3,1,32,128]{3,2,1,0:T(8,128)}, u32[]{:S(2)}, u32[]{:S(2)}) collective-permute-start(f32[3,1,32,128]{3,2,1,0:T(8,128)} %get-tuple-element.436), channel_id=1, source_target_pairs={{1,0},{2,1},{3,2},{4,3},{5,4},{6,5},{7,6},{8,7},{9,8},{10,9},{11,1... | collective-permute-start | bytes 147464 | tf_op jit(solution)/shard_map/ppermute | solution.py:22
  10.0 340.9 %collective-permute-start.3 = (f32[3,1,32,128]{3,2,1,0:T(8,128)}, f32[3,1,32,128]{3,2,1,0:T(8,128)}, u32[]{:S(2)}, u32[]{:S(2)}) collective-permute-start(f32[3,1,32,128]{3,2,1,0:T(8,128)} %get-tuple-element.437), channel_id=1, source_target_pairs={{0,1},{1,2},{2,3},{3,4},{4,5},{5,6},{6,7},{7,8},{8,9},{9,10},{10,1... | collective-permute-start | bytes 147464 | tf_op jit(solution)/shard_map/ppermute | solution.py:21
  15.5 334.2 %collective-permute-start.1 = (f32[3,12,32,4]{2,1,3,0:T(8,128)S(1)}, f32[3,12,32,4]{2,1,3,0:T(8,128)}, u32[]{:S(2)}, u32[]{:S(2)}) collective-permute-start(f32[3,12,32,4]{2,1,3,0:T(8,128)S(1)} %copy.21), channel_id=1, source_target_pairs={{0,128},{128,256},{256,384},{384,0},{1,129},{129,257},{257,385},{3... | collective-permute-start | bytes 55304 | tf_op jit(solution)/shard_map/ppermute | solution.py:21
  23.7 325.8 %collective-permute-start = (f32[3,12,32,4]{2,1,3,0:T(8,128)S(1)}, f32[3,12,32,4]{2,1,3,0:T(8,128)S(1)}, u32[]{:S(2)}, u32[]{:S(2)}) collective-permute-start(f32[3,12,32,4]{2,1,3,0:T(8,128)S(1)} %copy.20), channel_id=1, source_target_pairs={{128,0},{256,128},{384,256},{0,384},{129,1},{257,129},{385,257},{1... | collective-permute-start | bytes 55304 | tf_op jit(solution)/shard_map/ppermute | solution.py:22
  355.9 548.3 %copy-start.2 = (f32[1,2]{0,1:T(2,128)S(1)}, f32[1,2]{0,1:T(2,128)}, u32[]{:S(2)}) copy-start(f32[1,2]{0,1:T(2,128)} %get-tuple-element.393) | copy-start | bytes 28
  355.9 548.2 %copy-start.3 = (f32[1,2]{0,1:T(2,128)S(1)}, f32[1,2]{0,1:T(2,128)}, u32[]{:S(2)}) copy-start(f32[1,2]{0,1:T(2,128)} %get-tuple-element.394) | copy-start | bytes 28
  355.9 548.2 %copy-start.4 = (f32[1,2]{0,1:T(2,128)S(1)}, f32[1,2]{0,1:T(2,128)}, u32[]{:S(2)}) copy-start(f32[1,2]{0,1:T(2,128)} %get-tuple-element.395) | copy-start | bytes 28
  356.0 548.2 %copy-start.5 = (f32[1,2]{0,1:T(2,128)S(1)}, f32[1,2]{0,1:T(2,128)}, u32[]{:S(2)}) copy-start(f32[1,2]{0,1:T(2,128)} %get-tuple-element.396) | copy-start | bytes 28
  356.0 548.2 %copy-start.6 = (f32[1,2]{0,1:T(2,128)S(1)}, f32[1,2]{0,1:T(2,128)}, u32[]{:S(2)}) copy-start(f32[1,2]{0,1:T(2,128)} %get-tuple-element.397) | copy-start | bytes 28
  356.0 548.2 %copy-start.7 = (f32[1,2]{0,1:T(2,128)S(1)}, f32[1,2]{0,1:T(2,128)}, u32[]{:S(2)}) copy-start(f32[1,2]{0,1:T(2,128)} %get-tuple-element.398) | copy-start | bytes 28
  356.0 548.2 %copy-start.8 = (f32[1,2]{0,1:T(2,128)S(1)}, f32[1,2]{0,1:T(2,128)}, u32[]{:S(2)}) copy-start(f32[1,2]{0,1:T(2,128)} %get-tuple-element.399) | copy-start | bytes 28
  356.0 548.2 %copy-start.9 = (f32[1,2]{0,1:T(2,128)S(1)}, f32[1,2]{0,1:T(2,128)}, u32[]{:S(2)}) copy-start(f32[1,2]{0,1:T(2,128)} %get-tuple-element.400) | copy-start | bytes 28
  367.2 617.1 %all-gather.9.cloned.1.call-start = ((), (), s32[]{:S(2)}) async-start(), calls=%async_computation.1 | async-start | bytes 8454144 | tf_op jit(solution)/shard_map/all_gather | solution.py:29
  912.7 357.4 %copy-start.1 = (f32[3,4096]{1,0:T(4,128)S(1)}, f32[3,4096]{1,0:T(4,128)}, u32[]{:S(2)}) copy-start(f32[3,4096]{1,0:T(4,128)} %fusion.52) | copy-start | bytes 147460
Sparse Core Ops, SparseCore 0:
  367.3 82.7 all-gather.6
  904.2 80.0 all-gather.8
where the time goes:
time: 1300 us; the launch traced here: 1280 us
  other arithmetic  522 us (40%)
  blocking collectives  303 us (23%)
  local copies, waits for them, and re-layouts  191 us (15%)
  matrix products  103 us (8%)
  waiting for transfers between devices  71.6 us (6%)
  between operations  64.9 us (5%)
  starting transfers between devices  14.7 us (1%)
    select_n x381, other arithmetic, turn(): jnp.where(position < mine, new, old)  479 us
    unnamed x1, blocking collectives  250 us
    dynamic_slice x254, local copies, waits for them, and re-layouts, turn(): longer = join(total, jax.tree.map(lambda part: part[position], pieces))  153 us
    dot_general x127, matrix products, chain_ratio(): product = jnp.dot(latter, earlier, precision=lax.Precision.HIGHEST)  103 us
    all_gather x2, waiting for transfers between devices, prefix(): pieces = jax.tree.map(lambda part: lax.all_gather(part, axis), value)  71.5 us
    all_gather x1, blocking collectives, prefix(): pieces = jax.tree.map(lambda part: lax.all_gather(part, axis), value)  53.6 us
  transfers between devices with their start and end apart: 6, of which 1 were waited for; matrix products, arithmetic and copies ran while one was open for 18% of the time, Pallas kernels for 0%

commit v1 on v0

--- a/solution.py
+++ b/solution.py
@@ -26,19 +26,24 @@
 
 def prefix(value, axis, join, neutral, backward):
     count, mine = (lax.axis_size(axis), lax.axis_index(axis))
-    pieces = jax.tree.map(lambda part: lax.all_gather(part, axis), value)
-    if backward:
-        pieces = jax.tree.map(lambda part: part[::-1], pieces)
-        mine = count - 1 - mine
+    step = -1 if backward else 1
+    order = [(i, i + step) for i in range(count) if 0 <= i + step < count]
+    total = jax.tree.map(lambda part: lax.ppermute(part, axis, order), value)
+    inside = (mine >= 1) if not backward else (mine <= count - 2)
     total = jax.tree.map(
-        lambda part, zero: jnp.full_like(part, 0) + jnp.asarray(zero, part.dtype), value, neutral
+        lambda part, zero: jnp.where(inside, part, jnp.full_like(part, 0) + jnp.asarray(zero, part.dtype)),
+        total,
+        neutral,
     )
-
-    def turn(position, total):
-        longer = join(total, jax.tree.map(lambda part: part[position], pieces))
-        return jax.tree.map(lambda new, old: jnp.where(position < mine, new, old), longer, total)
-
-    return lax.fori_loop(0, count - 1, turn, total)
+    offset = 1
+    while offset < count:
+        pairs = [(i, i + step * offset) for i in range(count) if 0 <= i + step * offset < count]
+        earlier = jax.tree.map(lambda part: lax.ppermute(part, axis, pairs), total)
+        longer = join(earlier, total)
+        reach = (mine >= offset) if not backward else (mine <= count - 1 - offset)
+        total = jax.tree.map(lambda new, old: jnp.where(reach, new, old), longer, total)
+        offset *= 2
+    return total
 
 
 def stream_slope(padded, planes):

time: 1300 us -> 381 us (0.29)
  the two profiles are of different devices: /device:TPU:6 before, /device:TPU:120 now
where the time goes in v1:
time: 381 us; the launch traced here: 378 us
  starting transfers between devices  174 us (46%)
  waiting for transfers between devices  76.6 us (20%)
  between operations  60.3 us (16%)
  other arithmetic  44.2 us (12%)
  local copies, waits for them, and re-layouts  18.6 us (5%)
  matrix products  4.9 us (1%)
    ppermute x33, starting transfers between devices, prefix(): earlier = jax.tree.map(lambda part: lax.ppermute(part, axis, pairs), total)  144 us
    ppermute x33, waiting for transfers between devices, prefix(): earlier = jax.tree.map(lambda part: lax.ppermute(part, axis, pairs), total)  62.3 us
    ppermute x5, starting transfers between devices, prefix(): total = jax.tree.map(lambda part: lax.ppermute(part, axis, order), value)  17.3 us
    ppermute x5, waiting for transfers between devices, prefix(): total = jax.tree.map(lambda part: lax.ppermute(part, axis, order), value)  14.3 us
    unnamed x7, other arithmetic  7.75 us
  transfers between devices with their start and end apart: 42, of which 24 were waited for; matrix products, arithmetic and copies ran while one was open for 11% of the time, Pallas kernels for 0%

profile of v1, /device:TPU:120, one launch (start us, length us, event | category | flops | bytes accessed | tf_op | source)
XLA Modules:
  0.0 378.2 jit_solution(12429302670866315871)
XLA Ops:
  40.6 6.9 %subtract_divide_fusion.12 = (f32[1,2]{0,1:T(2,128)S(1)}, f32[1,2]{0,1:T(2,128)S(1)}, f32[1,2]{0,1:T(2,128)S(1)}, f32[1,2]{0,1:T(2,128)S(1)}, f32[1,2]{0,1:T(2,1...) fusion(f32[12,2]{0,1:T(2,128)S(1)} %scatter.9, ...), kind=kLoop, calls=%fused_computation.214 | loop fusion | flops 62 | bytes 252 | tf_op jit(solution)/shard_map/eval_jaxpr/div | solution.py:109
  85.8 5.7 %collective-permute-start.5 = (f32[2,2]{1,0:T(2,128)S(1)}, f32[2,2]{1,0:T(2,128)S(1)}, u32[]{:S(2)}, u32[]{:S(2)}) collective-permute-start(f32[2,2]{1,0:T(2,128)S(1)} %fusion.72), channel_id=1, source_target_pairs={{0,1},{1,2},{2,3},{3,4},{4,5},{5,6},{6,7},{7,8},{8,9},{9,10},{10,1... | collective-permute-start | bytes 56 | tf_op jit(solution)/shard_map/ppermute | solution.py:41
  93.6 6.1 %collective-permute-start.6 = (f32[2,2]{1,0:T(2,128)S(1)}, f32[2,2]{1,0:T(2,128)S(1)}, u32[]{:S(2)}, u32[]{:S(2)}) collective-permute-start(f32[2,2]{1,0:T(2,128)S(1)} %divide_select_fusion.6), channel_id=1, source_target_pairs={{0,2},{1,3},{2,4},{3,5},{4,6},{5,7},{6,8},{7,9},{8,10},{9,11},{10,... | collective-permute-start | bytes 56 | tf_op jit(solution)/shard_map/ppermute | solution.py:41
  109.8 5.9 %collective-permute-start.8 = (f32[2,2]{1,0:T(2,128)S(1)}, f32[2,2]{1,0:T(2,128)S(1)}, u32[]{:S(2)}, u32[]{:S(2)}) collective-permute-start(f32[2,2]{1,0:T(2,128)S(1)} %divide_select_fusion.4), channel_id=1, source_target_pairs={{0,8},{1,9},{2,10},{3,11},{4,12},{5,13},{6,14},{7,15},{8,16},{9,17... | collective-permute-start | bytes 56 | tf_op jit(solution)/shard_map/ppermute | solution.py:41
  127.2 9.6 %collective-permute-start.10 = (f32[2,2]{1,0:T(2,128)S(1)}, f32[2,2]{1,0:T(2,128)S(1)}, u32[]{:S(2)}, u32[]{:S(2)}) collective-permute-start(f32[2,2]{1,0:T(2,128)S(1)} %divide_select_fusion.2), channel_id=1, source_target_pairs={{0,32},{1,33},{2,34},{3,35},{4,36},{5,37},{6,38},{7,39},{8,40},{9,... | collective-permute-start | bytes 56 | tf_op jit(solution)/shard_map/ppermute | solution.py:41
  139.4 5.7 %collective-permute-start.11 = (f32[2,2]{1,0:T(2,128)S(1)}, f32[2,2]{1,0:T(2,128)S(1)}, u32[]{:S(2)}, u32[]{:S(2)}) collective-permute-start(f32[2,2]{1,0:T(2,128)S(1)} %divide_select_fusion.1), channel_id=1, source_target_pairs={{0,64},{1,65},{2,66},{3,67},{4,68},{5,69},{6,70},{7,71},{8,72},{9,... | collective-permute-start | bytes 56 | tf_op jit(solution)/shard_map/ppermute | solution.py:41
  152.5 5.0 %multiply_add_fusion = (f32[3,12,32,128]{3,2,1,0:T(8,128)S(1)}, f32[3,12,32,128]{3,2,1,0:T(8,128)}) fusion(f32[3,12,32,128]{3,2,1,0:T(8,128)} %param.13, f32[3,12,32,128]{3,2,1,0:T(8,128)S(1)} %copy-done, f32[3,12,28,128]{3,2,1,0:T(8,128)S(1)} %get-tuple-element.127, f32[3,12,4,128]{3,2,1,0:T(4,128)} %get-tuple-element.129, ...), kind=kLoop, calls=%fused_computation.55 | loop fusion | flops 7667712 | bytes 7802928 | tf_op jit(solution)/shard_map/add | solution.py:93
  158.7 7.0 %subtract_dynamic-update-slice_fusion = (f32[11,3,4096]{2,1,0:T(4,128)S(1)}, f32[1,3,4096]{2,1,0:T(4,128)S(1)}, f32[1,3,4096]{2,1,0:T(4,128)S(1)}, f32[1,3,4096]...) fusion(f32[]{:T(128)} %bitcast.9, f32[]{:T(128)} %bitcast.13, ...), kind=kLoop, calls=%fused_computation.125 | loop fusion | flops 651263 | bytes 1245312
  167.1 7.0 %fusion.37 = (f32[3,4096]{1,0:T(4,128)S(1)}, f32[3,4096]{1,0:T(4,128)S(1)}) fusion(f32[3,11,4096]{2,0,1:T(4,128)S(1)} %bitcast.295, f32[]{:T(128)S(6)} %div.1106, f32[]{:T(128)} %bitcast.47, f32[]{:T(128)} %bitcast.46, f32[11,3,4096]{2,1,0:T(4,128)S(1)} %slice_bitcast_fusion, f32[]{:T(128)} %bitcast.45, f32[]{:T(128)} %bitcast.44, f32[]{:T(128)} %bitcast.43, ...), kind=kLoop, calls=%fused_computation.80 | loop fusion | flops 700416 | bytes 737416 | tf_op jit(solution)/shard_map/add | solution.py:127
  179.7 10.7 %collective-permute-start.14 = (f32[3,4096]{1,0:T(4,128)S(1)}, f32[3,4096]{1,0:T(4,128)S(1)}, u32[]{:S(2)}, u32[]{:S(2)}) collective-permute-start(f32[3,4096]{1,0:T(4,128)S(1)} %broadcast_select_fusion.1), channel_id=1, source_target_pairs={{0,1},{1,2},{2,3},{3,4},{4,5},{5,6},{6,7},{7,8},{8,9},{9,10},{10,1... | collective-permute-start | bytes 147464 | tf_op jit(solution)/shard_map/ppermute | solution.py:41
  191.1 7.3 %collective-permute-start.13 = (f32[1,1]{1,0:T(1,128)}, f32[1,1]{1,0:T(1,128)}, u32[]{:S(2)}, u32[]{:S(2)}) collective-permute-start(f32[1,1]{1,0:T(1,128)} %bitcast.99), channel_id=1, source_target_pairs={{0,1},{1,2},{2,3},{3,4},{4,5},{5,6},{6,7},{7,8},{8,9},{9,10},{10,1... | collective-permute-start | bytes 20 | tf_op jit(solution)/shard_map/ppermute | solution.py:31
  199.1 6.0 %collective-permute-start.16 = (f32[3,4096]{1,0:T(4,128)S(1)}, f32[3,4096]{1,0:T(4,128)S(1)}, u32[]{:S(2)}, u32[]{:S(2)}) collective-permute-start(f32[3,4096]{1,0:T(4,128)S(1)} %add_select_fusion.13), channel_id=1, source_target_pairs={{0,2},{1,3},{2,4},{3,5},{4,6},{5,7},{6,8},{7,9},{8,10},{9,11},{10,... | collective-permute-start | bytes 147464 | tf_op jit(solution)/shard_map/ppermute | solution.py:41
  212.7 5.3 %collective-permute-start.17 = (f32[1,1]{1,0:T(1,128)}, f32[1,1]{1,0:T(1,128)}, u32[]{:S(2)}, u32[]{:S(2)}) collective-permute-start(f32[1,1]{1,0:T(1,128)} %select_n.250), channel_id=1, source_target_pairs={{0,2},{1,3},{2,4},{3,5},{4,6},{5,7},{6,8},{7,9},{8,10},{9,11},{10,... | collective-permute-start | bytes 20 | tf_op jit(solution)/shard_map/ppermute | solution.py:41
  222.4 6.3 %collective-permute-start.19 = (f32[1,1]{1,0:T(1,128)}, f32[1,1]{1,0:T(1,128)}, u32[]{:S(2)}, u32[]{:S(2)}) collective-permute-start(f32[1,1]{1,0:T(1,128)} %select_n.253), channel_id=1, source_target_pairs={{0,4},{1,5},{2,6},{3,7},{4,8},{5,9},{6,10},{7,11},{8,12},{9,13},{1... | collective-permute-start | bytes 20 | tf_op jit(solution)/shard_map/ppermute | solution.py:41
  230.9 13.6 %collective-permute-start.22 = (f32[3,4096]{1,0:T(4,128)S(1)}, f32[3,4096]{1,0:T(4,128)S(1)}, u32[]{:S(2)}, u32[]{:S(2)}) collective-permute-start(f32[3,4096]{1,0:T(4,128)S(1)} %add_select_fusion.10), channel_id=1, source_target_pairs={{0,16},{1,17},{2,18},{3,19},{4,20},{5,21},{6,22},{7,23},{8,24},{9,... | collective-permute-start | bytes 147464 | tf_op jit(solution)/shard_map/ppermute | solution.py:41
  244.6 7.7 %collective-permute-start.21 = (f32[1,1]{1,0:T(1,128)}, f32[1,1]{1,0:T(1,128)}, u32[]{:S(2)}, u32[]{:S(2)}) collective-permute-start(f32[1,1]{1,0:T(1,128)} %select_n.256), channel_id=1, source_target_pairs={{0,8},{1,9},{2,10},{3,11},{4,12},{5,13},{6,14},{7,15},{8,16},{9,17... | collective-permute-start | bytes 20 | tf_op jit(solution)/shard_map/ppermute | solution.py:41
  281.8 8.7 %collective-permute-done.28 = f32[1,1]{1,0:T(1,128)} collective-permute-done((f32[1,1]{1,0:T(1,128)}, f32[1,1]{1,0:T(1,128)}, u32[]{:S(2)}, u32[]{:S(2)}) %collective-permute-start.28) | collective-permute-done | bytes 36 | tf_op jit(solution)/shard_map/ppermute | solution.py:31
  319.2 5.3 %collective-permute-done.34 = f32[1,1]{1,0:T(1,128)} collective-permute-done((f32[1,1]{1,0:T(1,128)}, f32[1,1]{1,0:T(1,128)}, u32[]{:S(2)}, u32[]{:S(2)}) %collective-permute-start.34) | collective-permute-done | bytes 36 | tf_op jit(solution)/shard_map/ppermute | solution.py:41
  327.1 4.9 %collective-permute-start.36 = (f32[1,1]{1,0:T(1,128)}, f32[1,1]{1,0:T(1,128)}, u32[]{:S(2)}, u32[]{:S(2)}) collective-permute-start(f32[1,1]{1,0:T(1,128)} %select_n.284), channel_id=1, source_target_pairs={{8,0},{9,1},{10,2},{11,3},{12,4},{13,5},{14,6},{15,7},{16,8},{17,9... | collective-permute-start | bytes 20 | tf_op jit(solution)/shard_map/ppermute | solution.py:41
  332.0 5.5 %collective-permute-done.36 = f32[1,1]{1,0:T(1,128)} collective-permute-done((f32[1,1]{1,0:T(1,128)}, f32[1,1]{1,0:T(1,128)}, u32[]{:S(2)}, u32[]{:S(2)}) %collective-permute-start.36) | collective-permute-done | bytes 36 | tf_op jit(solution)/shard_map/ppermute | solution.py:41
  341.3 4.9 %collective-permute-done.38 = f32[1,1]{1,0:T(1,128)} collective-permute-done((f32[1,1]{1,0:T(1,128)}, f32[1,1]{1,0:T(1,128)}, u32[]{:S(2)}, u32[]{:S(2)}) %collective-permute-start.38) | collective-permute-done | bytes 36 | tf_op jit(solution)/shard_map/ppermute | solution.py:41
  348.2 8.1 %collective-permute-done.40 = f32[1,1]{1,0:T(1,128)} collective-permute-done((f32[1,1]{1,0:T(1,128)}, f32[1,1]{1,0:T(1,128)}, u32[]{:S(2)}, u32[]{:S(2)}) %collective-permute-start.40) | collective-permute-done | bytes 36 | tf_op jit(solution)/shard_map/ppermute | solution.py:41
  358.3 6.9 %broadcast_multiply_fusion = (f32[3,1,4096]{2,0,1:T(4,128)S(1)}, f32[3,1,4096]{2,0,1:T(4,128)S(1)}, f32[3,1,4096]{2,0,1:T(4,128)S(1)}, f32[3,1,4096]{2,0,1:T(4,1...) fusion(f32[]{:T(128)} %bitcast.46, f32[]{:T(128)} %bitcast.44, ...), kind=kLoop, calls=%fused_computation.173 | loop fusion | flops 380928 | bytes 1081428 | tf_op jit(solution)/shard_map/vmap()/eval_jaxpr/mul | solution.py:101
  368.1 9.0 %collective-permute-done.41 = f32[3,4096]{1,0:T(4,128)S(1)} collective-permute-done((f32[3,4096]{1,0:T(4,128)S(1)}, f32[3,4096]{1,0:T(4,128)S(1)}, u32[]{:S(2)}, u32[]{:S(2)}) %collective-permute-start.41) | collective-permute-done | bytes 49184 | tf_op jit(solution)/shard_map/ppermute | solution.py:41
  (168 shorter events, 148.6 us)
Async XLA Ops:
  2.1 150.4 %collective-permute-start.3 = (f32[3,1,32,128]{3,2,1,0:T(8,128)}, f32[3,1,32,128]{3,2,1,0:T(8,128)}, u32[]{:S(2)}, u32[]{:S(2)}) collective-permute-start(f32[3,1,32,128]{3,2,1,0:T(8,128)} %get-tuple-element.113), channel_id=1, source_target_pairs={{0,1},{1,2},{2,3},{3,4},{4,5},{5,6},{6,7},{7,8},{8,9},{9,10},{10,1... | collective-permute-start | bytes 147464 | tf_op jit(solution)/shard_map/ppermute | solution.py:21
  4.0 148.5 %collective-permute-start.2 = (f32[3,1,32,128]{3,2,1,0:T(8,128)}, f32[3,1,32,128]{3,2,1,0:T(8,128)}, u32[]{:S(2)}, u32[]{:S(2)}) collective-permute-start(f32[3,1,32,128]{3,2,1,0:T(8,128)} %get-tuple-element.112), channel_id=1, source_target_pairs={{1,0},{2,1},{3,2},{4,3},{5,4},{6,5},{7,6},{8,7},{9,8},{10,9},{11,1... | collective-permute-start | bytes 147464 | tf_op jit(solution)/shard_map/ppermute | solution.py:22
  9.5 141.5 %collective-permute-start.1 = (f32[3,12,32,4]{2,1,3,0:T(8,128)S(1)}, f32[3,12,32,4]{2,1,3,0:T(8,128)S(1)}, u32[]{:S(2)}, u32[]{:S(2)}) collective-permute-start(f32[3,12,32,4]{2,1,3,0:T(8,128)S(1)} %copy.57), channel_id=1, source_target_pairs={{0,128},{128,256},{256,384},{384,0},{1,129},{129,257},{257,385},{3... | collective-permute-start | bytes 55304 | tf_op jit(solution)/shard_map/ppermute | solution.py:21
  13.3 138.0 %collective-permute-start = (f32[3,12,32,4]{2,1,3,0:T(8,128)S(1)}, f32[3,12,32,4]{2,1,3,0:T(8,128)}, u32[]{:S(2)}, u32[]{:S(2)}) collective-permute-start(f32[3,12,32,4]{2,1,3,0:T(8,128)S(1)} %copy.56), channel_id=1, source_target_pairs={{128,0},{256,128},{384,256},{0,384},{129,1},{257,129},{385,257},{1... | collective-permute-start | bytes 55304 | tf_op jit(solution)/shard_map/ppermute | solution.py:22
  55.8 30.0 %collective-permute-start.4 = (f32[2,2]{1,0:T(2,128)S(1)}, f32[2,2]{1,0:T(2,128)S(1)}, u32[]{:S(2)}, u32[]{:S(2)}) collective-permute-start(f32[2,2]{1,0:T(2,128)S(1)} %pad_maximum_fusion.4), channel_id=1, source_target_pairs={{0,1},{1,2},{2,3},{3,4},{4,5},{5,6},{6,7},{7,8},{8,9},{9,10},{10,1... | collective-permute-start | bytes 56 | tf_op jit(solution)/shard_map/ppermute | solution.py:31
  109.8 9.4 %collective-permute-start.8 = (f32[2,2]{1,0:T(2,128)S(1)}, f32[2,2]{1,0:T(2,128)S(1)}, u32[]{:S(2)}, u32[]{:S(2)}) collective-permute-start(f32[2,2]{1,0:T(2,128)S(1)} %divide_select_fusion.4), channel_id=1, source_target_pairs={{0,8},{1,9},{2,10},{3,11},{4,12},{5,13},{6,14},{7,15},{8,16},{9,17... | collective-permute-start | bytes 56 | tf_op jit(solution)/shard_map/ppermute | solution.py:41
  127.2 10.9 %collective-permute-start.10 = (f32[2,2]{1,0:T(2,128)S(1)}, f32[2,2]{1,0:T(2,128)S(1)}, u32[]{:S(2)}, u32[]{:S(2)}) collective-permute-start(f32[2,2]{1,0:T(2,128)S(1)} %divide_select_fusion.2), channel_id=1, source_target_pairs={{0,32},{1,33},{2,34},{3,35},{4,36},{5,37},{6,38},{7,39},{8,40},{9,... | collective-permute-start | bytes 56 | tf_op jit(solution)/shard_map/ppermute | solution.py:41
  179.7 19.4 %collective-permute-start.14 = (f32[3,4096]{1,0:T(4,128)S(1)}, f32[3,4096]{1,0:T(4,128)S(1)}, u32[]{:S(2)}, u32[]{:S(2)}) collective-permute-start(f32[3,4096]{1,0:T(4,128)S(1)} %broadcast_select_fusion.1), channel_id=1, source_target_pairs={{0,1},{1,2},{2,3},{3,4},{4,5},{5,6},{6,7},{7,8},{8,9},{9,10},{10,1... | collective-permute-start | bytes 147464 | tf_op jit(solution)/shard_map/ppermute | solution.py:41
  199.1 11.7 %collective-permute-start.16 = (f32[3,4096]{1,0:T(4,128)S(1)}, f32[3,4096]{1,0:T(4,128)S(1)}, u32[]{:S(2)}, u32[]{:S(2)}) collective-permute-start(f32[3,4096]{1,0:T(4,128)S(1)} %add_select_fusion.13), channel_id=1, source_target_pairs={{0,2},{1,3},{2,4},{3,5},{4,6},{5,7},{6,8},{7,9},{8,10},{9,11},{10,... | collective-permute-start | bytes 147464 | tf_op jit(solution)/shard_map/ppermute | solution.py:41
  210.8 9.7 %collective-permute-start.18 = (f32[3,4096]{1,0:T(4,128)S(1)}, f32[3,4096]{1,0:T(4,128)S(1)}, u32[]{:S(2)}, u32[]{:S(2)}) collective-permute-start(f32[3,4096]{1,0:T(4,128)S(1)} %add_select_fusion.12), channel_id=1, source_target_pairs={{0,4},{1,5},{2,6},{3,7},{4,8},{5,9},{6,10},{7,11},{8,12},{9,13},{1... | collective-permute-start | bytes 147464 | tf_op jit(solution)/shard_map/ppermute | solution.py:41
  220.5 10.4 %collective-permute-start.20 = (f32[3,4096]{1,0:T(4,128)S(1)}, f32[3,4096]{1,0:T(4,128)S(1)}, u32[]{:S(2)}, u32[]{:S(2)}) collective-permute-start(f32[3,4096]{1,0:T(4,128)S(1)} %add_select_fusion.11), channel_id=1, source_target_pairs={{0,8},{1,9},{2,10},{3,11},{4,12},{5,13},{6,14},{7,15},{8,16},{9,17... | collective-permute-start | bytes 147464 | tf_op jit(solution)/shard_map/ppermute | solution.py:41
  230.9 23.7 %collective-permute-start.22 = (f32[3,4096]{1,0:T(4,128)S(1)}, f32[3,4096]{1,0:T(4,128)S(1)}, u32[]{:S(2)}, u32[]{:S(2)}) collective-permute-start(f32[3,4096]{1,0:T(4,128)S(1)} %add_select_fusion.10), channel_id=1, source_target_pairs={{0,16},{1,17},{2,18},{3,19},{4,20},{5,21},{6,22},{7,23},{8,24},{9,... | collective-permute-start | bytes 147464 | tf_op jit(solution)/shard_map/ppermute | solution.py:41
  244.6 9.4 %collective-permute-start.21 = (f32[1,1]{1,0:T(1,128)}, f32[1,1]{1,0:T(1,128)}, u32[]{:S(2)}, u32[]{:S(2)}) collective-permute-start(f32[1,1]{1,0:T(1,128)} %select_n.256), channel_id=1, source_target_pairs={{0,8},{1,9},{2,10},{3,11},{4,12},{5,13},{6,14},{7,15},{8,16},{9,17... | collective-permute-start | bytes 20 | tf_op jit(solution)/shard_map/ppermute | solution.py:41
  254.7 8.3 %collective-permute-start.24 = (f32[3,4096]{1,0:T(4,128)S(1)}, f32[3,4096]{1,0:T(4,128)S(1)}, u32[]{:S(2)}, u32[]{:S(2)}) collective-permute-start(f32[3,4096]{1,0:T(4,128)S(1)} %add_select_fusion.9), channel_id=1, source_target_pairs={{0,32},{1,33},{2,34},{3,35},{4,36},{5,37},{6,38},{7,39},{8,40},{9,... | collective-permute-start | bytes 147464 | tf_op jit(solution)/shard_map/ppermute | solution.py:41
  273.0 18.1 %collective-permute-start.29 = (f32[3,4096]{1,0:T(4,128)S(1)}, f32[3,4096]{1,0:T(4,128)S(1)}, u32[]{:S(2)}, u32[]{:S(2)}) collective-permute-start(f32[3,4096]{1,0:T(4,128)S(1)} %broadcast_select_fusion), channel_id=1, source_target_pairs={{1,0},{2,1},{3,2},{4,3},{5,4},{6,5},{7,6},{8,7},{9,8},{10,9},{11,1... | collective-permute-start | bytes 147464 | tf_op jit(solution)/shard_map/ppermute | solution.py:41
  277.6 12.9 %collective-permute-start.28 = (f32[1,1]{1,0:T(1,128)}, f32[1,1]{1,0:T(1,128)}, u32[]{:S(2)}, u32[]{:S(2)}) collective-permute-start(f32[1,1]{1,0:T(1,128)} %bitcast.113), channel_id=1, source_target_pairs={{1,0},{2,1},{3,2},{4,3},{5,4},{6,5},{7,6},{8,7},{9,8},{10,9},{11,1... | collective-permute-start | bytes 20 | tf_op jit(solution)/shard_map/ppermute | solution.py:31
  291.2 9.5 %collective-permute-start.31 = (f32[3,4096]{1,0:T(4,128)S(1)}, f32[3,4096]{1,0:T(4,128)S(1)}, u32[]{:S(2)}, u32[]{:S(2)}) collective-permute-start(f32[3,4096]{1,0:T(4,128)S(1)} %add_select_fusion.6), channel_id=1, source_target_pairs={{2,0},{3,1},{4,2},{5,3},{6,4},{7,5},{8,6},{9,7},{10,8},{11,9},{12,... | collective-permute-start | bytes 147464 | tf_op jit(solution)/shard_map/ppermute | solution.py:41
  300.7 10.4 %collective-permute-start.33 = (f32[3,4096]{1,0:T(4,128)S(1)}, f32[3,4096]{1,0:T(4,128)S(1)}, u32[]{:S(2)}, u32[]{:S(2)}) collective-permute-start(f32[3,4096]{1,0:T(4,128)S(1)} %add_select_fusion.5), channel_id=1, source_target_pairs={{4,0},{5,1},{6,2},{7,3},{8,4},{9,5},{10,6},{11,7},{12,8},{13,9},{1... | collective-permute-start | bytes 147464 | tf_op jit(solution)/shard_map/ppermute | solution.py:41
  311.2 14.0 %collective-permute-start.35 = (f32[3,4096]{1,0:T(4,128)S(1)}, f32[3,4096]{1,0:T(4,128)S(1)}, u32[]{:S(2)}, u32[]{:S(2)}) collective-permute-start(f32[3,4096]{1,0:T(4,128)S(1)} %add_select_fusion.4), channel_id=1, source_target_pairs={{8,0},{9,1},{10,2},{11,3},{12,4},{13,5},{14,6},{15,7},{16,8},{17,9... | collective-permute-start | bytes 147464 | tf_op jit(solution)/shard_map/ppermute | solution.py:41
  316.0 8.5 %collective-permute-start.34 = (f32[1,1]{1,0:T(1,128)}, f32[1,1]{1,0:T(1,128)}, u32[]{:S(2)}, u32[]{:S(2)}) collective-permute-start(f32[1,1]{1,0:T(1,128)} %select_n.281), channel_id=1, source_target_pairs={{4,0},{5,1},{6,2},{7,3},{8,4},{9,5},{10,6},{11,7},{12,8},{13,9},{1... | collective-permute-start | bytes 20 | tf_op jit(solution)/shard_map/ppermute | solution.py:41
  325.2 31.8 %collective-permute-start.37 = (f32[3,4096]{1,0:T(4,128)S(1)}, f32[3,4096]{1,0:T(4,128)S(1)}, u32[]{:S(2)}, u32[]{:S(2)}) collective-permute-start(f32[3,4096]{1,0:T(4,128)S(1)} %add_select_fusion.3), channel_id=1, source_target_pairs={{16,0},{17,1},{18,2},{19,3},{20,4},{21,5},{22,6},{23,7},{24,8},{25... | collective-permute-start | bytes 147464 | tf_op jit(solution)/shard_map/ppermute | solution.py:41
  327.1 10.3 %collective-permute-start.36 = (f32[1,1]{1,0:T(1,128)}, f32[1,1]{1,0:T(1,128)}, u32[]{:S(2)}, u32[]{:S(2)}) collective-permute-start(f32[1,1]{1,0:T(1,128)} %select_n.284), channel_id=1, source_target_pairs={{8,0},{9,1},{10,2},{11,3},{12,4},{13,5},{14,6},{15,7},{16,8},{17,9... | collective-permute-start | bytes 20 | tf_op jit(solution)/shard_map/ppermute | solution.py:41
  346.9 9.4 %collective-permute-start.40 = (f32[1,1]{1,0:T(1,128)}, f32[1,1]{1,0:T(1,128)}, u32[]{:S(2)}, u32[]{:S(2)}) collective-permute-start(f32[1,1]{1,0:T(1,128)} %select_n.290), channel_id=1, source_target_pairs={{32,0},{33,1},{34,2},{35,3},{36,4},{37,5},{38,6},{39,7},{40,8},{41... | collective-permute-start | bytes 20 | tf_op jit(solution)/shard_map/ppermute | solution.py:41
  365.3 11.8 %collective-permute-start.41 = (f32[3,4096]{1,0:T(4,128)S(1)}, f32[3,4096]{1,0:T(4,128)S(1)}, u32[]{:S(2)}, u32[]{:S(2)}) collective-permute-start(f32[3,4096]{1,0:T(4,128)S(1)} %add_select_fusion.1), channel_id=1, source_target_pairs={{64,0},{65,1},{66,2},{67,3},{68,4},{69,5},{70,6},{71,7},{72,8},{73... | collective-permute-start | bytes 147464 | tf_op jit(solution)/shard_map/ppermute | solution.py:41
  (29 other events, 856.5 us)

commit v2 on v1

--- a/solution.py
+++ b/solution.py
@@ -1,7 +1,14 @@
+import functools
+
 import jax
 import jax.numpy as jnp
 from jax import lax
 from jax.sharding import PartitionSpec as P
+from jax.experimental import pallas as pl
+from jax.experimental.pallas import tpu as pltpu
+
+MESH = pl.DeviceIdType.MESH
+LINES = 96
 
 STIFF = 1024
 
@@ -44,6 +51,84 @@
         total = jax.tree.map(lambda new, old: jnp.where(reach, new, old), longer, total)
         offset *= 2
     return total
+
+
+def scan_kernel(count, backward, x_ref, out_ref, totals, recv, send_sem, recv_sem):
+    me = lax.axis_index("gy")
+    row = lax.axis_index("gx")
+    sign = -1 if backward else 1
+    offsets = [1]
+    while offsets[-1] * 2 < count:
+        offsets.append(offsets[-1] * 2)
+    partners = []
+    for offset in offsets:
+        partners.append((me + offset) % count)
+        if 2 * offset != count:
+            partners.append((me + count - offset) % count)
+    barrier = pltpu.get_barrier_semaphore()
+    for partner in partners:
+        pl.semaphore_signal(barrier, inc=1, device_id=(row, partner), device_id_type=MESH)
+    pl.semaphore_wait(barrier, len(partners))
+    rounds = [1] + offsets
+    copies = []
+    for step, offset in enumerate(rounds):
+        source = x_ref if step == 0 else totals.at[step - 1]
+        target = (me + count + sign * offset) % count
+        copy = pltpu.make_async_remote_copy(
+            src_ref=source,
+            dst_ref=recv.at[step],
+            send_sem=send_sem.at[step],
+            recv_sem=recv_sem.at[step],
+            device_id=(row, target),
+            device_id_type=MESH,
+        )
+        copy.start()
+        copy.wait_recv()
+        copies.append(copy)
+        valid = (me + offset <= count - 1) if backward else (me >= offset)
+        earlier = recv[step]
+        if step == 0:
+            lines = jnp.zeros((LINES, 128), jnp.float32)
+            scale = jnp.ones((8, 128), jnp.float32)
+            neutral = jnp.concatenate([lines, scale], axis=0)
+            totals[step] = jnp.where(valid, earlier, neutral)
+        else:
+            latter = totals[step - 1]
+            factor = latter[LINES : LINES + 1, :]
+            joined_lines = latter[:LINES] + factor * earlier[:LINES]
+            joined_scale = latter[LINES:] * earlier[LINES:]
+            joined = jnp.concatenate([joined_lines, joined_scale], axis=0)
+            totals[step] = jnp.where(valid, joined, latter)
+    out_ref[...] = totals[len(rounds) - 1]
+    for copy in copies:
+        copy.wait_send()
+
+
+def line_scan(step_value, backward):
+    count = lax.axis_size("gy")
+    factor, lines = step_value
+    shape = lines.shape
+    packed = jnp.concatenate(
+        [lines.reshape(LINES, 128), jnp.broadcast_to(factor.reshape(1, 1), (8, 128))], axis=0
+    )
+    rounds = 1
+    while (1 << (rounds - 1)) * 2 < count:
+        rounds += 1
+    rounds += 1
+    result = pl.pallas_call(
+        functools.partial(scan_kernel, count, backward),
+        out_shape=jax.ShapeDtypeStruct(packed.shape, jnp.float32),
+        in_specs=[pl.BlockSpec(memory_space=pltpu.VMEM)],
+        out_specs=pl.BlockSpec(memory_space=pltpu.VMEM),
+        scratch_shapes=[
+            pltpu.VMEM((rounds,) + packed.shape, jnp.float32),
+            pltpu.VMEM((rounds,) + packed.shape, jnp.float32),
+            pltpu.SemaphoreType.DMA((rounds,)),
+            pltpu.SemaphoreType.DMA((rounds,)),
+        ],
+        compiler_params=pltpu.CompilerParams(collective_id=1 if backward else 0, has_side_effects=True),
+    )(packed)
+    return result[:LINES].reshape(shape)
 
 
 def stream_slope(padded, planes):
@@ -127,11 +212,11 @@
         last_solved + left_last * below_ratio / lower_denom * first_solved,
     )
     identity_step = (jnp.ones((1, 1), jnp.float32), jnp.zeros_like(first_solved))
-    below_offset = prefix(lower_step, "gy", compose, identity_step, False)[1]
+    below_offset = line_scan(lower_step, False)
     first_base = (first_solved - left_first * below_offset) / lower_denom
     first_slope = right_first / lower_denom
     upper_step = (jnp.reshape(-first_slope, (1, 1)), first_base)
-    above_value = prefix(upper_step, "gy", compose, identity_step, True)[1]
+    above_value = line_scan(upper_step, True)
     first_value = first_base - first_slope * above_value
     below_value = below_offset - below_ratio * first_value
     finished = (

time: 381 us -> 279 us (0.73)
  the two profiles are of different devices: /device:TPU:120 before, /device:TPU:6 now
where the time goes in v2:
time: 279 us; the launch traced here: 276 us
  Pallas kernels  74.9 us (27%)
  starting transfers between devices  72.7 us (26%)
  between operations  50.8 us (18%)
  other arithmetic  43.9 us (16%)
  local copies, waits for them, and re-layouts  20.4 us (7%)
  waiting for transfers between devices  8.5 us (3%)
  matrix products  5.1 us (2%)
    pallas_call x2, Pallas kernels, line_scan(): pl.pallas_call(functools.partial(scan_kernel, count, backward), out_shape...  74.9 us
    ppermute x7, starting transfers between devices, prefix(): earlier = jax.tree.map(lambda part: lax.ppermute(part, axis, pairs), total)  57.1 us
    unnamed x6, other arithmetic  15.3 us
    ppermute x2, starting transfers between devices, extended(): before = lax.ppermute(last, axis, up)  9.66 us
    ppermute x7, waiting for transfers between devices, prefix(): earlier = jax.tree.map(lambda part: lax.ppermute(part, axis, pairs), total)  8.49 us
    add x1, other arithmetic, shards(): last_solved + left_last * below_ratio / lower_denom * first_solved  6.87 us
    div x1, other arithmetic, shards(): lax.linalg.tridiagonal_solve(below_band, diagonal, above_band, columns)  6.81 us
  transfers between devices with their start and end apart: 12, of which 7 were waited for; matrix products, arithmetic and copies ran while one was open for 12% of the time, Pallas kernels for 0%

profile of v2, /device:TPU:6, one launch (start us, length us, event | category | flops | bytes accessed | tf_op | source)
XLA Modules:
  0.0 276.2 jit_solution(9793477198539430353)
XLA Ops:
  0.6 1.5 fusion.49
  2.1 2.3 collective-permute-start.3
  5.7 1.6 fusion.48
  7.7 7.3 %collective-permute-start.1 = (f32[3,12,32,4]{2,1,3,0:T(8,128)S(1)}, f32[3,12,32,4]{2,1,3,0:T(8,128)S(1)}, u32[]{:S(2)}, u32[]{:S(2)}) collective-permute-start(f32[3,12,32,4]{2,1,3,0:T(8,128)S(1)} %copy.20), channel_id=1, source_target_pairs={{0,128},{128,256},{256,384},{384,0},{1,129},{129,257},{257,385},{3... | collective-permute-start | bytes 55304 | tf_op jit(solution)/shard_map/ppermute | solution.py:28
  15.4 1.9 collective-permute-start
  40.3 6.8 %subtract_divide_fusion.12 = (f32[1,2]{0,1:T(2,128)S(1)}, f32[1,2]{0,1:T(2,128)S(1)}, f32[1,2]{0,1:T(2,128)S(1)}, f32[1,2]{0,1:T(2,128)S(1)}, f32[1,2]{0,1:T(2,1...) fusion(f32[12,2]{0,1:T(2,128)S(1)} %scatter.9, ...), kind=kLoop, calls=%fused_computation.152 | loop fusion | flops 62 | bytes 252 | tf_op jit(solution)/shard_map/eval_jaxpr/div | solution.py:194
  49.0 1.4 multiply_subtract_fusion.11
  54.8 2.7 collective-permute-start.4
  86.4 1.9 collective-permute-start.5
  90.5 4.0 %collective-permute-start.6 = (f32[2,2]{1,0:T(2,128)S(1)}, f32[2,2]{1,0:T(2,128)S(1)}, u32[]{:S(2)}, u32[]{:S(2)}) collective-permute-start(f32[2,2]{1,0:T(2,128)S(1)} %divide_select_fusion.6), channel_id=1, source_target_pairs={{0,2},{1,3},{2,4},{3,5},{4,6},{5,7},{6,8},{7,9},{8,10},{9,11},{10,... | collective-permute-start | bytes 56 | tf_op jit(solution)/shard_map/ppermute | solution.py:48
  94.4 1.3 collective-permute-done.6
  97.0 5.8 %collective-permute-start.7 = (f32[2,2]{1,0:T(2,128)S(1)}, f32[2,2]{1,0:T(2,128)S(1)}, u32[]{:S(2)}, u32[]{:S(2)}) collective-permute-start(f32[2,2]{1,0:T(2,128)S(1)} %divide_select_fusion.5), channel_id=1, source_target_pairs={{0,4},{1,5},{2,6},{3,7},{4,8},{5,9},{6,10},{7,11},{8,12},{9,13},{1... | collective-permute-start | bytes 56 | tf_op jit(solution)/shard_map/ppermute | solution.py:48
  105.4 11.9 %collective-permute-start.8 = (f32[2,2]{1,0:T(2,128)S(1)}, f32[2,2]{1,0:T(2,128)S(1)}, u32[]{:S(2)}, u32[]{:S(2)}) collective-permute-start(f32[2,2]{1,0:T(2,128)S(1)} %divide_select_fusion.4), channel_id=1, source_target_pairs={{0,8},{1,9},{2,10},{3,11},{4,12},{5,13},{6,14},{7,15},{8,16},{9,17... | collective-permute-start | bytes 56 | tf_op jit(solution)/shard_map/ppermute | solution.py:48
  117.3 1.3 collective-permute-done.8
  119.9 9.1 %collective-permute-start.9 = (f32[2,2]{1,0:T(2,128)S(1)}, f32[2,2]{1,0:T(2,128)S(1)}, u32[]{:S(2)}, u32[]{:S(2)}) collective-permute-start(f32[2,2]{1,0:T(2,128)S(1)} %divide_select_fusion.3), channel_id=1, source_target_pairs={{0,16},{1,17},{2,18},{3,19},{4,20},{5,21},{6,22},{7,23},{8,24},{9,... | collective-permute-start | bytes 56 | tf_op jit(solution)/shard_map/ppermute | solution.py:48
  131.6 6.1 %collective-permute-start.10 = (f32[2,2]{1,0:T(2,128)S(1)}, f32[2,2]{1,0:T(2,128)S(1)}, u32[]{:S(2)}, u32[]{:S(2)}) collective-permute-start(f32[2,2]{1,0:T(2,128)S(1)} %divide_select_fusion.2), channel_id=1, source_target_pairs={{0,32},{1,33},{2,34},{3,35},{4,36},{5,37},{6,38},{7,39},{8,40},{9,... | collective-permute-start | bytes 56 | tf_op jit(solution)/shard_map/ppermute | solution.py:48
  140.3 18.3 %collective-permute-start.11 = (f32[2,2]{1,0:T(2,128)S(1)}, f32[2,2]{1,0:T(2,128)S(1)}, u32[]{:S(2)}, u32[]{:S(2)}) collective-permute-start(f32[2,2]{1,0:T(2,128)S(1)} %divide_select_fusion.1), channel_id=1, source_target_pairs={{0,64},{1,65},{2,66},{3,67},{4,68},{5,69},{6,70},{7,71},{8,72},{9,... | collective-permute-start | bytes 56 | tf_op jit(solution)/shard_map/ppermute | solution.py:48
  166.5 5.0 %multiply_add_fusion = (f32[3,12,32,128]{3,2,1,0:T(8,128)S(1)}, f32[3,12,32,128]{3,2,1,0:T(8,128)}) fusion(f32[3,12,32,128]{3,2,1,0:T(8,128)} %param.13, f32[3,12,32,128]{3,2,1,0:T(8,128)S(1)} %copy-done, f32[3,12,28,128]{3,2,1,0:T(8,128)S(1)} %get-tuple-element.129, f32[3,12,4,128]{3,2,1,0:T(4,128)} %get-tuple-element.131, ...), kind=kLoop, calls=%fused_computation.55 | loop fusion | flops 7667712 | bytes 7802928 | tf_op jit(solution)/shard_map/add | solution.py:178
  171.9 7.6 %subtract_dynamic-update-slice_fusion = (f32[11,3,4096]{2,1,0:T(4,128)S(1)}, f32[1,3,4096]{2,1,0:T(4,128)S(1)}, f32[1,3,4096]{2,1,0:T(4,128)S(1)}, f32[1,3,4096]...) fusion(f32[]{:T(128)} %bitcast.9, f32[]{:T(128)} %bitcast.13, ...), kind=kLoop, calls=%fused_computation.86 | loop fusion | flops 663551 | bytes 1310852
  182.3 6.9 %multiply_add_fusion.1 = (f32[96,128]{1,0:T(8,128)S(1)}, f32[96,128]{1,0:T(8,128)S(1)}) fusion(f32[96,128]{1,0:T(8,128)S(1)} %squeeze.109, f32[]{:T(128)S(6)} %div.1148, f32[96,128]{1,0:T(8,128)S(1)} %div.1149, f32[]{:T(128)} %bitcast.48, f32[96,128]{1,0:T(8,128)S(1)} %squeeze.261, f32[]{:T(128)} %bitcast.47, f32[]{:T(128)} %bitcast.45, f32[]{:T(128)} %bitcast.44, ...), kind=kLoop, calls=%fused_computation.110 | loop fusion | flops 700416 | bytes 737416 | tf_op jit(solution)/shard_map/add | solution.py:212
  189.8 39.3 %shard_map.59 = f32[104,128]{1,0:T(8,128)} custom-call(f32[104,128]{1,0:T(8,128)} %concatenate.96.x_ref), custom_call_target="tpu_custom_call" | custom-call | tf_op jit(solution)/shard_map/pallas_call | solution.py:118
  229.1 1.4 subtract_divide_fusion.10
  231.2 35.6 %shard_map.60 = f32[104,128]{1,0:T(8,128)} custom-call(f32[104,128]{1,0:T(8,128)} %concatenate.97.x_ref), custom_call_target="tpu_custom_call" | custom-call | tf_op jit(solution)/shard_map/pallas_call | solution.py:118
  267.6 7.6 %subtract_bitcast_fusion = (f32[1,3,32,128]{3,1,2,0:T(4,128)S(1)}, f32[3,1,4096]{2,0,1:T(4,128)S(1)}) fusion(f32[3,1,4096]{2,0,1:T(4,128)S(1)} %reshape.3893, f32[3,1,4096]{2,0,1:T(4,128)S(1)} %mul.1674, f32[]{:T(128)S(6)} %sub.1202, f32[]{:T(128)} %bitcast.79, f32[]{:T(128)} %bitcast.85, f32[3,1,4096]{2,0,1:T(4,128)S(1)} %get-tuple-element.90, f32[]{:T(128)} %bitcast.48, ...), kind=kLoop, calls=%fused_computation.85 | loop fusion | flops 749568 | bytes 786576
  (95 shorter events, 37.0 us)
Async XLA Ops:
  2.1 164.4 %collective-permute-start.3 = (f32[3,1,32,128]{3,2,1,0:T(8,128)}, f32[3,1,32,128]{3,2,1,0:T(8,128)}, u32[]{:S(2)}, u32[]{:S(2)}) collective-permute-start(f32[3,1,32,128]{3,2,1,0:T(8,128)} %get-tuple-element.115), channel_id=1, source_target_pairs={{0,1},{1,2},{2,3},{3,4},{4,5},{5,6},{6,7},{7,8},{8,9},{9,10},{10,1... | collective-permute-start | bytes 147464 | tf_op jit(solution)/shard_map/ppermute | solution.py:28
  4.4 162.1 %collective-permute-start.2 = (f32[3,1,32,128]{3,2,1,0:T(8,128)}, f32[3,1,32,128]{3,2,1,0:T(8,128)}, u32[]{:S(2)}, u32[]{:S(2)}) collective-permute-start(f32[3,1,32,128]{3,2,1,0:T(8,128)} %get-tuple-element.114), channel_id=1, source_target_pairs={{1,0},{2,1},{3,2},{4,3},{5,4},{6,5},{7,6},{8,7},{9,8},{10,9},{11,1... | collective-permute-start | bytes 147464 | tf_op jit(solution)/shard_map/ppermute | solution.py:29
  7.3 10.0 %copy-start.1 = (f32[12]{0:T(128)S(1)}, f32[12]{0:T(128)}, u32[]{:S(2)}) copy-start(f32[12]{0:T(128)} %param.14) | copy-start | bytes 148
  7.3 10.0 %copy-start.2 = (f32[12]{0:T(128)S(1)}, f32[12]{0:T(128)}, u32[]{:S(2)}) copy-start(f32[12]{0:T(128)} %param.15) | copy-start | bytes 148
  7.3 50.2 %copy-start = (f32[3,12,32,128]{3,2,1,0:T(8,128)S(1)}, f32[3,12,32,128]{3,2,1,0:T(8,128)}, u32[]{:S(2)}) copy-start(f32[3,12,32,128]{3,2,1,0:T(8,128)} %param.12) | copy-start | bytes 1769476
  7.7 157.3 %collective-permute-start.1 = (f32[3,12,32,4]{2,1,3,0:T(8,128)S(1)}, f32[3,12,32,4]{2,1,3,0:T(8,128)S(1)}, u32[]{:S(2)}, u32[]{:S(2)}) collective-permute-start(f32[3,12,32,4]{2,1,3,0:T(8,128)S(1)} %copy.20), channel_id=1, source_target_pairs={{0,128},{128,256},{256,384},{384,0},{1,129},{129,257},{257,385},{3... | collective-permute-start | bytes 55304 | tf_op jit(solution)/shard_map/ppermute | solution.py:28
  15.4 149.9 %collective-permute-start = (f32[3,12,32,4]{2,1,3,0:T(8,128)S(1)}, f32[3,12,32,4]{2,1,3,0:T(8,128)}, u32[]{:S(2)}, u32[]{:S(2)}) collective-permute-start(f32[3,12,32,4]{2,1,3,0:T(8,128)S(1)} %copy.19), channel_id=1, source_target_pairs={{128,0},{256,128},{384,256},{0,384},{129,1},{257,129},{385,257},{1... | collective-permute-start | bytes 55304 | tf_op jit(solution)/shard_map/ppermute | solution.py:29
  54.8 31.6 %collective-permute-start.4 = (f32[2,2]{1,0:T(2,128)S(1)}, f32[2,2]{1,0:T(2,128)S(1)}, u32[]{:S(2)}, u32[]{:S(2)}) collective-permute-start(f32[2,2]{1,0:T(2,128)S(1)} %pad_maximum_fusion.4), channel_id=1, source_target_pairs={{0,1},{1,2},{2,3},{3,4},{4,5},{5,6},{6,7},{7,8},{8,9},{9,10},{10,1... | collective-permute-start | bytes 56 | tf_op jit(solution)/shard_map/ppermute | solution.py:38
  86.4 2.7 collective-permute-start.5
  90.5 5.3 %collective-permute-start.6 = (f32[2,2]{1,0:T(2,128)S(1)}, f32[2,2]{1,0:T(2,128)S(1)}, u32[]{:S(2)}, u32[]{:S(2)}) collective-permute-start(f32[2,2]{1,0:T(2,128)S(1)} %divide_select_fusion.6), channel_id=1, source_target_pairs={{0,2},{1,3},{2,4},{3,5},{4,6},{5,7},{6,8},{7,9},{8,10},{9,11},{10,... | collective-permute-start | bytes 56 | tf_op jit(solution)/shard_map/ppermute | solution.py:48
  97.0 7.1 %collective-permute-start.7 = (f32[2,2]{1,0:T(2,128)S(1)}, f32[2,2]{1,0:T(2,128)S(1)}, u32[]{:S(2)}, u32[]{:S(2)}) collective-permute-start(f32[2,2]{1,0:T(2,128)S(1)} %divide_select_fusion.5), channel_id=1, source_target_pairs={{0,4},{1,5},{2,6},{3,7},{4,8},{5,9},{6,10},{7,11},{8,12},{9,13},{1... | collective-permute-start | bytes 56 | tf_op jit(solution)/shard_map/ppermute | solution.py:48
  105.4 13.2 %collective-permute-start.8 = (f32[2,2]{1,0:T(2,128)S(1)}, f32[2,2]{1,0:T(2,128)S(1)}, u32[]{:S(2)}, u32[]{:S(2)}) collective-permute-start(f32[2,2]{1,0:T(2,128)S(1)} %divide_select_fusion.4), channel_id=1, source_target_pairs={{0,8},{1,9},{2,10},{3,11},{4,12},{5,13},{6,14},{7,15},{8,16},{9,17... | collective-permute-start | bytes 56 | tf_op jit(solution)/shard_map/ppermute | solution.py:48
  119.9 10.4 %collective-permute-start.9 = (f32[2,2]{1,0:T(2,128)S(1)}, f32[2,2]{1,0:T(2,128)S(1)}, u32[]{:S(2)}, u32[]{:S(2)}) collective-permute-start(f32[2,2]{1,0:T(2,128)S(1)} %divide_select_fusion.3), channel_id=1, source_target_pairs={{0,16},{1,17},{2,18},{3,19},{4,20},{5,21},{6,22},{7,23},{8,24},{9,... | collective-permute-start | bytes 56 | tf_op jit(solution)/shard_map/ppermute | solution.py:48
  131.6 7.4 %collective-permute-start.10 = (f32[2,2]{1,0:T(2,128)S(1)}, f32[2,2]{1,0:T(2,128)S(1)}, u32[]{:S(2)}, u32[]{:S(2)}) collective-permute-start(f32[2,2]{1,0:T(2,128)S(1)} %divide_select_fusion.2), channel_id=1, source_target_pairs={{0,32},{1,33},{2,34},{3,35},{4,36},{5,37},{6,38},{7,39},{8,40},{9,... | collective-permute-start | bytes 56 | tf_op jit(solution)/shard_map/ppermute | solution.py:48
  140.3 19.6 %collective-permute-start.11 = (f32[2,2]{1,0:T(2,128)S(1)}, f32[2,2]{1,0:T(2,128)S(1)}, u32[]{:S(2)}, u32[]{:S(2)}) collective-permute-start(f32[2,2]{1,0:T(2,128)S(1)} %divide_select_fusion.1), channel_id=1, source_target_pairs={{0,64},{1,65},{2,66},{3,67},{4,68},{5,69},{6,70},{7,71},{8,72},{9,... | collective-permute-start | bytes 56 | tf_op jit(solution)/shard_map/ppermute | solution.py:48

commit v3 on v2

--- a/solution.py
+++ b/solution.py
@@ -53,7 +53,37 @@
     return total
 
 
-def scan_kernel(count, backward, x_ref, out_ref, totals, recv, send_sem, recv_sem):
+def ratio_join(earlier, latter):
+    def entry(i, j):
+        return latter[2 * i : 2 * i + 1] * earlier[j : j + 1] + latter[2 * i + 1 : 2 * i + 2] * earlier[2 + j : 3 + j]
+
+    entries = [entry(0, 0), entry(0, 1), entry(1, 0), entry(1, 1)]
+    big = jnp.maximum(
+        jnp.maximum(jnp.abs(entries[0]), jnp.abs(entries[1])),
+        jnp.maximum(jnp.abs(entries[2]), jnp.abs(entries[3])),
+    )
+    rows = [part / big for part in entries]
+    return jnp.concatenate(rows + [jnp.zeros((4, 128), jnp.float32)], axis=0)
+
+
+def line_join(earlier, latter):
+    factor = latter[LINES : LINES + 1, :]
+    joined_lines = latter[:LINES] + factor * earlier[:LINES]
+    joined_scale = latter[LINES:] * earlier[LINES:]
+    return jnp.concatenate([joined_lines, joined_scale], axis=0)
+
+
+def ratio_neutral():
+    unit = jnp.ones((1, 128), jnp.float32)
+    blank = jnp.zeros((1, 128), jnp.float32)
+    return jnp.concatenate([unit, blank, blank, unit, blank, blank, blank, blank], axis=0)
+
+
+def line_neutral():
+    return jnp.concatenate([jnp.zeros((LINES, 128), jnp.float32), jnp.ones((8, 128), jnp.float32)], axis=0)
+
+
+def scan_kernel(count, backward, join, neutral, x_ref, out_ref, totals, recv, send_sem, recv_sem):
     me = lax.axis_index("gy")
     row = lax.axis_index("gx")
     sign = -1 if backward else 1
@@ -88,17 +118,10 @@
         valid = (me + offset <= count - 1) if backward else (me >= offset)
         earlier = recv[step]
         if step == 0:
-            lines = jnp.zeros((LINES, 128), jnp.float32)
-            scale = jnp.ones((8, 128), jnp.float32)
-            neutral = jnp.concatenate([lines, scale], axis=0)
-            totals[step] = jnp.where(valid, earlier, neutral)
+            totals[step] = jnp.where(valid, earlier, neutral())
         else:
             latter = totals[step - 1]
-            factor = latter[LINES : LINES + 1, :]
-            joined_lines = latter[:LINES] + factor * earlier[:LINES]
-            joined_scale = latter[LINES:] * earlier[LINES:]
-            joined = jnp.concatenate([joined_lines, joined_scale], axis=0)
-            totals[step] = jnp.where(valid, joined, latter)
+            totals[step] = jnp.where(valid, join(earlier, latter), latter)
     out_ref[...] = totals[len(rounds) - 1]
     for copy in copies:
         copy.wait_send()
@@ -116,7 +139,7 @@
         rounds += 1
     rounds += 1
     result = pl.pallas_call(
-        functools.partial(scan_kernel, count, backward),
+        functools.partial(scan_kernel, count, backward, line_join, line_neutral),
         out_shape=jax.ShapeDtypeStruct(packed.shape, jnp.float32),
         in_specs=[pl.BlockSpec(memory_space=pltpu.VMEM)],
         out_specs=pl.BlockSpec(memory_space=pltpu.VMEM),
@@ -131,6 +154,49 @@
     return result[:LINES].reshape(shape)
 
 
+def ratio_scan(matrix):
+    count = lax.axis_size("gy")
+    packed = jnp.concatenate(
+        [jnp.broadcast_to(matrix.reshape(4, 1), (4, 128)), jnp.zeros((4, 128), jnp.float32)], axis=0
+    )
+    rounds = 1
+    while (1 << (rounds - 1)) * 2 < count:
+        rounds += 1
+    rounds += 1
+    result = pl.pallas_call(
+        functools.partial(scan_kernel, count, False, ratio_join, ratio_neutral),
+        out_shape=jax.ShapeDtypeStruct(packed.shape, jnp.float32),
+        in_specs=[pl.BlockSpec(memory_space=pltpu.VMEM)],
+        out_specs=pl.BlockSpec(memory_space=pltpu.VMEM),
+        scratch_shapes=[
+            pltpu.VMEM((rounds,) + packed.shape, jnp.float32),
+            pltpu.VMEM((rounds,) + packed.shape, jnp.float32),
+            pltpu.SemaphoreType.DMA((rounds,)),
+            pltpu.SemaphoreType.DMA((rounds,)),
+        ],
+        compiler_params=pltpu.CompilerParams(collective_id=2, has_side_effects=True),
+    )(packed)
+    return result[:4, 0].reshape(2, 2)
+
+
+def ratio_prefix(matrix):
+    count, mine = (lax.axis_size("gy"), lax.axis_index("gy"))
+    pieces = lax.all_gather(matrix, "gy")
+
+    def join(earlier, latter):
+        def entry(i, j):
+            return latter[:, 2 * i] * earlier[:, j] + latter[:, 2 * i + 1] * earlier[:, 2 + j]
+
+        entries = jnp.stack([entry(0, 0), entry(0, 1), entry(1, 0), entry(1, 1)], axis=1)
+        return entries / jnp.max(jnp.abs(entries), axis=1, keepdims=True)
+
+    inclusive = lax.associative_scan(join, pieces, axis=0)
+    identity = jnp.array([[1.0, 0.0, 0.0, 1.0]], jnp.float32)
+    exclusive = jnp.concatenate([identity, inclusive[: count - 1]], axis=0)
+    own = lax.dynamic_index_in_dim(exclusive, mine, axis=0, keepdims=False)
+    return own[1] / own[3]
+
+
 def stream_slope(padded, planes):
     summed = STENCIL[0] * (padded[..., 5 : 5 + planes] - padded[..., 3 : 3 + planes])
     for offset in range(2, 5):
@@ -179,51 +245,53 @@
     lower_coef = -2.0 * STIFF / (gap_sum * lower_gap)
     upper_coef = -2.0 * STIFF / (gap_sum * upper_gap)
     diagonal = 1.0 - lower_coef - upper_coef
-    below_band = lower_coef.at[0].set(0.0)
-    above_band = upper_coef.at[-1].set(0.0)
     rows_here = velocity.shape[1]
-    line_values = forcing.reshape(3, rows_here, -1)
-    solved = lax.linalg.tridiagonal_solve(
-        jnp.stack([below_band] * 3),
-        jnp.stack([diagonal] * 3),
-        jnp.stack([above_band] * 3),
-        line_values,
-    )
-    columns = jnp.zeros((rows_here, 2), jnp.float32)
-    columns = columns.at[0, 0].set(lower_coef[0]).at[rows_here - 1, 1].set(upper_coef[-1])
-    spikes = lax.linalg.tridiagonal_solve(below_band, diagonal, above_band, columns)
-    left_spike = spikes[:, 0]
-    right_spike = spikes[:, 1]
-    left_first = left_spike[0]
-    left_last = left_spike[-1]
-    right_first = right_spike[0]
-    right_last = right_spike[-1]
-    cross_term = left_last * right_first - right_last * left_first
-    unit_matrix = jnp.eye(2, dtype=jnp.float32)
-    below_prefix = prefix(
-        ratio_matrix(cross_term, right_last, -left_first), "gy", chain_ratio, unit_matrix, False
-    )
-    below_ratio = below_prefix[0, 1] / below_prefix[1, 1]
-    first_solved = solved[:, 0]
-    last_solved = solved[:, -1]
-    lower_denom = 1.0 - left_first * below_ratio
-    lower_step = (
-        jnp.reshape(-left_last / lower_denom, (1, 1)),
-        last_solved + left_last * below_ratio / lower_denom * first_solved,
-    )
-    identity_step = (jnp.ones((1, 1), jnp.float32), jnp.zeros_like(first_solved))
-    below_offset = line_scan(lower_step, False)
-    first_base = (first_solved - left_first * below_offset) / lower_denom
-    first_slope = right_first / lower_denom
-    upper_step = (jnp.reshape(-first_slope, (1, 1)), first_base)
-    above_value = line_scan(upper_step, True)
-    first_value = first_base - first_slope * above_value
-    below_value = below_offset - below_ratio * first_value
-    finished = (
-        solved
-        - below_value[:, None, :] * left_spike[None, :, None]
-        - above_value[:, None, :] * right_spike[None, :, None]
-    )
+
+    top = (jnp.ones((), jnp.float32), jnp.zeros((), jnp.float32))
+    bottom = (jnp.zeros((), jnp.float32), jnp.ones((), jnp.float32))
+    for i in range(rows_here):
+        scale = 1.0 / diagonal[i]
+        up, low = upper_coef[i] * scale, -lower_coef[i] * scale
+        top, bottom = (
+            (up * bottom[0], up * bottom[1]),
+            (low * top[0] + bottom[0], low * top[1] + bottom[1]),
+        )
+    big = jnp.maximum(
+        jnp.maximum(jnp.abs(top[0]), jnp.abs(top[1])), jnp.maximum(jnp.abs(bottom[0]), jnp.abs(bottom[1]))
+    )
+    matrix = jnp.stack([top[0], top[1], bottom[0], bottom[1]]) / big
+    modified_prev = ratio_prefix(matrix)
+
+    pivots, modified = [], []
+    for i in range(rows_here):
+        pivot = diagonal[i] - lower_coef[i] * modified_prev
+        modified_prev = upper_coef[i] / pivot
+        pivots.append(pivot)
+        modified.append(modified_prev)
+
+    line_rows = forcing.reshape(3, rows_here, -1)
+    zero_lines = jnp.zeros_like(line_rows[:, 0])
+    carried = zero_lines
+    weight = jnp.ones((), jnp.float32)
+    reduced, weights = [], []
+    for i in range(rows_here):
+        carried = (line_rows[:, i] - lower_coef[i] * carried) / pivots[i]
+        weight = -lower_coef[i] / pivots[i] * weight
+        reduced.append(carried)
+        weights.append(weight)
+    below_carry = line_scan((jnp.reshape(weight, (1, 1)), carried), False)
+    reduced = [value + w * below_carry for value, w in zip(reduced, weights)]
+
+    carried = zero_lines
+    weight = jnp.ones((), jnp.float32)
+    local, back_weights = [None] * rows_here, [None] * rows_here
+    for i in reversed(range(rows_here)):
+        carried = reduced[i] - modified[i] * carried
+        weight = -modified[i] * weight
+        local[i] = carried
+        back_weights[i] = weight
+    above_carry = line_scan((jnp.reshape(weight, (1, 1)), carried), True)
+    finished = jnp.stack([value + w * above_carry for value, w in zip(local, back_weights)], axis=1)
     return (finished.reshape(velocity.shape), advection)
 
 

time: 279 us -> 265 us (0.950)
  starting transfers between devices: 72.7 us -> 14.6 us
  blocking collectives: 0 us -> 47.3 us
  between operations: 50.8 us -> 69 us
  waiting for transfers between devices: 8.5 us -> 0.01 us
  other arithmetic: 43.9 us -> 35.9 us
  matrix products: 5.1 us -> 0 us
    ppermute x8 -> x0, starting transfers between devices: 59.8 us -> none  [the longest x7 57.1 us: prefix(): earlier = jax.tree.map(lambda part: lax.ppermute(part, axis, pairs), total)]
    all_gather x0 -> x1, blocking collectives: none -> 47.3 us  [ratio_prefix(): pieces = lax.all_gather(matrix, 'gy')]
    ppermute x8 -> x0, waiting for transfers between devices: 8.49 us -> none  [the longest x7 8.49 us: prefix(): earlier = jax.tree.map(lambda part: lax.ppermute(part, axis, pairs), total)]
    add x1 -> x18, other arithmetic: 6.87 us -> 0.21 us  [the longest x7 0.11 us: ratio_prefix(): inclusive = lax.associative_scan(join, pieces, axis=0)]
    dot_general x7 -> x0, matrix products: 5.1 us -> none  [chain_ratio(): product = jnp.dot(latter, earlier, precision=lax.Precision.HIGHEST)]
    sub x2 -> x1, other arithmetic: 1.53 us -> 6.53 us  [shards(): carried = reduced[i] - modified[i] * carried]
    select_n x8 -> x0, other arithmetic: 3.96 us -> none  [the longest x7 3.95 us: prefix(): jnp.where(reach, new, old)]
    unnamed x6 -> x13, other arithmetic: 15.3 us -> 11.9 us
  transfers between devices with their start and end apart: 12 -> 4, of which waited for: 7 -> 0; matrix products, arithmetic and copies ran while one was open for 12% -> 8% of each run, Pallas kernels for 0% -> 0%
where the time goes in v3:
time: 265 us; the launch traced here: 263 us
  Pallas kernels  73.7 us (28%)
  between operations  69 us (26%)
  blocking collectives  47.3 us (18%)
  other arithmetic  35.9 us (14%)
  local copies, waits for them, and re-layouts  22 us (8%)
  starting transfers between devices  14.6 us (6%)
    pallas_call x2, Pallas kernels, line_scan(): pl.pallas_call(functools.partial(scan_kernel, count, backward, line_join,...  73.7 us
    all_gather x1, blocking collectives, ratio_prefix(): pieces = lax.all_gather(matrix, 'gy')  47.3 us
    unnamed x13, other arithmetic  11.9 us
    ppermute x2, starting transfers between devices, extended(): before = lax.ppermute(last, axis, up)  10.6 us
    div x2, other arithmetic, shards(): carried = (line_rows[:, i] - lower_coef[i] * carried) / pivots[i]  7.06 us
    sub x1, other arithmetic, shards(): carried = reduced[i] - modified[i] * carried  6.53 us
  transfers between devices with their start and end apart: 4, of which 0 were waited for; matrix products, arithmetic and copies ran while one was open for 8% of the time, Pallas kernels for 0%

profile of v3, /device:TPU:6, one launch (start us, length us, event | category | flops | bytes accessed | tf_op | source)
XLA Modules:
  0.0 262.5 jit_solution(1452087821147866015)
XLA Ops:
  0.6 1.6 fusion.37
  2.6 2.7 %collective-permute-start = (f32[3,12,32,4]{2,1,3,0:T(8,128)S(1)}, f32[3,12,32,4]{2,1,3,0:T(8,128)S(1)}, u32[]{:S(2)}, u32[]{:S(2)}) collective-permute-start(f32[3,12,32,4]{2,1,3,0:T(8,128)S(1)} %copy.131), channel_id=1, source_target_pairs={{128,0},{256,128},{384,256},{0,384},{129,1},{257,129},{385,257},{1... | collective-permute-start | bytes 55304 | tf_op jit(solution)/shard_map/ppermute | solution.py:29
  5.7 6.9 %collective-permute-start.1 = (f32[3,12,32,4]{2,1,3,0:T(8,128)S(1)}, f32[3,12,32,4]{2,1,3,0:T(8,128)}, u32[]{:S(2)}, u32[]{:S(2)}) collective-permute-start(f32[3,12,32,4]{2,1,3,0:T(8,128)S(1)} %copy.132), channel_id=1, source_target_pairs={{0,128},{128,256},{256,384},{384,0},{1,129},{129,257},{257,385},{3... | collective-permute-start | bytes 55304 | tf_op jit(solution)/shard_map/ppermute | solution.py:28
  13.3 1.3 collective-permute-start.2
  14.6 3.7 %collective-permute-start.3 = (f32[3,1,32,128]{3,2,1,0:T(8,128)}, f32[3,1,32,128]{3,2,1,0:T(8,128)}, u32[]{:S(2)}, u32[]{:S(2)}) collective-permute-start(f32[3,1,32,128]{3,2,1,0:T(8,128)} %get-tuple-element.67), channel_id=1, source_target_pairs={{0,1},{1,2},{2,3},{3,4},{4,5},{5,6},{6,7},{7,8},{8,9},{9,10},{10,1... | collective-permute-start | bytes 147464 | tf_op jit(solution)/shard_map/ppermute | solution.py:28
  19.6 0.7 fusion.53
  21.5 0.7 fusion.51
  43.4 47.3 %all-gather = f32[128,1,4]{2,1,0:T(1,128)S(1)} all-gather(f32[1,1,4]{2,1,0:T(1,128)S(1)} %fusion.34), channel_id=1, replica_groups=mesh['gx'=4,'gy'=128] {'gy'}, dimensions={0}, use_global_device_ids=true | all-gather | bytes 2064 | tf_op jit(solution)/shard_map/all_gather | solution.py:184
  115.6 0.8 slice_bitcast_fusion.2
  116.5 0.9 fusion.41
  117.5 1.1 fusion.43
  118.6 1.1 fusion.45
  151.7 1.2 copy.127
  152.9 4.9 %multiply_add_fusion = (f32[3,12,32,128]{3,2,1,0:T(8,128)S(1)}, f32[3,12,32,128]{3,2,1,0:T(8,128)}) fusion(f32[3,12,32,128]{3,2,1,0:T(8,128)} %param.6, f32[3,12,32,128]{3,2,1,0:T(8,128)S(1)} %copy-done, f32[3,12,28,128]{3,2,1,0:T(8,128)} %get-tuple-element.81, f32[3,12,4,128]{3,2,1,0:T(4,128)} %get-tuple-element.83, ...), kind=kLoop, calls=%fused_computation.52 | loop fusion | flops 7667712 | bytes 7802928 | tf_op jit(solution)/shard_map/add | solution.py:244
  158.9 6.9 %subtract_divide_fusion.10 = (f32[96,128]{1,0:T(8,128)S(1)}, f32[96,128]{1,0:T(8,128)S(1)}) fusion(f32[96,128]{1,0:T(8,128)S(1)} %squeeze.131, f32[]{:T(128)S(6)} %sub.480, f32[]{:T(128)} %bitcast.39, f32[]{:T(128)S(6)} %sub.478, f32[96,128]{1,0:T(8,128)S(1)} %squeeze.132, f32[]{:T(128)S(6)} %sub.476, f32[96,128]{1,0:T(8,128)S(1)} %squeeze.133, ...), kind=kLoop, calls=%fused_computation.105 | loop fusion | flops 405504 | bytes 688216 | tf_op jit(solution)/shard_map/div | solution.py:278
  166.4 38.1 %shard_map.68 = f32[104,128]{1,0:T(8,128)} custom-call(f32[104,128]{1,0:T(8,128)} %concatenate.138.x_ref), custom_call_target="tpu_custom_call" | custom-call | tf_op jit(solution)/shard_map/pallas_call | solution.py:141
  204.5 6.5 %multiply_subtract_fusion.10 = (f32[96,128]{1,0:T(8,128)S(1)}, f32[96,128]{1,0:T(8,128)S(1)}, f32[96,128]{1,0:T(8,128)S(1)}, f32[96,128]{1,0:T(8,128)S(1)}, f32[...) fusion(f32[96,128]{1,0:T(8,128)S(1)} %get-tuple-element.41, ...), kind=kLoop, calls=%fused_computation.104 | loop fusion | flops 909312 | bytes 1278120 | tf_op jit(solution)/shard_map/sub | solution.py:289
  211.7 35.6 %shard_map.69 = f32[104,128]{1,0:T(8,128)} custom-call(f32[104,128]{1,0:T(8,128)} %concatenate.139.x_ref), custom_call_target="tpu_custom_call" | custom-call | tf_op jit(solution)/shard_map/pallas_call | solution.py:141
  247.3 0.8 broadcast_multiply_fusion.1
  248.1 0.8 broadcast_multiply_fusion
  249.7 7.0 %add_bitcast_fusion = (f32[1,3,32,128]{3,1,2,0:T(4,128)S(1)}, f32[3,1,4096]{2,0,1:T(4,128)S(1)}, f32[3,1,4096]{2,0,1:T(4,128)S(1)}, f32[3,1,4096]{2,0,1:T(4,128)...) fusion(f32[3,1,4096]{2,0,1:T(4,128)S(1)} %mul.2118, f32[]{:T(128)S(6)} %mul.2038, ...), kind=kLoop, calls=%fused_computation.59 | loop fusion | flops 442368 | bytes 983132
  256.7 1.3 add_bitcast_fusion.1
  260.1 0.7 add_bitcast_fusion.8
  261.7 0.8 copy-done.1
  (174 shorter events, 20.0 us)
Async XLA Ops:
  2.2 10.5 %copy-start = (f32[3,12,32,128]{3,2,1,0:T(8,128)S(1)}, f32[3,12,32,128]{3,2,1,0:T(8,128)}, u32[]{:S(2)}) copy-start(f32[3,12,32,128]{3,2,1,0:T(8,128)} %param.5) | copy-start | bytes 1769476
  2.2 16.1 %copy-start.3 = (f32[12]{0:T(128)S(1)}, f32[12]{0:T(128)}, u32[]{:S(2)}) copy-start(f32[12]{0:T(128)} %param.7) | copy-start | bytes 148
  2.2 16.1 %copy-start.4 = (f32[12]{0:T(128)S(1)}, f32[12]{0:T(128)}, u32[]{:S(2)}) copy-start(f32[12]{0:T(128)} %param.8) | copy-start | bytes 148
  2.6 148.8 %collective-permute-start = (f32[3,12,32,4]{2,1,3,0:T(8,128)S(1)}, f32[3,12,32,4]{2,1,3,0:T(8,128)S(1)}, u32[]{:S(2)}, u32[]{:S(2)}) collective-permute-start(f32[3,12,32,4]{2,1,3,0:T(8,128)S(1)} %copy.131), channel_id=1, source_target_pairs={{128,0},{256,128},{384,256},{0,384},{129,1},{257,129},{385,257},{1... | collective-permute-start | bytes 55304 | tf_op jit(solution)/shard_map/ppermute | solution.py:29
  5.7 146.0 %collective-permute-start.1 = (f32[3,12,32,4]{2,1,3,0:T(8,128)S(1)}, f32[3,12,32,4]{2,1,3,0:T(8,128)}, u32[]{:S(2)}, u32[]{:S(2)}) collective-permute-start(f32[3,12,32,4]{2,1,3,0:T(8,128)S(1)} %copy.132), channel_id=1, source_target_pairs={{0,128},{128,256},{256,384},{384,0},{1,129},{129,257},{257,385},{3... | collective-permute-start | bytes 55304 | tf_op jit(solution)/shard_map/ppermute | solution.py:28
  13.3 139.6 %collective-permute-start.2 = (f32[3,1,32,128]{3,2,1,0:T(8,128)}, f32[3,1,32,128]{3,2,1,0:T(8,128)}, u32[]{:S(2)}, u32[]{:S(2)}) collective-permute-start(f32[3,1,32,128]{3,2,1,0:T(8,128)} %get-tuple-element.66), channel_id=1, source_target_pairs={{1,0},{2,1},{3,2},{4,3},{5,4},{6,5},{7,6},{8,7},{9,8},{10,9},{11,1... | collective-permute-start | bytes 147464 | tf_op jit(solution)/shard_map/ppermute | solution.py:29
  14.6 138.3 %collective-permute-start.3 = (f32[3,1,32,128]{3,2,1,0:T(8,128)}, f32[3,1,32,128]{3,2,1,0:T(8,128)}, u32[]{:S(2)}, u32[]{:S(2)}) collective-permute-start(f32[3,1,32,128]{3,2,1,0:T(8,128)} %get-tuple-element.67), channel_id=1, source_target_pairs={{0,1},{1,2},{2,3},{3,4},{4,5},{5,6},{6,7},{7,8},{8,9},{9,10},{10,1... | collective-permute-start | bytes 147464 | tf_op jit(solution)/shard_map/ppermute | solution.py:28
  119.7 6.1 %copy-start.2 = (f32[1,4]{0,1:T(4,128)S(1)}, f32[1,4]{0,1:T(4,128)}, u32[]{:S(2)}) copy-start(f32[1,4]{0,1:T(4,128)} %constant.34.clone) | copy-start | bytes 52
  261.7 0.8 copy-start.1

commit v4 on v3

--- a/solution.py
+++ b/solution.py
@@ -230,6 +230,128 @@
     return jnp.stack([jnp.stack([cross_term, top_right]), jnp.stack([bottom_left, unit_entry])])
 
 
+def radix_plan(count):
+    plan = [list(range(1, min(4, count - 1) + 1))]
+    span = len(plan[0])
+    while span < count - 1:
+        offsets = [span * j for j in range(1, 4) if span * j < count]
+        plan.append(offsets)
+        span = span * (1 + len(offsets))
+    return plan
+
+
+def radix_scan(me, row, count, backward, element, parts, recv, send_sem, recv_sem, base, copies):
+    sign = -1 if backward else 1
+    plan = radix_plan(count)
+    slot = base
+    for level, offsets in enumerate(plan):
+        source = element if level == 0 else parts.at[level - 1]
+        started = []
+        for offset in offsets:
+            target = (me + count + sign * offset) % count
+            copy = pltpu.make_async_remote_copy(
+                src_ref=source,
+                dst_ref=recv.at[slot],
+                send_sem=send_sem.at[slot],
+                recv_sem=recv_sem.at[slot],
+                device_id=(row, target),
+                device_id_type=MESH,
+            )
+            copy.start()
+            started.append((offset, slot, copy))
+            slot += 1
+        acc = line_neutral() if level == 0 else parts[level - 1]
+        for offset, index, copy in started:
+            copy.wait_recv()
+            copies.append(copy)
+            valid = (me + offset <= count - 1) if backward else (me >= offset)
+            acc = jnp.where(valid, line_join(recv[index], acc), acc)
+        parts[level] = acc
+    return parts[len(plan) - 1]
+
+
+def carry_kernel(count, rows_here, element_ref, rows_ref, coef_ref, out_ref, parts_down, up_element, parts_up,
+                 recv, send_sem, recv_sem):
+    me = lax.axis_index("gy")
+    row = lax.axis_index("gx")
+    plan = radix_plan(count)
+    residues = set()
+    for offsets in plan:
+        for offset in offsets:
+            residues.add(offset % count)
+            residues.add((count - offset) % count)
+    residues.discard(0)
+    barrier = pltpu.get_barrier_semaphore()
+    for residue in sorted(residues):
+        pl.semaphore_signal(barrier, inc=1, device_id=(row, (me + residue) % count), device_id_type=MESH)
+    pl.semaphore_wait(barrier, len(residues))
+    copies = []
+    slots = sum(len(offsets) for offsets in plan)
+
+    below_carry = radix_scan(
+        me, row, count, False, element_ref, parts_down, recv, send_sem, recv_sem, 0, copies
+    )[:LINES]
+    coef = coef_ref[...]
+    carried = None
+    weight = None
+    for i in reversed(range(rows_here)):
+        sensitivity = coef[i : i + 1]
+        modified = coef[16 + i : 17 + i]
+        reduced = rows_ref[i] + sensitivity * below_carry
+        if carried is None:
+            carried = reduced
+            weight = -modified
+        else:
+            carried = reduced - modified * carried
+            weight = -modified * weight
+        out_ref[i] = carried
+    up_element[...] = jnp.concatenate([carried, jnp.broadcast_to(weight, (8, 128))], axis=0)
+    above_carry = radix_scan(
+        me, row, count, True, up_element, parts_up, recv, send_sem, recv_sem, slots, copies
+    )[:LINES]
+    weight = None
+    for i in reversed(range(rows_here)):
+        modified = coef[16 + i : 17 + i]
+        weight = -modified if weight is None else -modified * weight
+        out_ref[i] = out_ref[i] + weight * above_carry
+    for copy in copies:
+        copy.wait_send()
+
+
+def carry_solve(element_factor, element_lines, rows, sensitivities, modified):
+    count = lax.axis_size("gy")
+    rows_here = len(rows)
+    packed = jnp.concatenate(
+        [element_lines.reshape(LINES, 128), jnp.broadcast_to(element_factor.reshape(1, 1), (8, 128))], axis=0
+    )
+    stacked = jnp.stack([value.reshape(LINES, 128) for value in rows], axis=0)
+    scalars = (
+        [jnp.reshape(value, (1,)) for value in sensitivities]
+        + [jnp.zeros((16 - rows_here,), jnp.float32)]
+        + [jnp.reshape(value, (1,)) for value in modified]
+        + [jnp.zeros((16 - rows_here,), jnp.float32)]
+    )
+    coef = jnp.broadcast_to(jnp.concatenate(scalars).reshape(32, 1), (32, 128))
+    plan = radix_plan(count)
+    slots = 2 * sum(len(offsets) for offsets in plan)
+    big = (LINES + 8, 128)
+    return pl.pallas_call(
+        functools.partial(carry_kernel, count, rows_here),
+        out_shape=jax.ShapeDtypeStruct((rows_here, LINES, 128), jnp.float32),
+        in_specs=[pl.BlockSpec(memory_space=pltpu.VMEM)] * 3,
+        out_specs=pl.BlockSpec(memory_space=pltpu.VMEM),
+        scratch_shapes=[
+            pltpu.VMEM((len(plan),) + big, jnp.float32),
+            pltpu.VMEM(big, jnp.float32),
+            pltpu.VMEM((len(plan),) + big, jnp.float32),
+            pltpu.VMEM((slots,) + big, jnp.float32),
+            pltpu.SemaphoreType.DMA((slots,)),
+            pltpu.SemaphoreType.DMA((slots,)),
+        ],
+        compiler_params=pltpu.CompilerParams(collective_id=0, has_side_effects=True),
+    )(packed, stacked, coef)
+
+
 def shards(velocity, old_advection, lower_gap, upper_gap):
     planes = velocity.shape[3]
     padded = extended(velocity, (("gx", 3),), 4, True)
@@ -279,19 +401,8 @@
         weight = -lower_coef[i] / pivots[i] * weight
         reduced.append(carried)
         weights.append(weight)
-    below_carry = line_scan((jnp.reshape(weight, (1, 1)), carried), False)
-    reduced = [value + w * below_carry for value, w in zip(reduced, weights)]
-
-    carried = zero_lines
-    weight = jnp.ones((), jnp.float32)
-    local, back_weights = [None] * rows_here, [None] * rows_here
-    for i in reversed(range(rows_here)):
-        carried = reduced[i] - modified[i] * carried
-        weight = -modified[i] * weight
-        local[i] = carried
-        back_weights[i] = weight
-    above_carry = line_scan((jnp.reshape(weight, (1, 1)), carried), True)
-    finished = jnp.stack([value + w * above_carry for value, w in zip(local, back_weights)], axis=1)
+    solved = carry_solve(weight, carried, reduced, weights, modified)
+    finished = jnp.transpose(solved.reshape(rows_here, 3, 32, -1), (1, 0, 2, 3))
     return (finished.reshape(velocity.shape), advection)
 
 

time: 265 us -> 251 us (0.947)
  other arithmetic: 35.9 us -> 26.1 us
  Pallas kernels: 73.7 us -> 65.7 us
  blocking collectives: 47.3 us -> 50.3 us
  local copies, waits for them, and re-layouts: 22 us -> 24.7 us
    pallas_call x2 -> x1, Pallas kernels: 73.7 us -> 65.7 us  [carry_solve(): pl.pallas_call(functools.partial(carry_kernel, count, rows_here), out_sha...]
    sub x1 -> x0, other arithmetic: 6.53 us -> none  [shards(): carried = reduced[i] - modified[i] * carried]
    all_gather x1, blocking collectives: 47.3 us -> 50.3 us  [ratio_prefix(): pieces = lax.all_gather(matrix, 'gy')]
    unnamed x13 -> x11, other arithmetic: 11.9 us -> 9.67 us
  transfers between devices with their start and end apart: 4 -> 4, of which waited for: 0 -> 0; matrix products, arithmetic and copies ran while one was open for 8% -> 9% of each run, Pallas kernels for 0% -> 0%
where the time goes in v4:
time: 251 us; the launch traced here: 248 us
  between operations  68.6 us (27%)
  Pallas kernels  65.7 us (26%)
  blocking collectives  50.3 us (20%)
  other arithmetic  26.1 us (10%)
  local copies, waits for them, and re-layouts  24.7 us (10%)
  starting transfers between devices  12.9 us (5%)
    pallas_call x1, Pallas kernels, carry_solve(): pl.pallas_call(functools.partial(carry_kernel, count, rows_here), out_sha...  65.7 us
    all_gather x1, blocking collectives, ratio_prefix(): pieces = lax.all_gather(matrix, 'gy')  50.3 us
    unnamed x11, other arithmetic  9.67 us
    ppermute x2, starting transfers between devices, extended(): before = lax.ppermute(last, axis, up)  9.66 us
    div x2, other arithmetic, shards(): carried = (line_rows[:, i] - lower_coef[i] * carried) / pivots[i]  7.08 us
    add x1, other arithmetic, shards(): forcing = velocity + GAMMA * advection + ZETA * old_advection  5.09 us
  transfers between devices with their start and end apart: 4, of which 0 were waited for; matrix products, arithmetic and copies ran while one was open for 9% of the time, Pallas kernels for 0%

profile of v4, /device:TPU:6, one launch (start us, length us, event | category | flops | bytes accessed | tf_op | source)
XLA Modules:
  0.0 248.3 jit_solution(10586267445147340173)
XLA Ops:
  0.6 1.5 fusion.58
  2.1 2.3 collective-permute-start.3
  4.4 1.3 collective-permute-start.2
  5.7 1.6 fusion.57
  7.7 7.3 %collective-permute-start.1 = (f32[3,12,32,4]{2,1,3,0:T(8,128)S(1)}, f32[3,12,32,4]{2,1,3,0:T(8,128)S(1)}, u32[]{:S(2)}, u32[]{:S(2)}) collective-permute-start(f32[3,12,32,4]{2,1,3,0:T(8,128)S(1)} %copy.217), channel_id=1, source_target_pairs={{0,128},{128,256},{256,384},{384,0},{1,129},{129,257},{257,385},{3... | collective-permute-start | bytes 55304 | tf_op jit(solution)/shard_map/ppermute | solution.py:28
  15.4 1.9 collective-permute-start
  18.1 0.9 fusion.63
  19.7 1.1 fusion.61
  21.5 1.1 fusion.59
  23.3 0.8 slice_bitcast_fusion.2
  49.2 50.3 %all-gather = f32[128,1,4]{2,1,0:T(1,128)S(1)} all-gather(f32[1,1,4]{2,1,0:T(1,128)S(1)} %fusion.49), channel_id=1, replica_groups=mesh['gx'=4,'gy'=128] {'gy'}, dimensions={0}, use_global_device_ids=true | all-gather | bytes 2064 | tf_op jit(solution)/shard_map/all_gather | solution.py:184
  153.6 1.2 copy.198
  154.8 5.1 %multiply_add_fusion = (f32[3,12,32,128]{3,2,1,0:T(8,128)}, f32[3,12,32,128]{3,2,1,0:T(8,128)}) fusion(f32[3,12,32,128]{3,2,1,0:T(8,128)} %param.6, f32[3,12,32,128]{3,2,1,0:T(8,128)S(1)} %copy-done, f32[3,12,28,128]{3,2,1,0:T(8,128)S(1)} %get-tuple-element.50, f32[3,12,4,128]{3,2,1,0:T(4,128)} %get-tuple-element.52, ...), kind=kLoop, calls=%fused_computation.53 | loop fusion | flops 7667712 | bytes 7802928 | tf_op jit(solution)/shard_map/add | solution.py:366
  159.9 1.2 reshape.953
  161.6 3.3 %fusion.32 = (f32[3,1,4096]{2,0,1:T(4,128)S(1)}, f32[3,1,4096]{2,0,1:T(4,128)S(1)}) fusion(f32[3,1,4096]{2,1,0:T(1,128)S(1)} %get-tuple-element.18, f32[]{:T(128)S(6)} %sub.504, f32[]{:T(128)S(6)} %mul.1226, f32[]{:T(128)S(6)} %sub.513, f32[]{:T(128)S(6)} %sub.511, f32[]{:T(128)S(6)} %sub.509, f32[]{:T(128)S(6)} %sub.507, f32[]{:T(128)} %bitcast.13, ...), kind=kLoop, calls=%fused_computation.58 | loop fusion | flops 196608 | bytes 393260 | tf_op jit(solution)/shard_map/div | solution.py:400
  165.0 3.8 %subtract_divide_fusion = f32[96,128]{1,0:T(8,128)S(1)} fusion(f32[96,128]{1,0:T(8,128)S(1)} %bitcast.195, f32[96,128]{1,0:T(8,128)S(1)} %bitcast.197, f32[96,128]{1,0:T(8,128)S(1)} %bitcast.182, f32[96,128]{1,0:T(8,128)S(1)} %bitcast.199, f32[96,128]{1,0:T(8,128)S(1)} %bitcast.185, f32[96,128]{1,0:T(8,128)S(1)} %bitcast.201, f32[96,128]{1,0:T(8,128)S(1)} %reshape.1001, ...), kind=kLoop, calls=%fused_computation.91 | loop fusion | flops 233472 | bytes 393268 | tf_op jit(solution)/shard_map/div | solution.py:400
  170.2 1.3 constant_dynamic-update-slice_fusion.8
  172.1 1.2 constant_dynamic-update-slice_fusion.6
  174.0 1.2 constant_dynamic-update-slice_fusion.4
  175.9 1.3 constant_dynamic-update-slice_fusion.2
  177.9 1.3 constant_dynamic-update-slice_fusion
  179.8 0.8 broadcast_in_dim.2.coef_ref
  180.6 65.7 %shard_map.68 = f32[12,96,128]{2,1,0:T(8,128)} custom-call(f32[104,128]{1,0:T(8,128)} %concatenate.137.element_ref, f32[12,96,128]{2,1,0:T(8,128)} %copy-done.1, f32[32,128]{1,0:T(8,128)} %broadcast_in_dim.2.coef_ref), custom_call_target="tpu_custom_call" | custom-call | tf_op jit(solution)/shard_map/pallas_call | solution.py:338
  246.4 1.9 copy.257
  (127 shorter events, 20.3 us)
Async XLA Ops:
  2.1 152.7 %collective-permute-start.3 = (f32[3,1,32,128]{3,2,1,0:T(8,128)}, f32[3,1,32,128]{3,2,1,0:T(8,128)}, u32[]{:S(2)}, u32[]{:S(2)}) collective-permute-start(f32[3,1,32,128]{3,2,1,0:T(8,128)} %get-tuple-element.36), channel_id=1, source_target_pairs={{0,1},{1,2},{2,3},{3,4},{4,5},{5,6},{6,7},{7,8},{8,9},{9,10},{10,1... | collective-permute-start | bytes 147464 | tf_op jit(solution)/shard_map/ppermute | solution.py:28
  4.4 150.4 %collective-permute-start.2 = (f32[3,1,32,128]{3,2,1,0:T(8,128)}, f32[3,1,32,128]{3,2,1,0:T(8,128)}, u32[]{:S(2)}, u32[]{:S(2)}) collective-permute-start(f32[3,1,32,128]{3,2,1,0:T(8,128)} %get-tuple-element.35), channel_id=1, source_target_pairs={{1,0},{2,1},{3,2},{4,3},{5,4},{6,5},{7,6},{8,7},{9,8},{10,9},{11,1... | collective-permute-start | bytes 147464 | tf_op jit(solution)/shard_map/ppermute | solution.py:29
  7.3 10.0 %copy-start = (f32[3,12,32,128]{3,2,1,0:T(8,128)S(1)}, f32[3,12,32,128]{3,2,1,0:T(8,128)}, u32[]{:S(2)}) copy-start(f32[3,12,32,128]{3,2,1,0:T(8,128)} %param.5) | copy-start | bytes 1769476
  7.7 145.7 %collective-permute-start.1 = (f32[3,12,32,4]{2,1,3,0:T(8,128)S(1)}, f32[3,12,32,4]{2,1,3,0:T(8,128)S(1)}, u32[]{:S(2)}, u32[]{:S(2)}) collective-permute-start(f32[3,12,32,4]{2,1,3,0:T(8,128)S(1)} %copy.217), channel_id=1, source_target_pairs={{0,128},{128,256},{256,384},{384,0},{1,129},{129,257},{257,385},{3... | collective-permute-start | bytes 55304 | tf_op jit(solution)/shard_map/ppermute | solution.py:28
  15.4 138.3 %collective-permute-start = (f32[3,12,32,4]{2,1,3,0:T(8,128)S(1)}, f32[3,12,32,4]{2,1,3,0:T(8,128)}, u32[]{:S(2)}, u32[]{:S(2)}) collective-permute-start(f32[3,12,32,4]{2,1,3,0:T(8,128)S(1)} %copy.216), channel_id=1, source_target_pairs={{128,0},{256,128},{384,256},{0,384},{129,1},{257,129},{385,257},{1... | collective-permute-start | bytes 55304 | tf_op jit(solution)/shard_map/ppermute | solution.py:29
  22.6 1.5 copy-start.3
  22.6 1.5 copy-start.4
  24.1 103.5 %copy-start.2 = (f32[1,4]{0,1:T(4,128)S(1)}, f32[1,4]{0,1:T(4,128)}, u32[]{:S(2)}) copy-start(f32[1,4]{0,1:T(4,128)} %constant.13.clone) | copy-start | bytes 52
  179.8 0.8 copy-start.1

commit v5 on v4

--- a/solution.py
+++ b/solution.py
@@ -182,19 +182,16 @@
 def ratio_prefix(matrix):
     count, mine = (lax.axis_size("gy"), lax.axis_index("gy"))
     pieces = lax.all_gather(matrix, "gy")
-
-    def join(earlier, latter):
-        def entry(i, j):
-            return latter[:, 2 * i] * earlier[:, j] + latter[:, 2 * i + 1] * earlier[:, 2 + j]
-
-        entries = jnp.stack([entry(0, 0), entry(0, 1), entry(1, 0), entry(1, 1)], axis=1)
-        return entries / jnp.max(jnp.abs(entries), axis=1, keepdims=True)
-
-    inclusive = lax.associative_scan(join, pieces, axis=0)
-    identity = jnp.array([[1.0, 0.0, 0.0, 1.0]], jnp.float32)
-    exclusive = jnp.concatenate([identity, inclusive[: count - 1]], axis=0)
-    own = lax.dynamic_index_in_dim(exclusive, mine, axis=0, keepdims=False)
-    return own[1] / own[3]
+    total = [jnp.ones((), jnp.float32), jnp.zeros((), jnp.float32), jnp.zeros((), jnp.float32), jnp.ones((), jnp.float32)]
+    for position in range(count - 1):
+        piece = pieces[position]
+        entries = [
+            piece[2 * i] * total[j] + piece[2 * i + 1] * total[2 + j] for i in range(2) for j in range(2)
+        ]
+        big = jnp.maximum(jnp.maximum(jnp.abs(entries[0]), jnp.abs(entries[1])), jnp.maximum(jnp.abs(entries[2]), jnp.abs(entries[3])))
+        inside = position < mine
+        total = [jnp.where(inside, value / big, old) for value, old in zip(entries, total)]
+    return total[1] / total[3]
 
 
 def stream_slope(padded, planes):

time: 251 us -> 906 us (3.61)
  between operations: 68.6 us -> 704 us
  local copies, waits for them, and re-layouts: 24.7 us -> 39.2 us
    slice x22 -> x28, local copies, waits for them, and re-layouts: 3.99 us -> 19.9 us  [the longest x15 10.9 us: ratio_prefix(): piece[2 * i + 1] * total[2 + j]]
  transfers between devices with their start and end apart: 4 -> 4, of which waited for: 0 -> 0; matrix products, arithmetic and copies ran while one was open for 9% -> 4% of each run, Pallas kernels for 0% -> 0%
where the time goes in v5:
time: 906 us; the launch traced here: 895 us
  between operations  704 us (78%)
  Pallas kernels  65.7 us (7%)
  blocking collectives  50.3 us (6%)
  local copies, waits for them, and re-layouts  39.2 us (4%)
  other arithmetic  22.9 us (3%)
  starting transfers between devices  12.9 us (1%)
    pallas_call x1, Pallas kernels, carry_solve(): pl.pallas_call(functools.partial(carry_kernel, count, rows_here), out_sha...  65.7 us
    all_gather x1, blocking collectives, ratio_prefix(): pieces = lax.all_gather(matrix, 'gy')  50.3 us
  transfers between devices with their start and end apart: 4, of which 0 were waited for; matrix products, arithmetic and copies ran while one was open for 4% of the time, Pallas kernels for 0%

profile of v5, /device:TPU:6, one launch (start us, length us, event | category | flops | bytes accessed | tf_op | source)
XLA Modules:
  0.0 895.2 jit_solution(230206623560218395)
XLA Ops:
  0.6 1.5 fusion.58
  2.1 2.3 collective-permute-start.3
  4.4 1.3 collective-permute-start.2
  5.7 1.5 fusion.57
  7.6 7.3 collective-permute-start.1
  15.3 1.9 collective-permute-start
  18.1 0.9 fusion.63
  19.7 1.1 fusion.61
  21.5 1.1 fusion.59
  23.2 0.8 slice_bitcast_fusion.2
  49.1 50.3 %all-gather = f32[128,1,4]{2,1,0:T(1,128)S(1)} all-gather(f32[1,1,4]{2,1,0:T(1,128)S(1)} %fusion.49), channel_id=1, replica_groups=mesh['gx'=4,'gy'=128] {'gy'}, dimensions={0}, use_global_device_ids=true | all-gather | bytes 2064 | tf_op jit(solution)/shard_map/all_gather | solution.py:184
  800.2 1.2 copy.33
  801.3 5.3 multiply_add_fusion
  806.7 1.2 reshape.1639
  808.4 3.4 fusion.32
  811.8 3.8 subtract_divide_fusion
  817.0 1.3 constant_dynamic-update-slice_fusion.8
  818.9 1.3 constant_dynamic-update-slice_fusion.6
  820.9 1.3 constant_dynamic-update-slice_fusion.4
  822.8 1.3 constant_dynamic-update-slice_fusion.2
  824.8 1.3 constant_dynamic-update-slice_fusion
  826.7 0.8 broadcast_in_dim.2.coef_ref
  827.5 65.7 %shard_map.59 = f32[12,96,128]{2,1,0:T(8,128)} custom-call(f32[104,128]{1,0:T(8,128)} %concatenate.77.element_ref, f32[12,96,128]{2,1,0:T(8,128)} %copy-done.1, f32[32,128]{1,0:T(8,128)} %broadcast_in_dim.2.coef_ref), custom_call_target="tpu_custom_call" | custom-call | tf_op jit(solution)/shard_map/pallas_call | solution.py:335
  893.3 1.9 copy.90
  (66 shorter events, 31.2 us)
Async XLA Ops:
  2.1 799.2 %collective-permute-start.3 = (f32[3,1,32,128]{3,2,1,0:T(8,128)}, f32[3,1,32,128]{3,2,1,0:T(8,128)}, u32[]{:S(2)}, u32[]{:S(2)}) collective-permute-start(f32[3,1,32,128]{3,2,1,0:T(8,128)} %get-tuple-element.36), channel_id=1, source_target_pairs={{0,1},{1,2},{2,3},{3,4},{4,5},{5,6},{6,7},{7,8},{8,9},{9,10},{10,1... | collective-permute-start | bytes 147464 | tf_op jit(solution)/shard_map/ppermute | solution.py:28
  4.4 796.9 %collective-permute-start.2 = (f32[3,1,32,128]{3,2,1,0:T(8,128)}, f32[3,1,32,128]{3,2,1,0:T(8,128)}, u32[]{:S(2)}, u32[]{:S(2)}) collective-permute-start(f32[3,1,32,128]{3,2,1,0:T(8,128)} %get-tuple-element.35), channel_id=1, source_target_pairs={{1,0},{2,1},{3,2},{4,3},{5,4},{6,5},{7,6},{8,7},{9,8},{10,9},{11,1... | collective-permute-start | bytes 147464 | tf_op jit(solution)/shard_map/ppermute | solution.py:29
  7.2 10.0 %copy-start = (f32[3,12,32,128]{3,2,1,0:T(8,128)S(1)}, f32[3,12,32,128]{3,2,1,0:T(8,128)}, u32[]{:S(2)}) copy-start(f32[3,12,32,128]{3,2,1,0:T(8,128)} %param.4) | copy-start | bytes 1769476
  7.6 792.2 %collective-permute-start.1 = (f32[3,12,32,4]{2,1,3,0:T(8,128)S(1)}, f32[3,12,32,4]{2,1,3,0:T(8,128)S(1)}, u32[]{:S(2)}, u32[]{:S(2)}) collective-permute-start(f32[3,12,32,4]{2,1,3,0:T(8,128)S(1)} %copy.50), channel_id=1, source_target_pairs={{0,128},{128,256},{256,384},{384,0},{1,129},{129,257},{257,385},{3... | collective-permute-start | bytes 55304 | tf_op jit(solution)/shard_map/ppermute | solution.py:28
  15.3 784.8 %collective-permute-start = (f32[3,12,32,4]{2,1,3,0:T(8,128)S(1)}, f32[3,12,32,4]{2,1,3,0:T(8,128)}, u32[]{:S(2)}, u32[]{:S(2)}) collective-permute-start(f32[3,12,32,4]{2,1,3,0:T(8,128)S(1)} %copy.49), channel_id=1, source_target_pairs={{128,0},{256,128},{384,256},{0,384},{129,1},{257,129},{385,257},{1... | collective-permute-start | bytes 55304 | tf_op jit(solution)/shard_map/ppermute | solution.py:29
  22.6 1.5 copy-start.2
  22.6 1.5 copy-start.3
  826.7 0.8 copy-start.1

commit v6 on v5

--- a/solution.py
+++ b/solution.py
@@ -179,19 +179,41 @@
     return result[:4, 0].reshape(2, 2)
 
 
+def prefix_kernel(count, pieces_ref, out_ref):
+    mine = lax.axis_index("gy")
+
+    def turn(position, total):
+        piece = pieces_ref[pl.ds(pl.multiple_of(position * 8, 8), 8), :]
+        entries = [
+            piece[2 * i : 2 * i + 1] * total[j] + piece[2 * i + 1 : 2 * i + 2] * total[2 + j]
+            for i in range(2)
+            for j in range(2)
+        ]
+        big = jnp.maximum(
+            jnp.maximum(jnp.abs(entries[0]), jnp.abs(entries[1])),
+            jnp.maximum(jnp.abs(entries[2]), jnp.abs(entries[3])),
+        )
+        inside = position < mine
+        return tuple(jnp.where(inside, value / big, old) for value, old in zip(entries, total))
+
+    unit = jnp.ones((1, 128), jnp.float32)
+    blank = jnp.zeros((1, 128), jnp.float32)
+    total = lax.fori_loop(0, count - 1, turn, (unit, blank, blank, unit))
+    out_ref[...] = jnp.broadcast_to(total[1] / total[3], (8, 128))
+
+
 def ratio_prefix(matrix):
-    count, mine = (lax.axis_size("gy"), lax.axis_index("gy"))
+    count = lax.axis_size("gy")
     pieces = lax.all_gather(matrix, "gy")
-    total = [jnp.ones((), jnp.float32), jnp.zeros((), jnp.float32), jnp.zeros((), jnp.float32), jnp.ones((), jnp.float32)]
-    for position in range(count - 1):
-        piece = pieces[position]
-        entries = [
-            piece[2 * i] * total[j] + piece[2 * i + 1] * total[2 + j] for i in range(2) for j in range(2)
-        ]
-        big = jnp.maximum(jnp.maximum(jnp.abs(entries[0]), jnp.abs(entries[1])), jnp.maximum(jnp.abs(entries[2]), jnp.abs(entries[3])))
-        inside = position < mine
-        total = [jnp.where(inside, value / big, old) for value, old in zip(entries, total)]
-    return total[1] / total[3]
+    padded = jnp.concatenate([pieces, jnp.zeros((count, 4), jnp.float32)], axis=1)
+    spread = jnp.broadcast_to(padded.reshape(count * 8, 1), (count * 8, 128))
+    result = pl.pallas_call(
+        functools.partial(prefix_kernel, count),
+        out_shape=jax.ShapeDtypeStruct((8, 128), jnp.float32),
+        in_specs=[pl.BlockSpec(memory_space=pltpu.VMEM)],
+        out_specs=pl.BlockSpec(memory_space=pltpu.VMEM),
+    )(spread)
+    return result[0, 0]
 
 
 def stream_slope(padded, planes):

time: 906 us -> 227 us (0.25)
  between operations: 704 us -> 48.1 us
  local copies, waits for them, and re-layouts: 39.2 us -> 21.7 us
    slice x28 -> x1, local copies, waits for them, and re-layouts: 19.9 us -> 1.19 us  [ratio_prefix(): return result[0, 0]]
  transfers between devices with their start and end apart: 4 -> 4, of which waited for: 0 -> 0; matrix products, arithmetic and copies ran while one was open for 4% -> 7% of each run, Pallas kernels for 0% -> 2%
where the time goes in v6:
time: 227 us; the launch traced here: 225 us
  Pallas kernels  69.4 us (31%)
  blocking collectives  50.3 us (22%)
  between operations  48.1 us (21%)
  other arithmetic  22.3 us (10%)
  local copies, waits for them, and re-layouts  21.7 us (10%)
  starting transfers between devices  12.9 us (6%)
    pallas_call x1, Pallas kernels, carry_solve(): pl.pallas_call(functools.partial(carry_kernel, count, rows_here), out_sha...  65.5 us
    all_gather x1, blocking collectives, ratio_prefix(): pieces = lax.all_gather(matrix, 'gy')  50.3 us
    ppermute x2, starting transfers between devices, extended(): before = lax.ppermute(last, axis, up)  9.65 us
    unnamed x11, other arithmetic  9.54 us
    div x2, other arithmetic, shards(): carried = (line_rows[:, i] - lower_coef[i] * carried) / pivots[i]  7.01 us
    add x1, other arithmetic, shards(): forcing = velocity + GAMMA * advection + ZETA * old_advection  5.11 us
  transfers between devices with their start and end apart: 4, of which 0 were waited for; matrix products, arithmetic and copies ran while one was open for 7% of the time, Pallas kernels for 2%

profile of v6, /device:TPU:6, one launch (start us, length us, event | category | flops | bytes accessed | tf_op | source)
XLA Modules:
  0.0 224.7 jit_solution(12264144618288411991)
XLA Ops:
  0.6 1.5 fusion.58
  2.1 2.3 %collective-permute-start.3 = (f32[3,1,32,128]{3,2,1,0:T(8,128)}, f32[3,1,32,128]{3,2,1,0:T(8,128)}, u32[]{:S(2)}, u32[]{:S(2)}) collective-permute-start(f32[3,1,32,128]{3,2,1,0:T(8,128)} %get-tuple-element.36), channel_id=1, source_target_pairs={{0,1},{1,2},{2,3},{3,4},{4,5},{5,6},{6,7},{7,8},{8,9},{9,10},{10,1... | collective-permute-start | bytes 147464 | tf_op jit(solution)/shard_map/ppermute | solution.py:28
  4.4 1.3 collective-permute-start.2
  5.7 1.6 fusion.57
  7.7 7.3 %collective-permute-start.1 = (f32[3,12,32,4]{2,1,3,0:T(8,128)S(1)}, f32[3,12,32,4]{2,1,3,0:T(8,128)S(1)}, u32[]{:S(2)}, u32[]{:S(2)}) collective-permute-start(f32[3,12,32,4]{2,1,3,0:T(8,128)S(1)} %copy.50), channel_id=1, source_target_pairs={{0,128},{128,256},{256,384},{384,0},{1,129},{129,257},{257,385},{3... | collective-permute-start | bytes 55304 | tf_op jit(solution)/shard_map/ppermute | solution.py:28
  15.4 1.9 collective-permute-start
  19.8 1.1 fusion.61
  21.5 1.1 fusion.59
  49.9 50.3 %all-gather = f32[128,1,4]{2,1,0:T(1,128)S(1)} all-gather(f32[1,1,4]{2,1,0:T(1,128)S(1)} %fusion.49), channel_id=1, replica_groups=mesh['gx'=4,'gy'=128] {'gy'}, dimensions={0}, use_global_device_ids=true | all-gather | bytes 2064 | tf_op jit(solution)/shard_map/all_gather | solution.py:207
  100.3 1.0 broadcast_in_dim.7.pieces_ref
  101.3 3.8 %shard_map.59 = f32[8,128]{1,0:T(8,128)} custom-call(f32[1024,128]{1,0:T(8,128)} %broadcast_in_dim.7.pieces_ref), custom_call_target="tpu_custom_call" | custom-call | tf_op jit(solution)/shard_map/pallas_call | solution.py:210
  105.2 1.2 slice.413
  130.4 1.2 copy.33
  131.6 5.1 %multiply_add_fusion = (f32[3,12,32,128]{3,2,1,0:T(8,128)}, f32[3,12,32,128]{3,2,1,0:T(8,128)}) fusion(f32[3,12,32,128]{3,2,1,0:T(8,128)} %param.5, f32[3,12,32,128]{3,2,1,0:T(8,128)S(1)} %copy-done, f32[3,12,28,128]{3,2,1,0:T(8,128)S(1)} %get-tuple-element.50, f32[3,12,4,128]{3,2,1,0:T(4,128)} %get-tuple-element.52, ...), kind=kLoop, calls=%fused_computation.53 | loop fusion | flops 7667712 | bytes 7802928 | tf_op jit(solution)/shard_map/add | solution.py:385
  136.7 1.2 reshape.625
  138.5 3.2 %fusion.32 = (f32[3,1,4096]{2,0,1:T(4,128)S(1)}, f32[3,1,4096]{2,0,1:T(4,128)S(1)}) fusion(f32[3,1,4096]{2,1,0:T(1,128)S(1)} %get-tuple-element.18, f32[]{:T(128)S(6)} %sub.504, f32[]{:T(128)S(6)} %mul.810, f32[]{:T(128)S(6)} %sub.513, f32[]{:T(128)S(6)} %sub.511, f32[]{:T(128)S(6)} %sub.509, f32[]{:T(128)S(6)} %sub.507, f32[]{:T(128)} %bitcast.13, ...), kind=kLoop, calls=%fused_computation.58 | loop fusion | flops 196608 | bytes 393260 | tf_op jit(solution)/shard_map/div | solution.py:419
  141.7 3.8 %subtract_divide_fusion = f32[96,128]{1,0:T(8,128)S(1)} fusion(f32[96,128]{1,0:T(8,128)S(1)} %bitcast.186, f32[96,128]{1,0:T(8,128)S(1)} %bitcast.188, f32[96,128]{1,0:T(8,128)S(1)} %bitcast.173, f32[96,128]{1,0:T(8,128)S(1)} %bitcast.190, f32[96,128]{1,0:T(8,128)S(1)} %bitcast.176, f32[96,128]{1,0:T(8,128)S(1)} %bitcast.192, f32[96,128]{1,0:T(8,128)S(1)} %reshape.672, ...), kind=kLoop, calls=%fused_computation.91 | loop fusion | flops 233472 | bytes 393268 | tf_op jit(solution)/shard_map/div | solution.py:419
  146.9 1.3 constant_dynamic-update-slice_fusion.8
  148.8 1.3 constant_dynamic-update-slice_fusion.6
  150.7 1.2 constant_dynamic-update-slice_fusion.4
  152.6 1.2 constant_dynamic-update-slice_fusion.2
  154.5 1.3 constant_dynamic-update-slice_fusion
  157.2 65.5 %shard_map.60 = f32[12,96,128]{2,1,0:T(8,128)} custom-call(f32[104,128]{1,0:T(8,128)} %concatenate.81.element_ref, f32[12,96,128]{2,1,0:T(8,128)} %copy-done.1, f32[32,128]{1,0:T(8,128)} %broadcast_in_dim.8.coef_ref), custom_call_target="tpu_custom_call" | custom-call | tf_op jit(solution)/shard_map/pallas_call | solution.py:357
  222.8 1.9 copy.90
  (43 shorter events, 13.9 us)
Async XLA Ops:
  2.1 129.5 %collective-permute-start.3 = (f32[3,1,32,128]{3,2,1,0:T(8,128)}, f32[3,1,32,128]{3,2,1,0:T(8,128)}, u32[]{:S(2)}, u32[]{:S(2)}) collective-permute-start(f32[3,1,32,128]{3,2,1,0:T(8,128)} %get-tuple-element.36), channel_id=1, source_target_pairs={{0,1},{1,2},{2,3},{3,4},{4,5},{5,6},{6,7},{7,8},{8,9},{9,10},{10,1... | collective-permute-start | bytes 147464 | tf_op jit(solution)/shard_map/ppermute | solution.py:28
  4.4 127.2 %collective-permute-start.2 = (f32[3,1,32,128]{3,2,1,0:T(8,128)}, f32[3,1,32,128]{3,2,1,0:T(8,128)}, u32[]{:S(2)}, u32[]{:S(2)}) collective-permute-start(f32[3,1,32,128]{3,2,1,0:T(8,128)} %get-tuple-element.35), channel_id=1, source_target_pairs={{1,0},{2,1},{3,2},{4,3},{5,4},{6,5},{7,6},{8,7},{9,8},{10,9},{11,1... | collective-permute-start | bytes 147464 | tf_op jit(solution)/shard_map/ppermute | solution.py:29
  7.3 10.0 %copy-start = (f32[3,12,32,128]{3,2,1,0:T(8,128)S(1)}, f32[3,12,32,128]{3,2,1,0:T(8,128)}, u32[]{:S(2)}) copy-start(f32[3,12,32,128]{3,2,1,0:T(8,128)} %param.4) | copy-start | bytes 1769476
  7.7 122.4 %collective-permute-start.1 = (f32[3,12,32,4]{2,1,3,0:T(8,128)S(1)}, f32[3,12,32,4]{2,1,3,0:T(8,128)S(1)}, u32[]{:S(2)}, u32[]{:S(2)}) collective-permute-start(f32[3,12,32,4]{2,1,3,0:T(8,128)S(1)} %copy.50), channel_id=1, source_target_pairs={{0,128},{128,256},{256,384},{384,0},{1,129},{129,257},{257,385},{3... | collective-permute-start | bytes 55304 | tf_op jit(solution)/shard_map/ppermute | solution.py:28
  15.4 115.0 %collective-permute-start = (f32[3,12,32,4]{2,1,3,0:T(8,128)S(1)}, f32[3,12,32,4]{2,1,3,0:T(8,128)}, u32[]{:S(2)}, u32[]{:S(2)}) collective-permute-start(f32[3,12,32,4]{2,1,3,0:T(8,128)S(1)} %copy.49), channel_id=1, source_target_pairs={{128,0},{256,128},{384,256},{0,384},{129,1},{257,129},{385,257},{1... | collective-permute-start | bytes 55304 | tf_op jit(solution)/shard_map/ppermute | solution.py:29
  22.6 1.5 copy-start.2
  22.6 1.5 copy-start.3
  156.4 0.8 copy-start.1

commit v7 on v6

--- a/solution.py
+++ b/solution.py
@@ -179,11 +179,57 @@
     return result[:4, 0].reshape(2, 2)
 
 
-def prefix_kernel(count, pieces_ref, out_ref):
+def prefix_kernel(count, element_ref, out_ref, pieces, send_sem, recv_sem):
     mine = lax.axis_index("gy")
+    row = lax.axis_index("gx")
+    barrier = pltpu.get_barrier_semaphore()
+
+    def greet(step, carry):
+        pl.semaphore_signal(barrier, inc=1, device_id=(row, (mine + step) % count), device_id_type=MESH)
+        return carry
+
+    lax.fori_loop(1, count, greet, 0)
+    pl.semaphore_wait(barrier, count - 1)
+
+    def outgoing(step):
+        return pltpu.make_async_remote_copy(
+            src_ref=element_ref,
+            dst_ref=pieces.at[mine],
+            send_sem=send_sem.at[step],
+            recv_sem=recv_sem.at[mine],
+            device_id=(row, (mine + step) % count),
+            device_id_type=MESH,
+        )
+
+    def incoming(step):
+        source = (mine + count - step) % count
+        return pltpu.make_async_remote_copy(
+            src_ref=element_ref,
+            dst_ref=pieces.at[source],
+            send_sem=send_sem.at[step],
+            recv_sem=recv_sem.at[source],
+            device_id=(row, source),
+            device_id_type=MESH,
+        )
+
+    def send(step, carry):
+        outgoing(step).start()
+        return carry
+
+    def arrive(step, carry):
+        incoming(step).wait_recv()
+        return carry
+
+    def drain(step, carry):
+        outgoing(step).wait_send()
+        return carry
+
+    lax.fori_loop(1, count, send, 0)
+    lax.fori_loop(1, count, arrive, 0)
+    pieces[mine] = element_ref[...]
 
     def turn(position, total):
-        piece = pieces_ref[pl.ds(pl.multiple_of(position * 8, 8), 8), :]
+        piece = pieces[position]
         entries = [
             piece[2 * i : 2 * i + 1] * total[j] + piece[2 * i + 1 : 2 * i + 2] * total[2 + j]
             for i in range(2)
@@ -200,19 +246,26 @@
     blank = jnp.zeros((1, 128), jnp.float32)
     total = lax.fori_loop(0, count - 1, turn, (unit, blank, blank, unit))
     out_ref[...] = jnp.broadcast_to(total[1] / total[3], (8, 128))
+    lax.fori_loop(1, count, drain, 0)
 
 
 def ratio_prefix(matrix):
     count = lax.axis_size("gy")
-    pieces = lax.all_gather(matrix, "gy")
-    padded = jnp.concatenate([pieces, jnp.zeros((count, 4), jnp.float32)], axis=1)
-    spread = jnp.broadcast_to(padded.reshape(count * 8, 1), (count * 8, 128))
+    element = jnp.broadcast_to(
+        jnp.concatenate([matrix, jnp.zeros((4,), jnp.float32)]).reshape(8, 1), (8, 128)
+    )
     result = pl.pallas_call(
         functools.partial(prefix_kernel, count),
         out_shape=jax.ShapeDtypeStruct((8, 128), jnp.float32),
         in_specs=[pl.BlockSpec(memory_space=pltpu.VMEM)],
         out_specs=pl.BlockSpec(memory_space=pltpu.VMEM),
-    )(spread)
+        scratch_shapes=[
+            pltpu.VMEM((count, 8, 128), jnp.float32),
+            pltpu.SemaphoreType.DMA((count,)),
+            pltpu.SemaphoreType.DMA((count,)),
+        ],
+        compiler_params=pltpu.CompilerParams(collective_id=1, has_side_effects=True),
+    )(element)
     return result[0, 0]
 
 

time: 227 us -> 220 us (0.969)
  the two profiles are of different devices: /device:TPU:6 before, /device:TPU:56 now
where the time goes in v7:
time: 220 us; the launch traced here: 219 us
  Pallas kernels  115 us (52%)
  between operations  48.1 us (22%)
  other arithmetic  22.3 us (10%)
  local copies, waits for them, and re-layouts  21.3 us (10%)
  starting transfers between devices  12.6 us (6%)
    pallas_call x1, Pallas kernels, carry_solve(): pl.pallas_call(functools.partial(carry_kernel, count, rows_here), out_sha...  74.1 us
    pallas_call x1, Pallas kernels, ratio_prefix(): pl.pallas_call(functools.partial(prefix_kernel, count), out_shape=jax.Sha...  40.7 us
    unnamed x10, other arithmetic  9.47 us
    ppermute x2, starting transfers between devices, extended(): after = lax.ppermute(first, axis, down)  7.3 us
    div x2, other arithmetic, shards(): carried = (line_rows[:, i] - lower_coef[i] * carried) / pivots[i]  7.01 us
    ppermute x2, starting transfers between devices, extended(): before = lax.ppermute(last, axis, up)  5.31 us
    add x1, other arithmetic, shards(): forcing = velocity + GAMMA * advection + ZETA * old_advection  5.11 us
  transfers between devices with their start and end apart: 4, of which 0 were waited for; matrix products, arithmetic and copies ran while one was open for 7% of the time, Pallas kernels for 19%

profile of v7, /device:TPU:56, one launch (start us, length us, event | category | flops | bytes accessed | tf_op | source)
XLA Modules:
  0.0 219.0 jit_solution(16280519111325461992)
XLA Ops:
  0.6 1.5 fusion.57
  2.1 1.9 collective-permute-start.3
  4.0 3.6 %collective-permute-start.2 = (f32[3,1,32,128]{3,2,1,0:T(8,128)}, f32[3,1,32,128]{3,2,1,0:T(8,128)}, u32[]{:S(2)}, u32[]{:S(2)}) collective-permute-start(f32[3,1,32,128]{3,2,1,0:T(8,128)} %get-tuple-element.35), channel_id=1, source_target_pairs={{1,0},{2,1},{3,2},{4,3},{5,4},{6,5},{7,6},{8,7},{9,8},{10,9},{11,1... | collective-permute-start | bytes 147464 | tf_op jit(solution)/shard_map/ppermute | solution.py:29
  7.7 1.6 fusion.56
  9.7 3.4 %collective-permute-start.1 = (f32[3,12,32,4]{2,1,3,0:T(8,128)S(1)}, f32[3,12,32,4]{2,1,3,0:T(8,128)S(1)}, u32[]{:S(2)}, u32[]{:S(2)}) collective-permute-start(f32[3,12,32,4]{2,1,3,0:T(8,128)S(1)} %copy.50), channel_id=1, source_target_pairs={{0,128},{128,256},{256,384},{384,0},{1,129},{129,257},{257,385},{3... | collective-permute-start | bytes 55304 | tf_op jit(solution)/shard_map/ppermute | solution.py:28
  13.4 3.7 %collective-permute-start = (f32[3,12,32,4]{2,1,3,0:T(8,128)S(1)}, f32[3,12,32,4]{2,1,3,0:T(8,128)}, u32[]{:S(2)}, u32[]{:S(2)}) collective-permute-start(f32[3,12,32,4]{2,1,3,0:T(8,128)S(1)} %copy.49), channel_id=1, source_target_pairs={{128,0},{256,128},{384,256},{0,384},{129,1},{257,129},{385,257},{1... | collective-permute-start | bytes 55304 | tf_op jit(solution)/shard_map/ppermute | solution.py:29
  17.9 0.9 fusion.62
  19.5 1.1 fusion.60
  21.3 1.1 fusion.58
  23.0 0.8 slice_bitcast_fusion.2
  50.3 40.7 %shard_map.59 = f32[8,128]{1,0:T(8,128)} custom-call(f32[8,128]{1,0:T(8,128)} %broadcast_in_dim.4.element_ref), custom_call_target="tpu_custom_call" | custom-call | tf_op jit(solution)/shard_map/pallas_call | solution.py:257
  91.0 1.2 slice.413
  116.2 1.2 copy.33
  117.4 5.1 %multiply_add_fusion = (f32[3,12,32,128]{3,2,1,0:T(8,128)}, f32[3,12,32,128]{3,2,1,0:T(8,128)}) fusion(f32[3,12,32,128]{3,2,1,0:T(8,128)} %param.5, f32[3,12,32,128]{3,2,1,0:T(8,128)S(1)} %copy-done, f32[3,12,28,128]{3,2,1,0:T(8,128)S(1)} %get-tuple-element.50, f32[3,12,4,128]{3,2,1,0:T(4,128)} %get-tuple-element.52, ...), kind=kLoop, calls=%fused_computation.53 | loop fusion | flops 7667712 | bytes 7802928 | tf_op jit(solution)/shard_map/add | solution.py:438
  122.5 1.2 reshape.566
  124.2 3.2 %fusion.32 = (f32[3,1,4096]{2,0,1:T(4,128)S(1)}, f32[3,1,4096]{2,0,1:T(4,128)S(1)}) fusion(f32[3,1,4096]{2,1,0:T(1,128)S(1)} %get-tuple-element.18, f32[]{:T(128)S(6)} %sub.504, f32[]{:T(128)S(6)} %mul.810, f32[]{:T(128)S(6)} %sub.513, f32[]{:T(128)S(6)} %sub.511, f32[]{:T(128)S(6)} %sub.509, f32[]{:T(128)S(6)} %sub.507, f32[]{:T(128)} %bitcast.13, ...), kind=kLoop, calls=%fused_computation.58 | loop fusion | flops 196608 | bytes 393260 | tf_op jit(solution)/shard_map/div | solution.py:472
  127.5 3.8 %subtract_divide_fusion = f32[96,128]{1,0:T(8,128)S(1)} fusion(f32[96,128]{1,0:T(8,128)S(1)} %bitcast.183, f32[96,128]{1,0:T(8,128)S(1)} %bitcast.185, f32[96,128]{1,0:T(8,128)S(1)} %bitcast.170, f32[96,128]{1,0:T(8,128)S(1)} %bitcast.187, f32[96,128]{1,0:T(8,128)S(1)} %bitcast.173, f32[96,128]{1,0:T(8,128)S(1)} %bitcast.189, f32[96,128]{1,0:T(8,128)S(1)} %reshape.611, ...), kind=kLoop, calls=%fused_computation.91 | loop fusion | flops 233472 | bytes 393268 | tf_op jit(solution)/shard_map/div | solution.py:472
  132.6 1.3 constant_dynamic-update-slice_fusion.8
  134.6 1.3 constant_dynamic-update-slice_fusion.6
  136.5 1.2 constant_dynamic-update-slice_fusion.4
  138.3 1.2 constant_dynamic-update-slice_fusion.2
  140.3 1.3 constant_dynamic-update-slice_fusion
  143.0 74.1 %shard_map.60 = f32[12,96,128]{2,1,0:T(8,128)} custom-call(f32[104,128]{1,0:T(8,128)} %concatenate.74.element_ref, f32[12,96,128]{2,1,0:T(8,128)} %copy-done.1, f32[32,128]{1,0:T(8,128)} %broadcast_in_dim.5.coef_ref), custom_call_target="tpu_custom_call" | custom-call | tf_op jit(solution)/shard_map/pallas_call | solution.py:410
  217.1 1.9 copy.90
  (41 shorter events, 12.7 us)
Async XLA Ops:
  2.1 115.3 %collective-permute-start.3 = (f32[3,1,32,128]{3,2,1,0:T(8,128)}, f32[3,1,32,128]{3,2,1,0:T(8,128)}, u32[]{:S(2)}, u32[]{:S(2)}) collective-permute-start(f32[3,1,32,128]{3,2,1,0:T(8,128)} %get-tuple-element.36), channel_id=1, source_target_pairs={{0,1},{1,2},{2,3},{3,4},{4,5},{5,6},{6,7},{7,8},{8,9},{9,10},{10,1... | collective-permute-start | bytes 147464 | tf_op jit(solution)/shard_map/ppermute | solution.py:28
  4.0 113.4 %collective-permute-start.2 = (f32[3,1,32,128]{3,2,1,0:T(8,128)}, f32[3,1,32,128]{3,2,1,0:T(8,128)}, u32[]{:S(2)}, u32[]{:S(2)}) collective-permute-start(f32[3,1,32,128]{3,2,1,0:T(8,128)} %get-tuple-element.35), channel_id=1, source_target_pairs={{1,0},{2,1},{3,2},{4,3},{5,4},{6,5},{7,6},{8,7},{9,8},{10,9},{11,1... | collective-permute-start | bytes 147464 | tf_op jit(solution)/shard_map/ppermute | solution.py:29
  9.3 7.8 %copy-start = (f32[3,12,32,128]{3,2,1,0:T(8,128)S(1)}, f32[3,12,32,128]{3,2,1,0:T(8,128)}, u32[]{:S(2)}) copy-start(f32[3,12,32,128]{3,2,1,0:T(8,128)} %param.4) | copy-start | bytes 1769476
  9.7 106.2 %collective-permute-start.1 = (f32[3,12,32,4]{2,1,3,0:T(8,128)S(1)}, f32[3,12,32,4]{2,1,3,0:T(8,128)S(1)}, u32[]{:S(2)}, u32[]{:S(2)}) collective-permute-start(f32[3,12,32,4]{2,1,3,0:T(8,128)S(1)} %copy.50), channel_id=1, source_target_pairs={{0,128},{128,256},{256,384},{384,0},{1,129},{129,257},{257,385},{3... | collective-permute-start | bytes 55304 | tf_op jit(solution)/shard_map/ppermute | solution.py:28
  13.4 102.8 %collective-permute-start = (f32[3,12,32,4]{2,1,3,0:T(8,128)S(1)}, f32[3,12,32,4]{2,1,3,0:T(8,128)}, u32[]{:S(2)}, u32[]{:S(2)}) collective-permute-start(f32[3,12,32,4]{2,1,3,0:T(8,128)S(1)} %copy.49), channel_id=1, source_target_pairs={{128,0},{256,128},{384,256},{0,384},{129,1},{257,129},{385,257},{1... | collective-permute-start | bytes 55304 | tf_op jit(solution)/shard_map/ppermute | solution.py:29
  22.4 1.5 copy-start.2
  22.4 1.5 copy-start.3
  142.2 0.8 copy-start.1

commit v8 on v7

--- a/solution.py
+++ b/solution.py
@@ -179,7 +179,7 @@
     return result[:4, 0].reshape(2, 2)
 
 
-def prefix_kernel(count, element_ref, out_ref, pieces, send_sem, recv_sem):
+def prefix_kernel(count, rows_here, element_ref, table_ref, out_ref, pieces, send_sem, recv_sem):
     mine = lax.axis_index("gy")
     row = lax.axis_index("gx")
     barrier = pltpu.get_barrier_semaphore()
@@ -245,19 +245,58 @@
     unit = jnp.ones((1, 128), jnp.float32)
     blank = jnp.zeros((1, 128), jnp.float32)
     total = lax.fori_loop(0, count - 1, turn, (unit, blank, blank, unit))
-    out_ref[...] = jnp.broadcast_to(total[1] / total[3], (8, 128))
+    modified_prev = total[1] / total[3]
+    weight = unit
+    for i in range(rows_here):
+        lower = table_ref[i : i + 1]
+        upper = table_ref[16 + i : 17 + i]
+        diagonal = table_ref[32 + i : 33 + i]
+        pivot = diagonal - lower * modified_prev
+        modified_prev = upper / pivot
+        weight = -lower / pivot * weight
+        out_ref[i : i + 1] = pivot
+        out_ref[16 + i : 17 + i] = modified_prev
+        out_ref[32 + i : 33 + i] = weight
     lax.fori_loop(1, count, drain, 0)
 
 
-def ratio_prefix(matrix):
+def matrix_kernel(rows_here, table_ref, out_ref):
+    unit = jnp.ones((1, 128), jnp.float32)
+    blank = jnp.zeros((1, 128), jnp.float32)
+    top = (unit, blank)
+    bottom = (blank, unit)
+    for i in range(rows_here):
+        scale = 1.0 / table_ref[32 + i : 33 + i]
+        up = table_ref[16 + i : 17 + i] * scale
+        low = -table_ref[i : i + 1] * scale
+        top, bottom = (
+            (up * bottom[0], up * bottom[1]),
+            (low * top[0] + bottom[0], low * top[1] + bottom[1]),
+        )
+    big = jnp.maximum(
+        jnp.maximum(jnp.abs(top[0]), jnp.abs(top[1])), jnp.maximum(jnp.abs(bottom[0]), jnp.abs(bottom[1]))
+    )
+    out_ref[...] = jnp.concatenate(
+        [top[0] / big, top[1] / big, bottom[0] / big, bottom[1] / big, blank, blank, blank, blank], axis=0
+    )
+
+
+def coefficient_table(lower_coef, upper_coef, diagonal):
     count = lax.axis_size("gy")
-    element = jnp.broadcast_to(
-        jnp.concatenate([matrix, jnp.zeros((4,), jnp.float32)]).reshape(8, 1), (8, 128)
-    )
-    result = pl.pallas_call(
-        functools.partial(prefix_kernel, count),
+    rows_here = lower_coef.shape[0]
+    filler = jnp.zeros((16 - rows_here,), jnp.float32)
+    column = jnp.concatenate([lower_coef, filler, upper_coef, filler, diagonal, filler])
+    table = jnp.broadcast_to(column.reshape(48, 1), (48, 128))
+    element = pl.pallas_call(
+        functools.partial(matrix_kernel, rows_here),
         out_shape=jax.ShapeDtypeStruct((8, 128), jnp.float32),
         in_specs=[pl.BlockSpec(memory_space=pltpu.VMEM)],
+        out_specs=pl.BlockSpec(memory_space=pltpu.VMEM),
+    )(table)
+    return pl.pallas_call(
+        functools.partial(prefix_kernel, count, rows_here),
+        out_shape=jax.ShapeDtypeStruct((48, 128), jnp.float32),
+        in_specs=[pl.BlockSpec(memory_space=pltpu.VMEM)] * 2,
         out_specs=pl.BlockSpec(memory_space=pltpu.VMEM),
         scratch_shapes=[
             pltpu.VMEM((count, 8, 128), jnp.float32),
@@ -265,8 +304,7 @@
             pltpu.SemaphoreType.DMA((count,)),
         ],
         compiler_params=pltpu.CompilerParams(collective_id=1, has_side_effects=True),
-    )(element)
-    return result[0, 0]
+    )(element, table)
 
 
 def stream_slope(padded, planes):
@@ -367,7 +405,7 @@
     carried = None
     weight = None
     for i in reversed(range(rows_here)):
-        sensitivity = coef[i : i + 1]
+        sensitivity = coef[32 + i : 33 + i]
         modified = coef[16 + i : 17 + i]
         reduced = rows_ref[i] + sensitivity * below_carry
         if carried is None:
@@ -390,20 +428,13 @@
         copy.wait_send()
 
 
-def carry_solve(element_factor, element_lines, rows, sensitivities, modified):
+def carry_solve(element_factor, element_lines, rows, coef):
     count = lax.axis_size("gy")
     rows_here = len(rows)
     packed = jnp.concatenate(
         [element_lines.reshape(LINES, 128), jnp.broadcast_to(element_factor.reshape(1, 1), (8, 128))], axis=0
     )
     stacked = jnp.stack([value.reshape(LINES, 128) for value in rows], axis=0)
-    scalars = (
-        [jnp.reshape(value, (1,)) for value in sensitivities]
-        + [jnp.zeros((16 - rows_here,), jnp.float32)]
-        + [jnp.reshape(value, (1,)) for value in modified]
-        + [jnp.zeros((16 - rows_here,), jnp.float32)]
-    )
-    coef = jnp.broadcast_to(jnp.concatenate(scalars).reshape(32, 1), (32, 128))
     plan = radix_plan(count)
     slots = 2 * sum(len(offsets) for offsets in plan)
     big = (LINES + 8, 128)
@@ -441,39 +472,15 @@
     diagonal = 1.0 - lower_coef - upper_coef
     rows_here = velocity.shape[1]
 
-    top = (jnp.ones((), jnp.float32), jnp.zeros((), jnp.float32))
-    bottom = (jnp.zeros((), jnp.float32), jnp.ones((), jnp.float32))
+    table = coefficient_table(lower_coef, upper_coef, diagonal)
+    line_rows = forcing.reshape(3, rows_here, -1)
+    carried = jnp.zeros_like(line_rows[:, 0])
+    reduced = []
     for i in range(rows_here):
-        scale = 1.0 / diagonal[i]
-        up, low = upper_coef[i] * scale, -lower_coef[i] * scale
-        top, bottom = (
-            (up * bottom[0], up * bottom[1]),
-            (low * top[0] + bottom[0], low * top[1] + bottom[1]),
-        )
-    big = jnp.maximum(
-        jnp.maximum(jnp.abs(top[0]), jnp.abs(top[1])), jnp.maximum(jnp.abs(bottom[0]), jnp.abs(bottom[1]))
-    )
-    matrix = jnp.stack([top[0], top[1], bottom[0], bottom[1]]) / big
-    modified_prev = ratio_prefix(matrix)
-
-    pivots, modified = [], []
-    for i in range(rows_here):
-        pivot = diagonal[i] - lower_coef[i] * modified_prev
-        modified_prev = upper_coef[i] / pivot
-        pivots.append(pivot)
-        modified.append(modified_prev)
-
-    line_rows = forcing.reshape(3, rows_here, -1)
-    zero_lines = jnp.zeros_like(line_rows[:, 0])
-    carried = zero_lines
-    weight = jnp.ones((), jnp.float32)
-    reduced, weights = [], []
-    for i in range(rows_here):
-        carried = (line_rows[:, i] - lower_coef[i] * carried) / pivots[i]
-        weight = -lower_coef[i] / pivots[i] * weight
+        carried = (line_rows[:, i] - lower_coef[i] * carried) / table[i, 0]
         reduced.append(carried)
-        weights.append(weight)
-    solved = carry_solve(weight, carried, reduced, weights, modified)
+    weight = table[32 + rows_here - 1, 0]
+    solved = carry_solve(weight, carried, reduced, table)
     finished = jnp.transpose(solved.reshape(rows_here, 3, 32, -1), (1, 0, 2, 3))
     return (finished.reshape(velocity.shape), advection)
 

time: 220 us -> 189 us (0.86)
  the two profiles are of different devices: /device:TPU:56 before, /device:TPU:1 now
where the time goes in v8:
time: 189 us; the launch traced here: 188 us
  Pallas kernels  110 us (58%)
  other arithmetic  39.3 us (21%)
  local copies, waits for them, and re-layouts  20.1 us (11%)
  starting transfers between devices  16.6 us (9%)
    pallas_call x1, Pallas kernels, carry_solve(): pl.pallas_call(functools.partial(carry_kernel, count, rows_here), out_sha...  68.9 us
    pallas_call x1, Pallas kernels, coefficient_table(): pl.pallas_call(functools.partial(prefix_kernel, count, rows_here), out_sh...  40 us
    unnamed x10, other arithmetic  18.4 us
    div x2, other arithmetic, shards(): carried = (line_rows[:, i] - lower_coef[i] * carried) / table[i, 0]  14.5 us
    ppermute x2, starting transfers between devices, extended(): after = lax.ppermute(first, axis, down)  12.7 us
    slice x6, local copies, waits for them, and re-layouts, roll_slope(): jnp.roll(values, -offset, along_axis) - jnp.roll(values, offset, along_axis)  5.18 us
    add x1, other arithmetic, shards(): forcing = velocity + GAMMA * advection + ZETA * old_advection  5.05 us
    ppermute x2, starting transfers between devices, extended(): before = lax.ppermute(last, axis, up)  3.85 us
  transfers between devices with their start and end apart: 4, of which 0 were waited for; matrix products, arithmetic and copies ran while one was open for 7% of the time, Pallas kernels for 22%

profile of v8, /device:TPU:1, one launch (start us, length us, event | category | flops | bytes accessed | tf_op | source)
XLA Modules:
  0.0 187.6 jit_solution(1788082011518203419)
XLA Ops:
  0.6 1.6 fusion.56
  2.6 5.2 %collective-permute-start = (f32[3,12,32,4]{2,1,3,0:T(8,128)S(1)}, f32[3,12,32,4]{2,1,3,0:T(8,128)S(1)}, u32[]{:S(2)}, u32[]{:S(2)}) collective-permute-start(f32[3,12,32,4]{2,1,3,0:T(8,128)S(1)} %copy.49), channel_id=1, source_target_pairs={{128,0},{256,128},{384,256},{0,384},{129,1},{257,129},{385,257},{1... | collective-permute-start | bytes 55304 | tf_op jit(solution)/shard_map/ppermute | solution.py:29
  8.2 1.9 %collective-permute-start.1 = (f32[3,12,32,4]{2,1,3,0:T(8,128)S(1)}, f32[3,12,32,4]{2,1,3,0:T(8,128)}, u32[]{:S(2)}, u32[]{:S(2)}) collective-permute-start(f32[3,12,32,4]{2,1,3,0:T(8,128)S(1)} %copy.50), channel_id=1, source_target_pairs={{0,128},{128,256},{256,384},{384,0},{1,129},{129,257},{257,385},{3... | collective-permute-start | bytes 55304 | tf_op jit(solution)/shard_map/ppermute | solution.py:28
  10.8 7.5 %collective-permute-start.2 = (f32[3,1,32,128]{3,2,1,0:T(8,128)}, f32[3,1,32,128]{3,2,1,0:T(8,128)}, u32[]{:S(2)}, u32[]{:S(2)}) collective-permute-start(f32[3,1,32,128]{3,2,1,0:T(8,128)} %get-tuple-element.35), channel_id=1, source_target_pairs={{1,0},{2,1},{3,2},{4,3},{5,4},{6,5},{7,6},{8,7},{9,8},{10,9},{11,1... | collective-permute-start | bytes 147464 | tf_op jit(solution)/shard_map/ppermute | solution.py:29
  18.3 1.9 %collective-permute-start.3 = (f32[3,1,32,128]{3,2,1,0:T(8,128)}, f32[3,1,32,128]{3,2,1,0:T(8,128)}, u32[]{:S(2)}, u32[]{:S(2)}) collective-permute-start(f32[3,1,32,128]{3,2,1,0:T(8,128)} %get-tuple-element.36), channel_id=1, source_target_pairs={{0,1},{1,2},{2,3},{3,4},{4,5},{5,6},{6,7},{7,8},{8,9},{9,10},{10,1... | collective-permute-start | bytes 147464 | tf_op jit(solution)/shard_map/ppermute | solution.py:28
  27.8 1.4 shard_map.59.element_ref
  29.1 40.0 %shard_map.60.coef_ref = f32[48,128]{1,0:T(8,128)} custom-call(f32[8,128]{1,0:T(8,128)} %shard_map.59.element_ref, f32[48,128]{1,0:T(8,128)} %broadcast_in_dim.4.table_ref), custom_call_target="tpu_custom_call" | custom-call | tf_op jit(solution)/shard_map/pallas_call | solution.py:296
  69.1 1.6 fusion.66
  73.5 5.0 %multiply_add_fusion = (f32[3,12,32,128]{3,2,1,0:T(8,128)}, f32[3,12,32,128]{3,2,1,0:T(8,128)}) fusion(f32[3,12,32,128]{3,2,1,0:T(8,128)} %param.5, f32[3,12,32,128]{3,2,1,0:T(8,128)S(1)} %copy-done, f32[3,12,28,128]{3,2,1,0:T(8,128)} %get-tuple-element.50, f32[3,12,4,128]{3,2,1,0:T(4,128)} %get-tuple-element.52, f32[3,12,4,128]{3,2,1,0:T(4,128)} %get-tuple-element.51, ...), kind=kLoop, calls=%fused_computation.53 | loop fusion | flops 7667712 | bytes 7802928 | tf_op jit(solution)/shard_map/add | solution.py:469
  80.3 6.3 %fusion.32 = (f32[3,1,4096]{2,0,1:T(4,128)S(1)}, f32[3,1,4096]{2,0,1:T(4,128)S(1)}) fusion(f32[3,1,4096]{2,1,0:T(1,128)S(1)} %get-tuple-element.18, f32[]{:T(128)} %bitcast.15, f32[]{:T(128)} %bitcast.14, f32[]{:T(128)} %bitcast.19, f32[]{:T(128)} %bitcast.18, f32[]{:T(128)} %bitcast.17, f32[]{:T(128)} %bitcast.16, f32[]{:T(128)} %bitcast.13, ...), kind=kLoop, calls=%fused_computation.58 | loop fusion | flops 196608 | bytes 393260 | tf_op jit(solution)/shard_map/div | solution.py:480
  86.7 1.2 constant_dynamic-update-slice_fusion.9
  87.9 8.1 %subtract_divide_fusion = f32[96,128]{1,0:T(8,128)S(1)} fusion(f32[96,128]{1,0:T(8,128)S(1)} %bitcast.143, f32[96,128]{1,0:T(8,128)S(1)} %bitcast.145, f32[96,128]{1,0:T(8,128)S(1)} %bitcast.130, f32[96,128]{1,0:T(8,128)S(1)} %bitcast.147, f32[96,128]{1,0:T(8,128)S(1)} %bitcast.133, f32[96,128]{1,0:T(8,128)S(1)} %bitcast.149, f32[96,128]{1,0:T(8,128)S(1)} %reshape.513, ...), kind=kLoop, calls=%fused_computation.91 | loop fusion | flops 233472 | bytes 393268 | tf_op jit(solution)/shard_map/div | solution.py:480
  96.1 1.3 concatenate.71.element_ref
  97.4 2.4 %constant_dynamic-update-slice_fusion.8 = (f32[12,96,128]{2,1,0:T(8,128)S(1)}, f32[1,96,128]{2,1,0:T(8,128)S(1)}) fusion(f32[12,96,128]{2,1,0:T(8,128)S(1)} %constant_dynamic-update-slice_fusion.9, f32[]{:T(128)} %bitcast.17, f32[]{:T(128)} %bitcast.16, f32[1,96,128]{2,1,0:T(8,128)S(1)} %div.522, f32[]{:T(128)} %bitcast.13, f32[]{:T(128)} %bitcast.12, ...), kind=kLoop, calls=%fused_computation.100 | loop fusion | flops 73728 | bytes 245776
  99.8 1.3 constant_dynamic-update-slice_fusion.7
  101.0 2.4 %constant_dynamic-update-slice_fusion.6 = (f32[12,96,128]{2,1,0:T(8,128)S(1)}, f32[1,96,128]{2,1,0:T(8,128)S(1)}) fusion(f32[12,96,128]{2,1,0:T(8,128)S(1)} %constant_dynamic-update-slice_fusion.7, f32[]{:T(128)} %bitcast.19, f32[]{:T(128)} %bitcast.18, f32[1,96,128]{2,1,0:T(8,128)S(1)} %get-tuple-element.11, f32[]{:T(128)} %bitcast.11, f32[]{:T(128)} %bitcast.10, ...), kind=kLoop, calls=%fused_computation.98 | loop fusion | flops 73728 | bytes 245776
  103.5 1.3 constant_dynamic-update-slice_fusion.5
  104.8 2.6 %constant_dynamic-update-slice_fusion.4 = (f32[12,96,128]{2,1,0:T(8,128)S(1)}, f32[1,96,128]{2,1,0:T(8,128)S(1)}) fusion(f32[12,96,128]{2,1,0:T(8,128)S(1)} %constant_dynamic-update-slice_fusion.5, f32[]{:T(128)} %bitcast.21, f32[]{:T(128)} %bitcast.20, f32[1,96,128]{2,1,0:T(8,128)S(1)} %get-tuple-element.9, f32[]{:T(128)} %bitcast.9, f32[]{:T(128)} %bitcast.8, ...), kind=kLoop, calls=%fused_computation.96 | loop fusion | flops 73728 | bytes 245776
  108.5 2.4 %constant_dynamic-update-slice_fusion.2 = (f32[12,96,128]{2,1,0:T(8,128)S(1)}, f32[1,96,128]{2,1,0:T(8,128)S(1)}) fusion(f32[12,96,128]{2,1,0:T(8,128)S(1)} %constant_dynamic-update-slice_fusion.3, f32[]{:T(128)} %bitcast.23, f32[]{:T(128)} %bitcast.22, f32[1,96,128]{2,1,0:T(8,128)S(1)} %get-tuple-element.7, f32[]{:T(128)} %bitcast.7, f32[]{:T(128)} %bitcast.6, ...), kind=kLoop, calls=%fused_computation.94 | loop fusion | flops 73728 | bytes 245776
  110.9 1.2 constant_dynamic-update-slice_fusion.1
  112.1 2.5 %constant_dynamic-update-slice_fusion = (f32[12,96,128]{2,1,0:T(8,128)S(1)}, f32[1,96,128]{2,1,0:T(8,128)S(1)}) fusion(f32[12,96,128]{2,1,0:T(8,128)S(1)} %constant_dynamic-update-slice_fusion.1, f32[]{:T(128)} %bitcast.25, f32[]{:T(128)} %bitcast.24, f32[1,96,128]{2,1,0:T(8,128)S(1)} %get-tuple-element.5, f32[]{:T(128)} %bitcast.5, f32[]{:T(128)} %bitcast.4, ...), kind=kLoop, calls=%fused_computation.92 | loop fusion | flops 73728 | bytes 245776
  114.7 1.3 fusion.38.rows_ref
  116.8 68.9 %shard_map.61 = f32[12,96,128]{2,1,0:T(8,128)} custom-call(f32[104,128]{1,0:T(8,128)} %concatenate.71.element_ref, f32[12,96,128]{2,1,0:T(8,128)} %copy-done.1, f32[48,128]{1,0:T(8,128)} %shard_map.60.coef_ref), custom_call_target="tpu_custom_call" | custom-call | tf_op jit(solution)/shard_map/pallas_call | solution.py:441
  185.7 1.9 %copy.90 = f32[12,3,32,128]{3,2,0,1:T(8,128)} copy(f32[12,3,32,128]{3,2,1,0:T(8,128)} %bitcast.129) | data formatting | bytes 1179648 | tf_op jit(solution)/shard_map/reshape | solution.py:484
  (37 shorter events, 14.8 us)
Async XLA Ops:
  2.2 7.9 %copy-start = (f32[3,12,32,128]{3,2,1,0:T(8,128)S(1)}, f32[3,12,32,128]{3,2,1,0:T(8,128)}, u32[]{:S(2)}) copy-start(f32[3,12,32,128]{3,2,1,0:T(8,128)} %param.4) | copy-start | bytes 1769476
  2.6 69.4 %collective-permute-start = (f32[3,12,32,4]{2,1,3,0:T(8,128)S(1)}, f32[3,12,32,4]{2,1,3,0:T(8,128)S(1)}, u32[]{:S(2)}, u32[]{:S(2)}) collective-permute-start(f32[3,12,32,4]{2,1,3,0:T(8,128)S(1)} %copy.49), channel_id=1, source_target_pairs={{128,0},{256,128},{384,256},{0,384},{129,1},{257,129},{385,257},{1... | collective-permute-start | bytes 55304 | tf_op jit(solution)/shard_map/ppermute | solution.py:29
  8.2 64.1 %collective-permute-start.1 = (f32[3,12,32,4]{2,1,3,0:T(8,128)S(1)}, f32[3,12,32,4]{2,1,3,0:T(8,128)}, u32[]{:S(2)}, u32[]{:S(2)}) collective-permute-start(f32[3,12,32,4]{2,1,3,0:T(8,128)S(1)} %copy.50), channel_id=1, source_target_pairs={{0,128},{128,256},{256,384},{384,0},{1,129},{129,257},{257,385},{3... | collective-permute-start | bytes 55304 | tf_op jit(solution)/shard_map/ppermute | solution.py:28
  10.8 62.7 %collective-permute-start.2 = (f32[3,1,32,128]{3,2,1,0:T(8,128)}, f32[3,1,32,128]{3,2,1,0:T(8,128)}, u32[]{:S(2)}, u32[]{:S(2)}) collective-permute-start(f32[3,1,32,128]{3,2,1,0:T(8,128)} %get-tuple-element.35), channel_id=1, source_target_pairs={{1,0},{2,1},{3,2},{4,3},{5,4},{6,5},{7,6},{8,7},{9,8},{10,9},{11,1... | collective-permute-start | bytes 147464 | tf_op jit(solution)/shard_map/ppermute | solution.py:29
  18.3 55.2 %collective-permute-start.3 = (f32[3,1,32,128]{3,2,1,0:T(8,128)}, f32[3,1,32,128]{3,2,1,0:T(8,128)}, u32[]{:S(2)}, u32[]{:S(2)}) collective-permute-start(f32[3,1,32,128]{3,2,1,0:T(8,128)} %get-tuple-element.36), channel_id=1, source_target_pairs={{0,1},{1,2},{2,3},{3,4},{4,5},{5,6},{6,7},{7,8},{8,9},{9,10},{10,1... | collective-permute-start | bytes 147464 | tf_op jit(solution)/shard_map/ppermute | solution.py:28
  24.3 2.7 %copy-start.2 = (f32[12]{0:T(128)S(1)}, f32[12]{0:T(128)}, u32[]{:S(2)}) copy-start(f32[12]{0:T(128)} %param.7) | copy-start | bytes 148
  24.3 2.7 %copy-start.3 = (f32[12]{0:T(128)S(1)}, f32[12]{0:T(128)}, u32[]{:S(2)}) copy-start(f32[12]{0:T(128)} %param.6) | copy-start | bytes 148
  116.0 0.8 copy-start.1

commit v9 on v8

--- a/solution.py
+++ b/solution.py
@@ -293,7 +293,7 @@
         in_specs=[pl.BlockSpec(memory_space=pltpu.VMEM)],
         out_specs=pl.BlockSpec(memory_space=pltpu.VMEM),
     )(table)
-    return pl.pallas_call(
+    return table, pl.pallas_call(
         functools.partial(prefix_kernel, count, rows_here),
         out_shape=jax.ShapeDtypeStruct((48, 128), jnp.float32),
         in_specs=[pl.BlockSpec(memory_space=pltpu.VMEM)] * 2,
@@ -380,8 +380,8 @@
     return parts[len(plan) - 1]
 
 
-def carry_kernel(count, rows_here, element_ref, rows_ref, coef_ref, out_ref, parts_down, up_element, parts_up,
-                 recv, send_sem, recv_sem):
+def carry_kernel(count, rows_here, rows_ref, given_ref, coef_ref, out_ref, down_element, parts_down, up_element,
+                 parts_up, recv, send_sem, recv_sem):
     me = lax.axis_index("gy")
     row = lax.axis_index("gx")
     plan = radix_plan(count)
@@ -398,16 +398,26 @@
     copies = []
     slots = sum(len(offsets) for offsets in plan)
 
+    coef = coef_ref[...]
+    given = given_ref[...]
+    carried = None
+    for i in range(rows_here):
+        lower = given[i : i + 1]
+        pivot = coef[i : i + 1]
+        carried = rows_ref[i] / pivot if carried is None else (rows_ref[i] - lower * carried) / pivot
+        out_ref[i] = carried
+    down_element[...] = jnp.concatenate(
+        [carried, jnp.broadcast_to(coef[32 + rows_here - 1 : 32 + rows_here], (8, 128))], axis=0
+    )
     below_carry = radix_scan(
-        me, row, count, False, element_ref, parts_down, recv, send_sem, recv_sem, 0, copies
+        me, row, count, False, down_element, parts_down, recv, send_sem, recv_sem, 0, copies
     )[:LINES]
-    coef = coef_ref[...]
     carried = None
     weight = None
     for i in reversed(range(rows_here)):
         sensitivity = coef[32 + i : 33 + i]
         modified = coef[16 + i : 17 + i]
-        reduced = rows_ref[i] + sensitivity * below_carry
+        reduced = out_ref[i] + sensitivity * below_carry
         if carried is None:
             carried = reduced
             weight = -modified
@@ -428,13 +438,9 @@
         copy.wait_send()
 
 
-def carry_solve(element_factor, element_lines, rows, coef):
+def carry_solve(stacked, given, coef):
     count = lax.axis_size("gy")
-    rows_here = len(rows)
-    packed = jnp.concatenate(
-        [element_lines.reshape(LINES, 128), jnp.broadcast_to(element_factor.reshape(1, 1), (8, 128))], axis=0
-    )
-    stacked = jnp.stack([value.reshape(LINES, 128) for value in rows], axis=0)
+    rows_here = stacked.shape[0]
     plan = radix_plan(count)
     slots = 2 * sum(len(offsets) for offsets in plan)
     big = (LINES + 8, 128)
@@ -444,6 +450,7 @@
         in_specs=[pl.BlockSpec(memory_space=pltpu.VMEM)] * 3,
         out_specs=pl.BlockSpec(memory_space=pltpu.VMEM),
         scratch_shapes=[
+            pltpu.VMEM(big, jnp.float32),
             pltpu.VMEM((len(plan),) + big, jnp.float32),
             pltpu.VMEM(big, jnp.float32),
             pltpu.VMEM((len(plan),) + big, jnp.float32),
@@ -452,7 +459,7 @@
             pltpu.SemaphoreType.DMA((slots,)),
         ],
         compiler_params=pltpu.CompilerParams(collective_id=0, has_side_effects=True),
-    )(packed, stacked, coef)
+    )(stacked, given, coef)
 
 
 def shards(velocity, old_advection, lower_gap, upper_gap):
@@ -472,15 +479,9 @@
     diagonal = 1.0 - lower_coef - upper_coef
     rows_here = velocity.shape[1]
 
-    table = coefficient_table(lower_coef, upper_coef, diagonal)
-    line_rows = forcing.reshape(3, rows_here, -1)
-    carried = jnp.zeros_like(line_rows[:, 0])
-    reduced = []
-    for i in range(rows_here):
-        carried = (line_rows[:, i] - lower_coef[i] * carried) / table[i, 0]
-        reduced.append(carried)
-    weight = table[32 + rows_here - 1, 0]
-    solved = carry_solve(weight, carried, reduced, table)
+    given, table = coefficient_table(lower_coef, upper_coef, diagonal)
+    stacked = jnp.transpose(forcing, (1, 0, 2, 3)).reshape(rows_here, LINES, 128)
+    solved = carry_solve(stacked, given, table)
     finished = jnp.transpose(solved.reshape(rows_here, 3, 32, -1), (1, 0, 2, 3))
     return (finished.reshape(velocity.shape), advection)
 

time: 189 us -> 145 us (0.77)
  the two profiles are of different devices: /device:TPU:1 before, /device:TPU:48 now
where the time goes in v9:
time: 145 us
  Pallas kernels  113 us (78%)
  local copies, waits for them, and re-layouts  14.6 us (10%)
  starting transfers between devices  11.4 us (8%)
  other arithmetic  4.95 us (3%)
    pallas_call x1, Pallas kernels, carry_solve(): pl.pallas_call(functools.partial(carry_kernel, count, rows_here), out_sha...  71.4 us
    pallas_call x1, Pallas kernels, coefficient_table(): pl.pallas_call(functools.partial(prefix_kernel, count, rows_here), out_sh...  40.1 us
    ppermute x2, starting transfers between devices, extended(): after = lax.ppermute(first, axis, down)  5.79 us
    ppermute x2, starting transfers between devices, extended(): before = lax.ppermute(last, axis, up)  5.6 us
    slice x6, local copies, waits for them, and re-layouts, roll_slope(): jnp.roll(values, -offset, along_axis) - jnp.roll(values, offset, along_axis)  5.16 us
    transpose x1, other arithmetic, shards(): jnp.transpose(forcing, (1, 0, 2, 3)).reshape(rows_here, LINES, 128)  4.95 us
  transfers between devices with their start and end apart: 4, of which 0 were waited for; matrix products, arithmetic and copies ran while one was open for 7% of the time, Pallas kernels for 29%

profile of v9, /device:TPU:48, one launch (start us, length us, event | category | flops | bytes accessed | tf_op | source)
XLA Modules:
  0.0 144.6 jit_solution(3052245729397736153)
XLA Ops:
  0.6 1.5 %fusion.33 = (f32[3,12,32,4]{3,2,1,0:T(8,128)S(1)}, f32[3,12,32,4]{3,2,1,0:T(8,128)S(1)}) fusion(f32[3,12,32,128]{3,2,1,0:T(8,128)} %param.4), kind=kLoop, calls=%fused_computation.60 | loop fusion | bytes 73728 | tf_op jit(solution)/shard_map/slice | solution.py:27
  2.1 0.4 copy.15
  2.5 3.4 %collective-permute-start.1 = (f32[3,12,32,4]{2,1,3,0:T(8,128)S(1)}, f32[3,12,32,4]{2,1,3,0:T(8,128)S(1)}, u32[]{:S(2)}, u32[]{:S(2)}) collective-permute-start(f32[3,12,32,4]{2,1,3,0:T(8,128)S(1)} %copy.15), channel_id=1, source_target_pairs={{0,128},{128,256},{256,384},{384,0},{1,129},{129,257},{257,385},{3... | collective-permute-start | bytes 55304 | tf_op jit(solution)/shard_map/ppermute | solution.py:28
  5.9 0.4 copy.14
  6.3 3.7 %collective-permute-start = (f32[3,12,32,4]{2,1,3,0:T(8,128)S(1)}, f32[3,12,32,4]{2,1,3,0:T(8,128)}, u32[]{:S(2)}, u32[]{:S(2)}) collective-permute-start(f32[3,12,32,4]{2,1,3,0:T(8,128)S(1)} %copy.14), channel_id=1, source_target_pairs={{128,0},{256,128},{384,256},{0,384},{129,1},{257,129},{385,257},{1... | collective-permute-start | bytes 55304 | tf_op jit(solution)/shard_map/ppermute | solution.py:29
  9.9 0.6 fusion.34
  10.6 2.1 %collective-permute-start.2 = (f32[3,1,32,128]{3,2,1,0:T(8,128)}, f32[3,1,32,128]{3,2,1,0:T(8,128)}, u32[]{:S(2)}, u32[]{:S(2)}) collective-permute-start(f32[3,1,32,128]{3,2,1,0:T(8,128)} %get-tuple-element.13), channel_id=1, source_target_pairs={{1,0},{2,1},{3,2},{4,3},{5,4},{6,5},{7,6},{8,7},{9,8},{10,9},{11,1... | collective-permute-start | bytes 147464 | tf_op jit(solution)/shard_map/ppermute | solution.py:29
  12.7 2.2 %collective-permute-start.3 = (f32[3,1,32,128]{3,2,1,0:T(8,128)}, f32[3,1,32,128]{3,2,1,0:T(8,128)}, u32[]{:S(2)}, u32[]{:S(2)}) collective-permute-start(f32[3,1,32,128]{3,2,1,0:T(8,128)} %get-tuple-element.14), channel_id=1, source_target_pairs={{0,1},{1,2},{2,3},{3,4},{4,5},{5,6},{6,7},{7,8},{8,9},{9,10},{10,1... | collective-permute-start | bytes 147464 | tf_op jit(solution)/shard_map/ppermute | solution.py:28
  14.9 0.8 slice_bitcast_fusion.2
  15.9 0.9 fusion.37
  16.8 1.1 fusion.39
  17.9 1.1 fusion.41
  19.0 0.7 fusion.40
  19.7 0.7 fusion.42
  20.4 0.6 fusion.38
  21.0 0.6 fusion.36
  21.8 0.7 broadcast_in_dim.2.table_ref.given_ref
  22.5 1.4 shard_map.59.element_ref
  23.8 40.1 %shard_map.60.coef_ref = f32[48,128]{1,0:T(8,128)} custom-call(f32[8,128]{1,0:T(8,128)} %shard_map.59.element_ref, f32[48,128]{1,0:T(8,128)} %broadcast_in_dim.2.table_ref.given_ref), custom_call_target="tpu_custom_call" | custom-call | tf_op jit(solution)/shard_map/pallas_call | solution.py:296
  64.3 1.2 copy.9
  65.5 4.9 %add_bitcast_fusion = (f32[12,3,32,128]{3,2,0,1:T(8,128)S(1)}, f32[3,12,32,128]{3,2,1,0:T(8,128)}) fusion(f32[3,12,32,128]{3,2,1,0:T(8,128)} %param.5, f32[3,12,32,128]{3,2,1,0:T(8,128)S(1)} %copy-done, f32[3,12,28,128]{3,2,1,0:T(8,128)} %get-tuple-element.28, f32[3,12,4,128]{3,2,1,0:T(4,128)} %get-tuple-element.30, f32[3,12,4,128]{3,2,1,0:T(4,128)} %get-tuple-element.29, ...), kind=kLoop, calls=%fused_computation.53 | loop fusion | flops 7667712 | bytes 7802928 | tf_op jit(solution)/shard_map/transpose | solution.py:483
  70.4 0.9 copy.12
  71.3 71.4 %shard_map.61 = f32[12,96,128]{2,1,0:T(8,128)} custom-call(f32[12,96,128]{2,1,0:T(8,128)} %bitcast.13, f32[48,128]{1,0:T(8,128)} %broadcast_in_dim.2.table_ref.given_ref, f32[48,128]{1,0:T(8,128)} %shard_map.60.coef_ref), custom_call_target="tpu_custom_call" | custom-call | tf_op jit(solution)/shard_map/pallas_call | solution.py:447
  142.7 1.9 %copy.17 = f32[12,3,32,128]{3,2,0,1:T(8,128)} copy(f32[12,3,32,128]{3,2,1,0:T(8,128)} %bitcast.14) | data formatting | bytes 1179648 | tf_op jit(solution)/shard_map/reshape | solution.py:485
  (15 shorter events, 0.5 us)
Async XLA Ops:
  2.1 7.8 %copy-start = (f32[3,12,32,128]{3,2,1,0:T(8,128)S(1)}, f32[3,12,32,128]{3,2,1,0:T(8,128)}, u32[]{:S(2)}) copy-start(f32[3,12,32,128]{3,2,1,0:T(8,128)} %param.4) | copy-start | bytes 1769476
  2.5 61.5 %collective-permute-start.1 = (f32[3,12,32,4]{2,1,3,0:T(8,128)S(1)}, f32[3,12,32,4]{2,1,3,0:T(8,128)S(1)}, u32[]{:S(2)}, u32[]{:S(2)}) collective-permute-start(f32[3,12,32,4]{2,1,3,0:T(8,128)S(1)} %copy.15), channel_id=1, source_target_pairs={{0,128},{128,256},{256,384},{384,0},{1,129},{129,257},{257,385},{3... | collective-permute-start | bytes 55304 | tf_op jit(solution)/shard_map/ppermute | solution.py:28
  6.3 58.0 %collective-permute-start = (f32[3,12,32,4]{2,1,3,0:T(8,128)S(1)}, f32[3,12,32,4]{2,1,3,0:T(8,128)}, u32[]{:S(2)}, u32[]{:S(2)}) collective-permute-start(f32[3,12,32,4]{2,1,3,0:T(8,128)S(1)} %copy.14), channel_id=1, source_target_pairs={{128,0},{256,128},{384,256},{0,384},{129,1},{257,129},{385,257},{1... | collective-permute-start | bytes 55304 | tf_op jit(solution)/shard_map/ppermute | solution.py:29
  10.6 54.9 %collective-permute-start.2 = (f32[3,1,32,128]{3,2,1,0:T(8,128)}, f32[3,1,32,128]{3,2,1,0:T(8,128)}, u32[]{:S(2)}, u32[]{:S(2)}) collective-permute-start(f32[3,1,32,128]{3,2,1,0:T(8,128)} %get-tuple-element.13), channel_id=1, source_target_pairs={{1,0},{2,1},{3,2},{4,3},{5,4},{6,5},{7,6},{8,7},{9,8},{10,9},{11,1... | collective-permute-start | bytes 147464 | tf_op jit(solution)/shard_map/ppermute | solution.py:29
  12.7 52.8 %collective-permute-start.3 = (f32[3,1,32,128]{3,2,1,0:T(8,128)}, f32[3,1,32,128]{3,2,1,0:T(8,128)}, u32[]{:S(2)}, u32[]{:S(2)}) collective-permute-start(f32[3,1,32,128]{3,2,1,0:T(8,128)} %get-tuple-element.14), channel_id=1, source_target_pairs={{0,1},{1,2},{2,3},{3,4},{4,5},{5,6},{6,7},{7,8},{8,9},{9,10},{10,1... | collective-permute-start | bytes 147464 | tf_op jit(solution)/shard_map/ppermute | solution.py:28
  19.0 2.7 %copy-start.1 = (f32[12]{0:T(128)S(1)}, f32[12]{0:T(128)}, u32[]{:S(2)}) copy-start(f32[12]{0:T(128)} %param.7) | copy-start | bytes 148
  19.0 2.7 %copy-start.2 = (f32[12]{0:T(128)S(1)}, f32[12]{0:T(128)}, u32[]{:S(2)}) copy-start(f32[12]{0:T(128)} %param.6) | copy-start | bytes 148

commit v10 on v9

--- a/solution.py
+++ b/solution.py
@@ -463,6 +463,12 @@
 
 
 def shards(velocity, old_advection, lower_gap, upper_gap):
+    gap_sum = lower_gap + upper_gap
+    lower_coef = -2.0 * STIFF / (gap_sum * lower_gap)
+    upper_coef = -2.0 * STIFF / (gap_sum * upper_gap)
+    diagonal = 1.0 - lower_coef - upper_coef
+    given, table = coefficient_table(lower_coef, upper_coef, diagonal)
+    given, table, velocity, old_advection = lax.optimization_barrier((given, table, velocity, old_advection))
     planes = velocity.shape[3]
     padded = extended(velocity, (("gx", 3),), 4, True)
     stream = stream_slope(padded, planes)
@@ -474,12 +480,8 @@
         velocity[0][None] * stream + velocity[1][None] * normal_slope + velocity[2][None] * spanwise
     )
     forcing = velocity + GAMMA * advection + ZETA * old_advection
-    lower_coef = -2.0 * STIFF / (gap_sum * lower_gap)
-    upper_coef = -2.0 * STIFF / (gap_sum * upper_gap)
-    diagonal = 1.0 - lower_coef - upper_coef
     rows_here = velocity.shape[1]
 
-    given, table = coefficient_table(lower_coef, upper_coef, diagonal)
     stacked = jnp.transpose(forcing, (1, 0, 2, 3)).reshape(rows_here, LINES, 128)
     solved = carry_solve(stacked, given, table)
     finished = jnp.transpose(solved.reshape(rows_here, 3, 32, -1), (1, 0, 2, 3))

time: 145 us -> 152 us (1.048)
  the two profiles are of different devices: /device:TPU:48 before, /device:TPU:80 now
where the time goes in v10:
time: 152 us; the launch traced here: 151 us
  Pallas kernels  116 us (76%)
  local copies, waits for them, and re-layouts  16.6 us (11%)
  starting transfers between devices  12.1 us (8%)
  other arithmetic  5.63 us (4%)
    pallas_call x1, Pallas kernels, carry_solve(): pl.pallas_call(functools.partial(carry_kernel, count, rows_here), out_sha...  69.8 us
    pallas_call x1, Pallas kernels, coefficient_table(): pl.pallas_call(functools.partial(prefix_kernel, count, rows_here), out_sh...  44.8 us
    ppermute x2, starting transfers between devices, extended(): after = lax.ppermute(first, axis, down)  6.81 us
    ppermute x2, starting transfers between devices, extended(): before = lax.ppermute(last, axis, up)  5.32 us
    slice x6, local copies, waits for them, and re-layouts, roll_slope(): jnp.roll(values, -offset, along_axis) - jnp.roll(values, offset, along_axis)  5.16 us
    transpose x1, other arithmetic, shards(): jnp.transpose(forcing, (1, 0, 2, 3)).reshape(rows_here, LINES, 128)  4.95 us
    optimization_barrier x1, local copies, waits for them, and re-layouts, shards(): lax.optimization_barrier((given, table, velocity, old_advection))  3.22 us
  transfers between devices with their start and end apart: 4, of which 0 were waited for; matrix products, arithmetic and copies ran while one was open for 6% of the time, Pallas kernels for 0%

profile of v10, /device:TPU:80, one launch (start us, length us, event | category | flops | bytes accessed | tf_op | source)
XLA Modules:
  0.0 151.1 jit_solution(14029594644353095166)
XLA Ops:
  0.6 0.7 subtract_subtract_fusion
  1.4 0.7 broadcast_in_dim.2.table_ref.given_ref
  2.1 1.4 shard_map.59.element_ref
  3.5 44.8 %shard_map.60.coef_ref = f32[48,128]{1,0:T(8,128)} custom-call(f32[8,128]{1,0:T(8,128)} %shard_map.59.element_ref, f32[48,128]{1,0:T(8,128)} %broadcast_in_dim.2.table_ref.given_ref), custom_call_target="tpu_custom_call" | custom-call | tf_op jit(solution)/shard_map/pallas_call | solution.py:296
  48.2 3.2 %copy.8 = f32[3,12,32,128]{2,1,3,0:T(8,128)} copy(f32[3,12,32,128]{3,2,1,0:T(8,128)} %param.4) | data formatting | bytes 1179648 | tf_op jit(solution)/shard_map/optimization_barrier | solution.py:471
  51.5 1.0 fusion.33
  52.4 3.4 %collective-permute-start.1 = (f32[3,12,32,4]{2,1,3,0:T(8,128)S(1)}, f32[3,12,32,4]{2,1,3,0:T(8,128)S(1)}, u32[]{:S(2)}, u32[]{:S(2)}) collective-permute-start(f32[3,12,32,4]{2,1,3,0:T(8,128)S(1)} %get-tuple-element.17), channel_id=1, source_target_pairs={{0,128},{128,256},{256,384},{384,0},{1,129},{129,257},{257,385},{3... | collective-permute-start | bytes 55304 | tf_op jit(solution)/shard_map/ppermute | solution.py:28
  55.8 3.7 %collective-permute-start = (f32[3,12,32,4]{2,1,3,0:T(8,128)S(1)}, f32[3,12,32,4]{2,1,3,0:T(8,128)}, u32[]{:S(2)}, u32[]{:S(2)}) collective-permute-start(f32[3,12,32,4]{2,1,3,0:T(8,128)S(1)} %get-tuple-element.16), channel_id=1, source_target_pairs={{128,0},{256,128},{384,256},{0,384},{129,1},{257,129},{385,257},{1... | collective-permute-start | bytes 55304 | tf_op jit(solution)/shard_map/ppermute | solution.py:29
  59.5 0.6 fusion.34
  60.1 3.2 %collective-permute-start.2 = (f32[3,1,32,128]{3,2,1,0:T(8,128)}, f32[3,1,32,128]{3,2,1,0:T(8,128)}, u32[]{:S(2)}, u32[]{:S(2)}) collective-permute-start(f32[3,1,32,128]{3,2,1,0:T(8,128)} %get-tuple-element.21), channel_id=1, source_target_pairs={{1,0},{2,1},{3,2},{4,3},{5,4},{6,5},{7,6},{8,7},{9,8},{10,9},{11,1... | collective-permute-start | bytes 147464 | tf_op jit(solution)/shard_map/ppermute | solution.py:29
  63.3 1.9 %collective-permute-start.3 = (f32[3,1,32,128]{3,2,1,0:T(8,128)}, f32[3,1,32,128]{3,2,1,0:T(8,128)}, u32[]{:S(2)}, u32[]{:S(2)}) collective-permute-start(f32[3,1,32,128]{3,2,1,0:T(8,128)} %get-tuple-element.22), channel_id=1, source_target_pairs={{0,1},{1,2},{2,3},{3,4},{4,5},{5,6},{6,7},{7,8},{8,9},{9,10},{10,1... | collective-permute-start | bytes 147464 | tf_op jit(solution)/shard_map/ppermute | solution.py:28
  65.2 0.8 slice_bitcast_fusion.2
  66.2 0.9 fusion.37
  67.1 1.1 fusion.39
  68.2 1.1 fusion.41
  69.3 0.7 fusion.40
  70.0 0.7 fusion.42
  70.7 0.7 fusion.38
  71.3 0.6 fusion.36
  72.3 1.2 copy.9
  73.5 4.9 %add_bitcast_fusion = (f32[12,3,32,128]{3,2,0,1:T(8,128)S(1)}, f32[3,12,32,128]{3,2,1,0:T(8,128)}) fusion(f32[3,12,32,128]{3,2,1,0:T(8,128)} %param.5, f32[3,12,32,128]{3,2,1,0:T(8,128)S(1)} %copy-done, f32[3,12,28,128]{3,2,1,0:T(8,128)} %get-tuple-element.36, f32[3,12,4,128]{3,2,1,0:T(4,128)} %get-tuple-element.38, f32[3,12,4,128]{3,2,1,0:T(4,128)} %get-tuple-element.37, ...), kind=kLoop, calls=%fused_computation.53 | loop fusion | flops 7667712 | bytes 7802928 | tf_op jit(solution)/shard_map/transpose | solution.py:485
  78.4 0.9 copy.12
  79.3 69.8 %shard_map.61 = f32[12,96,128]{2,1,0:T(8,128)} custom-call(f32[12,96,128]{2,1,0:T(8,128)} %bitcast.13, f32[48,128]{1,0:T(8,128)} %broadcast_in_dim.2.table_ref.given_ref, f32[48,128]{1,0:T(8,128)} %shard_map.60.coef_ref), custom_call_target="tpu_custom_call" | custom-call | tf_op jit(solution)/shard_map/pallas_call | solution.py:447
  149.1 1.9 %copy.15 = f32[12,3,32,128]{3,2,0,1:T(8,128)} copy(f32[12,3,32,128]{3,2,1,0:T(8,128)} %bitcast.14) | data formatting | bytes 1179648 | tf_op jit(solution)/shard_map/reshape | solution.py:487
  (10 shorter events, 0.5 us)
Async XLA Ops:
  48.2 11.3 %copy-start = (f32[3,12,32,128]{3,2,1,0:T(8,128)S(1)}, f32[3,12,32,128]{3,2,1,0:T(8,128)}, u32[]{:S(2)}) copy-start(f32[3,12,32,128]{3,2,1,0:T(8,128)} %param.4) | copy-start | bytes 1769476
  52.4 19.6 %collective-permute-start.1 = (f32[3,12,32,4]{2,1,3,0:T(8,128)S(1)}, f32[3,12,32,4]{2,1,3,0:T(8,128)S(1)}, u32[]{:S(2)}, u32[]{:S(2)}) collective-permute-start(f32[3,12,32,4]{2,1,3,0:T(8,128)S(1)} %get-tuple-element.17), channel_id=1, source_target_pairs={{0,128},{128,256},{256,384},{384,0},{1,129},{129,257},{257,385},{3... | collective-permute-start | bytes 55304 | tf_op jit(solution)/shard_map/ppermute | solution.py:28
  55.8 16.5 %collective-permute-start = (f32[3,12,32,4]{2,1,3,0:T(8,128)S(1)}, f32[3,12,32,4]{2,1,3,0:T(8,128)}, u32[]{:S(2)}, u32[]{:S(2)}) collective-permute-start(f32[3,12,32,4]{2,1,3,0:T(8,128)S(1)} %get-tuple-element.16), channel_id=1, source_target_pairs={{128,0},{256,128},{384,256},{0,384},{129,1},{257,129},{385,257},{1... | collective-permute-start | bytes 55304 | tf_op jit(solution)/shard_map/ppermute | solution.py:29
  60.1 13.3 %collective-permute-start.2 = (f32[3,1,32,128]{3,2,1,0:T(8,128)}, f32[3,1,32,128]{3,2,1,0:T(8,128)}, u32[]{:S(2)}, u32[]{:S(2)}) collective-permute-start(f32[3,1,32,128]{3,2,1,0:T(8,128)} %get-tuple-element.21), channel_id=1, source_target_pairs={{1,0},{2,1},{3,2},{4,3},{5,4},{6,5},{7,6},{8,7},{9,8},{10,9},{11,1... | collective-permute-start | bytes 147464 | tf_op jit(solution)/shard_map/ppermute | solution.py:29
  63.3 10.2 %collective-permute-start.3 = (f32[3,1,32,128]{3,2,1,0:T(8,128)}, f32[3,1,32,128]{3,2,1,0:T(8,128)}, u32[]{:S(2)}, u32[]{:S(2)}) collective-permute-start(f32[3,1,32,128]{3,2,1,0:T(8,128)} %get-tuple-element.22), channel_id=1, source_target_pairs={{0,1},{1,2},{2,3},{3,4},{4,5},{5,6},{6,7},{7,8},{8,9},{9,10},{10,1... | collective-permute-start | bytes 147464 | tf_op jit(solution)/shard_map/ppermute | solution.py:28

commit v11 on v9

--- a/solution.py
+++ b/solution.py
@@ -179,54 +179,52 @@
     return result[:4, 0].reshape(2, 2)
 
 
-def prefix_kernel(count, rows_here, element_ref, table_ref, out_ref, pieces, send_sem, recv_sem):
+def prefix_kernel(count, group, rows_here, element_ref, table_ref, out_ref, pieces, send_sem, recv_sem, local_sem):
     mine = lax.axis_index("gy")
     row = lax.axis_index("gx")
+    teams = count // group
+    team = mine // group
+    seat = mine % group
     barrier = pltpu.get_barrier_semaphore()
-
-    def greet(step, carry):
-        pl.semaphore_signal(barrier, inc=1, device_id=(row, (mine + step) % count), device_id_type=MESH)
-        return carry
-
-    lax.fori_loop(1, count, greet, 0)
-    pl.semaphore_wait(barrier, count - 1)
-
-    def outgoing(step):
+    partners = [team * group + (seat + step) % group for step in range(1, group)]
+    partners += [((team + step) % teams) * group + seat for step in range(1, teams)]
+    for partner in partners:
+        pl.semaphore_signal(barrier, inc=1, device_id=(row, partner), device_id_type=MESH)
+    pl.semaphore_wait(barrier, len(partners))
+
+    own = pltpu.make_async_copy(element_ref, pieces.at[mine], local_sem.at[0])
+    own.start()
+
+    def mate_copy(step, source_seat, target_seat):
         return pltpu.make_async_remote_copy(
             src_ref=element_ref,
-            dst_ref=pieces.at[mine],
+            dst_ref=pieces.at[team * group + source_seat],
             send_sem=send_sem.at[step],
-            recv_sem=recv_sem.at[mine],
-            device_id=(row, (mine + step) % count),
+            recv_sem=recv_sem.at[source_seat],
+            device_id=(row, team * group + target_seat),
             device_id_type=MESH,
         )
 
-    def incoming(step):
-        source = (mine + count - step) % count
+    def team_copy(step, source_team, target_team):
+        block = pieces.at[pl.ds(source_team * group, group)]
         return pltpu.make_async_remote_copy(
-            src_ref=element_ref,
-            dst_ref=pieces.at[source],
-            send_sem=send_sem.at[step],
-            recv_sem=recv_sem.at[source],
-            device_id=(row, source),
+            src_ref=block,
+            dst_ref=block,
+            send_sem=send_sem.at[group + step],
+            recv_sem=recv_sem.at[group + source_team],
+            device_id=(row, target_team * group + seat),
             device_id_type=MESH,
         )
 
-    def send(step, carry):
-        outgoing(step).start()
-        return carry
-
-    def arrive(step, carry):
-        incoming(step).wait_recv()
-        return carry
-
-    def drain(step, carry):
-        outgoing(step).wait_send()
-        return carry
-
-    lax.fori_loop(1, count, send, 0)
-    lax.fori_loop(1, count, arrive, 0)
-    pieces[mine] = element_ref[...]
+    for step in range(1, group):
+        mate_copy(step, seat, (seat + step) % group).start()
+    for step in range(1, group):
+        mate_copy(step, (seat + group - step) % group, seat).wait_recv()
+    own.wait()
+    for step in range(1, teams):
+        team_copy(step, team, (team + step) % teams).start()
+    for step in range(1, teams):
+        team_copy(step, (team + teams - step) % teams, team).wait_recv()
 
     def turn(position, total):
         piece = pieces[position]
@@ -257,7 +255,16 @@
         out_ref[i : i + 1] = pivot
         out_ref[16 + i : 17 + i] = modified_prev
         out_ref[32 + i : 33 + i] = weight
-    lax.fori_loop(1, count, drain, 0)
+    for step in range(1, group):
+        mate_copy(step, seat, (seat + step) % group).wait_send()
+    for step in range(1, teams):
+        team_copy(step, team, (team + step) % teams).wait_send()
+
+
+def team_size(count):
+    if count > 16 and count % 16 == 0:
+        return 16
+    return max(1, count // 2)
 
 
 def matrix_kernel(rows_here, table_ref, out_ref):
@@ -294,14 +301,15 @@
         out_specs=pl.BlockSpec(memory_space=pltpu.VMEM),
     )(table)
     return table, pl.pallas_call(
-        functools.partial(prefix_kernel, count, rows_here),
+        functools.partial(prefix_kernel, count, team_size(count), rows_here),
         out_shape=jax.ShapeDtypeStruct((48, 128), jnp.float32),
         in_specs=[pl.BlockSpec(memory_space=pltpu.VMEM)] * 2,
         out_specs=pl.BlockSpec(memory_space=pltpu.VMEM),
         scratch_shapes=[
             pltpu.VMEM((count, 8, 128), jnp.float32),
-            pltpu.SemaphoreType.DMA((count,)),
-            pltpu.SemaphoreType.DMA((count,)),
+            pltpu.SemaphoreType.DMA((team_size(count) + count // team_size(count),)),
+            pltpu.SemaphoreType.DMA((team_size(count) + count // team_size(count),)),
+            pltpu.SemaphoreType.DMA((1,)),
         ],
         compiler_params=pltpu.CompilerParams(collective_id=1, has_side_effects=True),
     )(element, table)

time: 145 us -> 135 us (0.931)
  the two profiles are of different devices: /device:TPU:48 before, /device:TPU:6 now
where the time goes in v11:
time: 135 us; the launch traced here: 134 us
  Pallas kernels  98.8 us (73%)
  local copies, waits for them, and re-layouts  14.6 us (11%)
  starting transfers between devices  14.6 us (11%)
  other arithmetic  4.95 us (4%)
    pallas_call x1, Pallas kernels, carry_solve(): pl.pallas_call(functools.partial(carry_kernel, count, rows_here), out_sha...  65.9 us
    pallas_call x1, Pallas kernels, coefficient_table(): pl.pallas_call(functools.partial(prefix_kernel, count, team_size(count),...  31.5 us
    ppermute x2, starting transfers between devices, extended(): before = lax.ppermute(last, axis, up)  11.4 us
    slice x6, local copies, waits for them, and re-layouts, roll_slope(): jnp.roll(values, -offset, along_axis) - jnp.roll(values, offset, along_axis)  5.16 us
    transpose x1, other arithmetic, shards(): jnp.transpose(forcing, (1, 0, 2, 3)).reshape(rows_here, LINES, 128)  4.95 us
    ppermute x2, starting transfers between devices, extended(): after = lax.ppermute(first, axis, down)  3.21 us
  transfers between devices with their start and end apart: 4, of which 0 were waited for; matrix products, arithmetic and copies ran while one was open for 7% of the time, Pallas kernels for 25%

profile of v11, /device:TPU:6, one launch (start us, length us, event | category | flops | bytes accessed | tf_op | source)
XLA Modules:
  0.0 133.7 jit_solution(1055736918714465779)
XLA Ops:
  0.6 1.5 %fusion.33 = (f32[3,12,32,4]{3,2,1,0:T(8,128)S(1)}, f32[3,12,32,4]{3,2,1,0:T(8,128)S(1)}) fusion(f32[3,12,32,128]{3,2,1,0:T(8,128)} %param.4), kind=kLoop, calls=%fused_computation.60 | loop fusion | bytes 73728 | tf_op jit(solution)/shard_map/slice | solution.py:27
  2.1 0.4 copy.15
  2.5 7.8 %collective-permute-start.1 = (f32[3,12,32,4]{2,1,3,0:T(8,128)S(1)}, f32[3,12,32,4]{2,1,3,0:T(8,128)S(1)}, u32[]{:S(2)}, u32[]{:S(2)}) collective-permute-start(f32[3,12,32,4]{2,1,3,0:T(8,128)S(1)} %copy.15), channel_id=1, source_target_pairs={{0,128},{128,256},{256,384},{384,0},{1,129},{129,257},{257,385},{3... | collective-permute-start | bytes 55304 | tf_op jit(solution)/shard_map/ppermute | solution.py:28
  10.3 0.4 copy.14
  10.6 1.9 %collective-permute-start = (f32[3,12,32,4]{2,1,3,0:T(8,128)S(1)}, f32[3,12,32,4]{2,1,3,0:T(8,128)}, u32[]{:S(2)}, u32[]{:S(2)}) collective-permute-start(f32[3,12,32,4]{2,1,3,0:T(8,128)S(1)} %copy.14), channel_id=1, source_target_pairs={{128,0},{256,128},{384,256},{0,384},{129,1},{257,129},{385,257},{1... | collective-permute-start | bytes 55304 | tf_op jit(solution)/shard_map/ppermute | solution.py:29
  12.6 0.6 fusion.34
  13.2 1.3 collective-permute-start.2
  14.5 3.6 %collective-permute-start.3 = (f32[3,1,32,128]{3,2,1,0:T(8,128)}, f32[3,1,32,128]{3,2,1,0:T(8,128)}, u32[]{:S(2)}, u32[]{:S(2)}) collective-permute-start(f32[3,1,32,128]{3,2,1,0:T(8,128)} %get-tuple-element.14), channel_id=1, source_target_pairs={{0,1},{1,2},{2,3},{3,4},{4,5},{5,6},{6,7},{7,8},{8,9},{9,10},{10,1... | collective-permute-start | bytes 147464 | tf_op jit(solution)/shard_map/ppermute | solution.py:28
  18.1 0.8 slice_bitcast_fusion.2
  19.1 0.9 fusion.37
  20.0 1.1 fusion.39
  21.2 1.1 fusion.41
  22.3 0.7 fusion.40
  22.9 0.7 fusion.42
  23.6 0.6 fusion.38
  24.3 0.6 fusion.36
  25.0 0.7 broadcast_in_dim.2.table_ref.given_ref
  25.7 1.4 %shard_map.59.element_ref = f32[8,128]{1,0:T(8,128)} custom-call(f32[48,128]{1,0:T(8,128)} %broadcast_in_dim.2.table_ref.given_ref), custom_call_target="tpu_custom_call" | custom-call | tf_op jit(solution)/shard_map/pallas_call | solution.py:297
  27.1 31.5 %shard_map.60.coef_ref = f32[48,128]{1,0:T(8,128)} custom-call(f32[8,128]{1,0:T(8,128)} %shard_map.59.element_ref, f32[48,128]{1,0:T(8,128)} %broadcast_in_dim.2.table_ref.given_ref), custom_call_target="tpu_custom_call" | custom-call | tf_op jit(solution)/shard_map/pallas_call | solution.py:303
  58.9 1.2 copy.9
  60.1 4.9 %add_bitcast_fusion = (f32[12,3,32,128]{3,2,0,1:T(8,128)S(1)}, f32[3,12,32,128]{3,2,1,0:T(8,128)}) fusion(f32[3,12,32,128]{3,2,1,0:T(8,128)} %param.5, f32[3,12,32,128]{3,2,1,0:T(8,128)S(1)} %copy-done, f32[3,12,28,128]{3,2,1,0:T(8,128)} %get-tuple-element.28, f32[3,12,4,128]{3,2,1,0:T(4,128)} %get-tuple-element.30, f32[3,12,4,128]{3,2,1,0:T(4,128)} %get-tuple-element.29, ...), kind=kLoop, calls=%fused_computation.53 | loop fusion | flops 7667712 | bytes 7802928 | tf_op jit(solution)/shard_map/transpose | solution.py:491
  65.1 0.9 copy.12
  65.9 65.9 %shard_map.61 = f32[12,96,128]{2,1,0:T(8,128)} custom-call(f32[12,96,128]{2,1,0:T(8,128)} %bitcast.13, f32[48,128]{1,0:T(8,128)} %broadcast_in_dim.2.table_ref.given_ref, f32[48,128]{1,0:T(8,128)} %shard_map.60.coef_ref), custom_call_target="tpu_custom_call" | custom-call | tf_op jit(solution)/shard_map/pallas_call | solution.py:455
  131.8 1.9 %copy.17 = f32[12,3,32,128]{3,2,0,1:T(8,128)} copy(f32[12,3,32,128]{3,2,1,0:T(8,128)} %bitcast.14) | data formatting | bytes 1179648 | tf_op jit(solution)/shard_map/reshape | solution.py:493
  (15 shorter events, 0.5 us)
Async XLA Ops:
  2.1 10.5 %copy-start = (f32[3,12,32,128]{3,2,1,0:T(8,128)S(1)}, f32[3,12,32,128]{3,2,1,0:T(8,128)}, u32[]{:S(2)}) copy-start(f32[3,12,32,128]{3,2,1,0:T(8,128)} %param.4) | copy-start | bytes 1769476
  2.5 56.1 %collective-permute-start.1 = (f32[3,12,32,4]{2,1,3,0:T(8,128)S(1)}, f32[3,12,32,4]{2,1,3,0:T(8,128)S(1)}, u32[]{:S(2)}, u32[]{:S(2)}) collective-permute-start(f32[3,12,32,4]{2,1,3,0:T(8,128)S(1)} %copy.15), channel_id=1, source_target_pairs={{0,128},{128,256},{256,384},{384,0},{1,129},{129,257},{257,385},{3... | collective-permute-start | bytes 55304 | tf_op jit(solution)/shard_map/ppermute | solution.py:28
  10.6 48.3 %collective-permute-start = (f32[3,12,32,4]{2,1,3,0:T(8,128)S(1)}, f32[3,12,32,4]{2,1,3,0:T(8,128)}, u32[]{:S(2)}, u32[]{:S(2)}) collective-permute-start(f32[3,12,32,4]{2,1,3,0:T(8,128)S(1)} %copy.14), channel_id=1, source_target_pairs={{128,0},{256,128},{384,256},{0,384},{129,1},{257,129},{385,257},{1... | collective-permute-start | bytes 55304 | tf_op jit(solution)/shard_map/ppermute | solution.py:29
  13.2 46.9 %collective-permute-start.2 = (f32[3,1,32,128]{3,2,1,0:T(8,128)}, f32[3,1,32,128]{3,2,1,0:T(8,128)}, u32[]{:S(2)}, u32[]{:S(2)}) collective-permute-start(f32[3,1,32,128]{3,2,1,0:T(8,128)} %get-tuple-element.13), channel_id=1, source_target_pairs={{1,0},{2,1},{3,2},{4,3},{5,4},{6,5},{7,6},{8,7},{9,8},{10,9},{11,1... | collective-permute-start | bytes 147464 | tf_op jit(solution)/shard_map/ppermute | solution.py:29
  14.5 45.6 %collective-permute-start.3 = (f32[3,1,32,128]{3,2,1,0:T(8,128)}, f32[3,1,32,128]{3,2,1,0:T(8,128)}, u32[]{:S(2)}, u32[]{:S(2)}) collective-permute-start(f32[3,1,32,128]{3,2,1,0:T(8,128)} %get-tuple-element.14), channel_id=1, source_target_pairs={{0,1},{1,2},{2,3},{3,4},{4,5},{5,6},{6,7},{7,8},{8,9},{9,10},{10,1... | collective-permute-start | bytes 147464 | tf_op jit(solution)/shard_map/ppermute | solution.py:28
  22.3 2.7 %copy-start.1 = (f32[12]{0:T(128)S(1)}, f32[12]{0:T(128)}, u32[]{:S(2)}) copy-start(f32[12]{0:T(128)} %param.7) | copy-start | bytes 148
  22.3 2.7 %copy-start.2 = (f32[12]{0:T(128)S(1)}, f32[12]{0:T(128)}, u32[]{:S(2)}) copy-start(f32[12]{0:T(128)} %param.6) | copy-start | bytes 148

commit v12 on v11

--- a/solution.py
+++ b/solution.py
@@ -238,7 +238,8 @@
             jnp.maximum(jnp.abs(entries[2]), jnp.abs(entries[3])),
         )
         inside = position < mine
-        return tuple(jnp.where(inside, value / big, old) for value, old in zip(entries, total))
+        shrink = 1.0 / big
+        return tuple(jnp.where(inside, value * shrink, old) for value, old in zip(entries, total))
 
     unit = jnp.ones((1, 128), jnp.float32)
     blank = jnp.zeros((1, 128), jnp.float32)

time: 135 us -> 135 us (level)
  no operation moved by 1% of the time
where the time goes in v12:
time: 135 us; the launch traced here: 134 us
  Pallas kernels  98.8 us (73%)
  local copies, waits for them, and re-layouts  14.6 us (11%)
  starting transfers between devices  14.6 us (11%)
  other arithmetic  4.95 us (4%)
    pallas_call x1, Pallas kernels, carry_solve(): pl.pallas_call(functools.partial(carry_kernel, count, rows_here), out_sha...  65.9 us
    pallas_call x1, Pallas kernels, coefficient_table(): pl.pallas_call(functools.partial(prefix_kernel, count, team_size(count),...  31.5 us
    ppermute x2, starting transfers between devices, extended(): before = lax.ppermute(last, axis, up)  11.4 us
    slice x6, local copies, waits for them, and re-layouts, roll_slope(): jnp.roll(values, -offset, along_axis) - jnp.roll(values, offset, along_axis)  5.16 us
    transpose x1, other arithmetic, shards(): jnp.transpose(forcing, (1, 0, 2, 3)).reshape(rows_here, LINES, 128)  4.95 us
    ppermute x2, starting transfers between devices, extended(): after = lax.ppermute(first, axis, down)  3.21 us
  transfers between devices with their start and end apart: 4, of which 0 were waited for; matrix products, arithmetic and copies ran while one was open for 7% of the time, Pallas kernels for 25%

profile of v12, /device:TPU:6, one launch (start us, length us, event | category | flops | bytes accessed | tf_op | source)
XLA Modules:
  0.0 133.7 jit_solution(17303768662608256316)
XLA Ops:
  0.6 1.5 %fusion.33 = (f32[3,12,32,4]{3,2,1,0:T(8,128)S(1)}, f32[3,12,32,4]{3,2,1,0:T(8,128)S(1)}) fusion(f32[3,12,32,128]{3,2,1,0:T(8,128)} %param.4), kind=kLoop, calls=%fused_computation.60 | loop fusion | bytes 73728 | tf_op jit(solution)/shard_map/slice | solution.py:27
  2.1 0.4 copy.15
  2.5 7.8 %collective-permute-start.1 = (f32[3,12,32,4]{2,1,3,0:T(8,128)S(1)}, f32[3,12,32,4]{2,1,3,0:T(8,128)S(1)}, u32[]{:S(2)}, u32[]{:S(2)}) collective-permute-start(f32[3,12,32,4]{2,1,3,0:T(8,128)S(1)} %copy.15), channel_id=1, source_target_pairs={{0,128},{128,256},{256,384},{384,0},{1,129},{129,257},{257,385},{3... | collective-permute-start | bytes 55304 | tf_op jit(solution)/shard_map/ppermute | solution.py:28
  10.3 0.4 copy.14
  10.6 1.9 %collective-permute-start = (f32[3,12,32,4]{2,1,3,0:T(8,128)S(1)}, f32[3,12,32,4]{2,1,3,0:T(8,128)}, u32[]{:S(2)}, u32[]{:S(2)}) collective-permute-start(f32[3,12,32,4]{2,1,3,0:T(8,128)S(1)} %copy.14), channel_id=1, source_target_pairs={{128,0},{256,128},{384,256},{0,384},{129,1},{257,129},{385,257},{1... | collective-permute-start | bytes 55304 | tf_op jit(solution)/shard_map/ppermute | solution.py:29
  12.6 0.6 fusion.34
  13.2 1.3 collective-permute-start.2
  14.5 3.6 %collective-permute-start.3 = (f32[3,1,32,128]{3,2,1,0:T(8,128)}, f32[3,1,32,128]{3,2,1,0:T(8,128)}, u32[]{:S(2)}, u32[]{:S(2)}) collective-permute-start(f32[3,1,32,128]{3,2,1,0:T(8,128)} %get-tuple-element.14), channel_id=1, source_target_pairs={{0,1},{1,2},{2,3},{3,4},{4,5},{5,6},{6,7},{7,8},{8,9},{9,10},{10,1... | collective-permute-start | bytes 147464 | tf_op jit(solution)/shard_map/ppermute | solution.py:28
  18.1 0.8 slice_bitcast_fusion.2
  19.1 0.9 fusion.37
  20.0 1.1 fusion.39
  21.2 1.1 fusion.41
  22.3 0.7 fusion.40
  22.9 0.7 fusion.42
  23.6 0.6 fusion.38
  24.3 0.6 fusion.36
  25.0 0.7 broadcast_in_dim.2.table_ref.given_ref
  25.7 1.4 %shard_map.59.element_ref = f32[8,128]{1,0:T(8,128)} custom-call(f32[48,128]{1,0:T(8,128)} %broadcast_in_dim.2.table_ref.given_ref), custom_call_target="tpu_custom_call" | custom-call | tf_op jit(solution)/shard_map/pallas_call | solution.py:298
  27.1 31.5 %shard_map.60.coef_ref = f32[48,128]{1,0:T(8,128)} custom-call(f32[8,128]{1,0:T(8,128)} %shard_map.59.element_ref, f32[48,128]{1,0:T(8,128)} %broadcast_in_dim.2.table_ref.given_ref), custom_call_target="tpu_custom_call" | custom-call | tf_op jit(solution)/shard_map/pallas_call | solution.py:304
  58.9 1.2 copy.9
  60.1 4.9 %add_bitcast_fusion = (f32[12,3,32,128]{3,2,0,1:T(8,128)S(1)}, f32[3,12,32,128]{3,2,1,0:T(8,128)}) fusion(f32[3,12,32,128]{3,2,1,0:T(8,128)} %param.5, f32[3,12,32,128]{3,2,1,0:T(8,128)S(1)} %copy-done, f32[3,12,28,128]{3,2,1,0:T(8,128)} %get-tuple-element.28, f32[3,12,4,128]{3,2,1,0:T(4,128)} %get-tuple-element.30, f32[3,12,4,128]{3,2,1,0:T(4,128)} %get-tuple-element.29, ...), kind=kLoop, calls=%fused_computation.53 | loop fusion | flops 7667712 | bytes 7802928 | tf_op jit(solution)/shard_map/transpose | solution.py:492
  65.1 0.9 copy.12
  65.9 65.9 %shard_map.61 = f32[12,96,128]{2,1,0:T(8,128)} custom-call(f32[12,96,128]{2,1,0:T(8,128)} %bitcast.13, f32[48,128]{1,0:T(8,128)} %broadcast_in_dim.2.table_ref.given_ref, f32[48,128]{1,0:T(8,128)} %shard_map.60.coef_ref), custom_call_target="tpu_custom_call" | custom-call | tf_op jit(solution)/shard_map/pallas_call | solution.py:456
  131.8 1.9 %copy.17 = f32[12,3,32,128]{3,2,0,1:T(8,128)} copy(f32[12,3,32,128]{3,2,1,0:T(8,128)} %bitcast.14) | data formatting | bytes 1179648 | tf_op jit(solution)/shard_map/reshape | solution.py:494
  (15 shorter events, 0.5 us)
Async XLA Ops:
  2.1 10.5 %copy-start = (f32[3,12,32,128]{3,2,1,0:T(8,128)S(1)}, f32[3,12,32,128]{3,2,1,0:T(8,128)}, u32[]{:S(2)}) copy-start(f32[3,12,32,128]{3,2,1,0:T(8,128)} %param.4) | copy-start | bytes 1769476
  2.5 56.1 %collective-permute-start.1 = (f32[3,12,32,4]{2,1,3,0:T(8,128)S(1)}, f32[3,12,32,4]{2,1,3,0:T(8,128)S(1)}, u32[]{:S(2)}, u32[]{:S(2)}) collective-permute-start(f32[3,12,32,4]{2,1,3,0:T(8,128)S(1)} %copy.15), channel_id=1, source_target_pairs={{0,128},{128,256},{256,384},{384,0},{1,129},{129,257},{257,385},{3... | collective-permute-start | bytes 55304 | tf_op jit(solution)/shard_map/ppermute | solution.py:28
  10.6 48.3 %collective-permute-start = (f32[3,12,32,4]{2,1,3,0:T(8,128)S(1)}, f32[3,12,32,4]{2,1,3,0:T(8,128)}, u32[]{:S(2)}, u32[]{:S(2)}) collective-permute-start(f32[3,12,32,4]{2,1,3,0:T(8,128)S(1)} %copy.14), channel_id=1, source_target_pairs={{128,0},{256,128},{384,256},{0,384},{129,1},{257,129},{385,257},{1... | collective-permute-start | bytes 55304 | tf_op jit(solution)/shard_map/ppermute | solution.py:29
  13.2 46.9 %collective-permute-start.2 = (f32[3,1,32,128]{3,2,1,0:T(8,128)}, f32[3,1,32,128]{3,2,1,0:T(8,128)}, u32[]{:S(2)}, u32[]{:S(2)}) collective-permute-start(f32[3,1,32,128]{3,2,1,0:T(8,128)} %get-tuple-element.13), channel_id=1, source_target_pairs={{1,0},{2,1},{3,2},{4,3},{5,4},{6,5},{7,6},{8,7},{9,8},{10,9},{11,1... | collective-permute-start | bytes 147464 | tf_op jit(solution)/shard_map/ppermute | solution.py:29
  14.5 45.6 %collective-permute-start.3 = (f32[3,1,32,128]{3,2,1,0:T(8,128)}, f32[3,1,32,128]{3,2,1,0:T(8,128)}, u32[]{:S(2)}, u32[]{:S(2)}) collective-permute-start(f32[3,1,32,128]{3,2,1,0:T(8,128)} %get-tuple-element.14), channel_id=1, source_target_pairs={{0,1},{1,2},{2,3},{3,4},{4,5},{5,6},{6,7},{7,8},{8,9},{9,10},{10,1... | collective-permute-start | bytes 147464 | tf_op jit(solution)/shard_map/ppermute | solution.py:28
  22.3 2.7 %copy-start.1 = (f32[12]{0:T(128)S(1)}, f32[12]{0:T(128)}, u32[]{:S(2)}) copy-start(f32[12]{0:T(128)} %param.7) | copy-start | bytes 148
  22.3 2.7 %copy-start.2 = (f32[12]{0:T(128)S(1)}, f32[12]{0:T(128)}, u32[]{:S(2)}) copy-start(f32[12]{0:T(128)} %param.6) | copy-start | bytes 148

commit v13 on v11

--- a/solution.py
+++ b/solution.py
@@ -349,10 +349,10 @@
 
 
 def radix_plan(count):
-    plan = [list(range(1, min(4, count - 1) + 1))]
+    plan = [list(range(1, min(8, count - 1) + 1))]
     span = len(plan[0])
     while span < count - 1:
-        offsets = [span * j for j in range(1, 4) if span * j < count]
+        offsets = [span * j for j in range(1, 8) if span * j < count]
         plan.append(offsets)
         span = span * (1 + len(offsets))
     return plan

time: 135 us -> 170 us (1.26)
  the two profiles are of different devices: /device:TPU:6 before, /device:TPU:8 now
where the time goes in v13:
time: 170 us
  Pallas kernels  138 us (81%)
  local copies, waits for them, and re-layouts  14.6 us (9%)
  starting transfers between devices  11.4 us (7%)
  other arithmetic  4.95 us (3%)
    pallas_call x1, Pallas kernels, carry_solve(): pl.pallas_call(functools.partial(carry_kernel, count, rows_here), out_sha...  102 us
    pallas_call x1, Pallas kernels, coefficient_table(): pl.pallas_call(functools.partial(prefix_kernel, count, team_size(count),...  34.9 us
    ppermute x2, starting transfers between devices, extended(): before = lax.ppermute(last, axis, up)  5.81 us
    ppermute x2, starting transfers between devices, extended(): after = lax.ppermute(first, axis, down)  5.57 us
    slice x6, local copies, waits for them, and re-layouts, roll_slope(): jnp.roll(values, -offset, along_axis) - jnp.roll(values, offset, along_axis)  5.16 us
    transpose x1, other arithmetic, shards(): jnp.transpose(forcing, (1, 0, 2, 3)).reshape(rows_here, LINES, 128)  4.95 us
  transfers between devices with their start and end apart: 4, of which 0 were waited for; matrix products, arithmetic and copies ran while one was open for 6% of the time, Pallas kernels for 21%

profile of v13, /device:TPU:8, one launch (start us, length us, event | category | flops | bytes accessed | tf_op | source)
XLA Modules:
  0.0 169.9 jit_solution(16414662673126358656)
XLA Ops:
  0.6 1.5 fusion.33
  2.1 0.4 copy.15
  2.5 3.4 %collective-permute-start.1 = (f32[3,12,32,4]{2,1,3,0:T(8,128)S(1)}, f32[3,12,32,4]{2,1,3,0:T(8,128)S(1)}, u32[]{:S(2)}, u32[]{:S(2)}) collective-permute-start(f32[3,12,32,4]{2,1,3,0:T(8,128)S(1)} %copy.15), channel_id=1, source_target_pairs={{0,128},{128,256},{256,384},{384,0},{1,129},{129,257},{257,385},{3... | collective-permute-start | bytes 55304 | tf_op jit(solution)/shard_map/ppermute | solution.py:28
  5.9 0.4 copy.14
  6.3 3.7 %collective-permute-start = (f32[3,12,32,4]{2,1,3,0:T(8,128)S(1)}, f32[3,12,32,4]{2,1,3,0:T(8,128)}, u32[]{:S(2)}, u32[]{:S(2)}) collective-permute-start(f32[3,12,32,4]{2,1,3,0:T(8,128)S(1)} %copy.14), channel_id=1, source_target_pairs={{128,0},{256,128},{384,256},{0,384},{129,1},{257,129},{385,257},{1... | collective-permute-start | bytes 55304 | tf_op jit(solution)/shard_map/ppermute | solution.py:29
  9.9 0.6 fusion.34
  10.6 1.9 %collective-permute-start.2 = (f32[3,1,32,128]{3,2,1,0:T(8,128)}, f32[3,1,32,128]{3,2,1,0:T(8,128)}, u32[]{:S(2)}, u32[]{:S(2)}) collective-permute-start(f32[3,1,32,128]{3,2,1,0:T(8,128)} %get-tuple-element.13), channel_id=1, source_target_pairs={{1,0},{2,1},{3,2},{4,3},{5,4},{6,5},{7,6},{8,7},{9,8},{10,9},{11,1... | collective-permute-start | bytes 147464 | tf_op jit(solution)/shard_map/ppermute | solution.py:29
  12.5 2.4 %collective-permute-start.3 = (f32[3,1,32,128]{3,2,1,0:T(8,128)}, f32[3,1,32,128]{3,2,1,0:T(8,128)}, u32[]{:S(2)}, u32[]{:S(2)}) collective-permute-start(f32[3,1,32,128]{3,2,1,0:T(8,128)} %get-tuple-element.14), channel_id=1, source_target_pairs={{0,1},{1,2},{2,3},{3,4},{4,5},{5,6},{6,7},{7,8},{8,9},{9,10},{10,1... | collective-permute-start | bytes 147464 | tf_op jit(solution)/shard_map/ppermute | solution.py:28
  14.9 0.8 slice_bitcast_fusion.2
  15.9 0.9 fusion.37
  16.8 1.1 fusion.39
  17.9 1.1 fusion.41
  19.0 0.7 fusion.40
  19.7 0.7 fusion.42
  20.4 0.6 fusion.38
  21.0 0.6 fusion.36
  21.8 0.7 broadcast_in_dim.2.table_ref.given_ref
  22.5 1.4 shard_map.59.element_ref
  23.8 34.9 %shard_map.60.coef_ref = f32[48,128]{1,0:T(8,128)} custom-call(f32[8,128]{1,0:T(8,128)} %shard_map.59.element_ref, f32[48,128]{1,0:T(8,128)} %broadcast_in_dim.2.table_ref.given_ref), custom_call_target="tpu_custom_call" | custom-call | tf_op jit(solution)/shard_map/pallas_call | solution.py:303
  59.1 1.2 copy.9
  60.3 4.9 %add_bitcast_fusion = (f32[12,3,32,128]{3,2,0,1:T(8,128)S(1)}, f32[3,12,32,128]{3,2,1,0:T(8,128)}) fusion(f32[3,12,32,128]{3,2,1,0:T(8,128)} %param.5, f32[3,12,32,128]{3,2,1,0:T(8,128)S(1)} %copy-done, f32[3,12,28,128]{3,2,1,0:T(8,128)} %get-tuple-element.28, f32[3,12,4,128]{3,2,1,0:T(4,128)} %get-tuple-element.30, f32[3,12,4,128]{3,2,1,0:T(4,128)} %get-tuple-element.29, ...), kind=kLoop, calls=%fused_computation.53 | loop fusion | flops 7667712 | bytes 7802928 | tf_op jit(solution)/shard_map/transpose | solution.py:491
  65.2 0.9 copy.12
  66.1 101.9 %shard_map.61 = f32[12,96,128]{2,1,0:T(8,128)} custom-call(f32[12,96,128]{2,1,0:T(8,128)} %bitcast.13, f32[48,128]{1,0:T(8,128)} %broadcast_in_dim.2.table_ref.given_ref, f32[48,128]{1,0:T(8,128)} %shard_map.60.coef_ref), custom_call_target="tpu_custom_call" | custom-call | tf_op jit(solution)/shard_map/pallas_call | solution.py:455
  168.0 1.9 %copy.17 = f32[12,3,32,128]{3,2,0,1:T(8,128)} copy(f32[12,3,32,128]{3,2,1,0:T(8,128)} %bitcast.14) | data formatting | bytes 1179648 | tf_op jit(solution)/shard_map/reshape | solution.py:493
  (15 shorter events, 0.5 us)
Async XLA Ops:
  2.1 7.8 %copy-start = (f32[3,12,32,128]{3,2,1,0:T(8,128)S(1)}, f32[3,12,32,128]{3,2,1,0:T(8,128)}, u32[]{:S(2)}) copy-start(f32[3,12,32,128]{3,2,1,0:T(8,128)} %param.4) | copy-start | bytes 1769476
  2.5 56.3 %collective-permute-start.1 = (f32[3,12,32,4]{2,1,3,0:T(8,128)S(1)}, f32[3,12,32,4]{2,1,3,0:T(8,128)S(1)}, u32[]{:S(2)}, u32[]{:S(2)}) collective-permute-start(f32[3,12,32,4]{2,1,3,0:T(8,128)S(1)} %copy.15), channel_id=1, source_target_pairs={{0,128},{128,256},{256,384},{384,0},{1,129},{129,257},{257,385},{3... | collective-permute-start | bytes 55304 | tf_op jit(solution)/shard_map/ppermute | solution.py:28
  6.3 52.8 %collective-permute-start = (f32[3,12,32,4]{2,1,3,0:T(8,128)S(1)}, f32[3,12,32,4]{2,1,3,0:T(8,128)}, u32[]{:S(2)}, u32[]{:S(2)}) collective-permute-start(f32[3,12,32,4]{2,1,3,0:T(8,128)S(1)} %copy.14), channel_id=1, source_target_pairs={{128,0},{256,128},{384,256},{0,384},{129,1},{257,129},{385,257},{1... | collective-permute-start | bytes 55304 | tf_op jit(solution)/shard_map/ppermute | solution.py:29
  10.6 49.7 %collective-permute-start.2 = (f32[3,1,32,128]{3,2,1,0:T(8,128)}, f32[3,1,32,128]{3,2,1,0:T(8,128)}, u32[]{:S(2)}, u32[]{:S(2)}) collective-permute-start(f32[3,1,32,128]{3,2,1,0:T(8,128)} %get-tuple-element.13), channel_id=1, source_target_pairs={{1,0},{2,1},{3,2},{4,3},{5,4},{6,5},{7,6},{8,7},{9,8},{10,9},{11,1... | collective-permute-start | bytes 147464 | tf_op jit(solution)/shard_map/ppermute | solution.py:29
  12.5 47.8 %collective-permute-start.3 = (f32[3,1,32,128]{3,2,1,0:T(8,128)}, f32[3,1,32,128]{3,2,1,0:T(8,128)}, u32[]{:S(2)}, u32[]{:S(2)}) collective-permute-start(f32[3,1,32,128]{3,2,1,0:T(8,128)} %get-tuple-element.14), channel_id=1, source_target_pairs={{0,1},{1,2},{2,3},{3,4},{4,5},{5,6},{6,7},{7,8},{8,9},{9,10},{10,1... | collective-permute-start | bytes 147464 | tf_op jit(solution)/shard_map/ppermute | solution.py:28
  19.0 2.7 %copy-start.1 = (f32[12]{0:T(128)S(1)}, f32[12]{0:T(128)}, u32[]{:S(2)}) copy-start(f32[12]{0:T(128)} %param.7) | copy-start | bytes 148
  19.0 2.7 %copy-start.2 = (f32[12]{0:T(128)S(1)}, f32[12]{0:T(128)}, u32[]{:S(2)}) copy-start(f32[12]{0:T(128)} %param.6) | copy-start | bytes 148

commit v14 on v11

--- a/solution.py
+++ b/solution.py
@@ -412,8 +412,9 @@
     for i in range(rows_here):
         lower = given[i : i + 1]
         pivot = coef[i : i + 1]
-        carried = rows_ref[i] / pivot if carried is None else (rows_ref[i] - lower * carried) / pivot
-        out_ref[i] = carried
+        line = rows_ref[:, i].reshape(LINES, 128)
+        carried = line / pivot if carried is None else (line - lower * carried) / pivot
+        out_ref[:, i] = carried.reshape(out_ref.shape[0], out_ref.shape[2], 128)
     down_element[...] = jnp.concatenate(
         [carried, jnp.broadcast_to(coef[32 + rows_here - 1 : 32 + rows_here], (8, 128))], axis=0
     )
@@ -425,14 +426,14 @@
     for i in reversed(range(rows_here)):
         sensitivity = coef[32 + i : 33 + i]
         modified = coef[16 + i : 17 + i]
-        reduced = out_ref[i] + sensitivity * below_carry
+        reduced = out_ref[:, i].reshape(LINES, 128) + sensitivity * below_carry
         if carried is None:
             carried = reduced
             weight = -modified
         else:
             carried = reduced - modified * carried
             weight = -modified * weight
-        out_ref[i] = carried
+        out_ref[:, i] = carried.reshape(out_ref.shape[0], out_ref.shape[2], 128)
     up_element[...] = jnp.concatenate([carried, jnp.broadcast_to(weight, (8, 128))], axis=0)
     above_carry = radix_scan(
         me, row, count, True, up_element, parts_up, recv, send_sem, recv_sem, slots, copies
@@ -441,20 +442,21 @@
     for i in reversed(range(rows_here)):
         modified = coef[16 + i : 17 + i]
         weight = -modified if weight is None else -modified * weight
-        out_ref[i] = out_ref[i] + weight * above_carry
+        value = out_ref[:, i].reshape(LINES, 128) + weight * above_carry
+        out_ref[:, i] = value.reshape(out_ref.shape[0], out_ref.shape[2], 128)
     for copy in copies:
         copy.wait_send()
 
 
 def carry_solve(stacked, given, coef):
     count = lax.axis_size("gy")
-    rows_here = stacked.shape[0]
+    rows_here = stacked.shape[1]
     plan = radix_plan(count)
     slots = 2 * sum(len(offsets) for offsets in plan)
     big = (LINES + 8, 128)
     return pl.pallas_call(
         functools.partial(carry_kernel, count, rows_here),
-        out_shape=jax.ShapeDtypeStruct((rows_here, LINES, 128), jnp.float32),
+        out_shape=jax.ShapeDtypeStruct(stacked.shape, jnp.float32),
         in_specs=[pl.BlockSpec(memory_space=pltpu.VMEM)] * 3,
         out_specs=pl.BlockSpec(memory_space=pltpu.VMEM),
         scratch_shapes=[
@@ -488,9 +490,7 @@
     rows_here = velocity.shape[1]
 
     given, table = coefficient_table(lower_coef, upper_coef, diagonal)
-    stacked = jnp.transpose(forcing, (1, 0, 2, 3)).reshape(rows_here, LINES, 128)
-    solved = carry_solve(stacked, given, table)
-    finished = jnp.transpose(solved.reshape(rows_here, 3, 32, -1), (1, 0, 2, 3))
+    finished = carry_solve(forcing, given, table)
     return (finished.reshape(velocity.shape), advection)
 
 

time: 135 us -> 135 us (level)
    add x0 -> x1, other arithmetic: none -> 5.07 us  [shards(): forcing = velocity + GAMMA * advection + ZETA * old_advection]
    transpose x1 -> x0, other arithmetic: 4.95 us -> none  [shards(): jnp.transpose(forcing, (1, 0, 2, 3)).reshape(rows_here, LINES, 128)]
    reshape x1 -> x0, local copies, waits for them, and re-layouts: 1.92 us -> none  [shards(): finished = jnp.transpose(solved.reshape(rows_here, 3, 32, -1), (1, 0, 2, 3))]
    unnamed x8 -> x9, local copies, waits for them, and re-layouts: 0.75 us -> 2.5 us
where the time goes in v14:
time: 135 us; the launch traced here: 134 us
  Pallas kernels  100 us (74%)
  starting transfers between devices  14.6 us (11%)
  local copies, waits for them, and re-layouts  13.6 us (10%)
  other arithmetic  5.08 us (4%)
    pallas_call x1, Pallas kernels, carry_solve(): pl.pallas_call(functools.partial(carry_kernel, count, rows_here), out_sha...  65.9 us
    pallas_call x1, Pallas kernels, coefficient_table(): pl.pallas_call(functools.partial(prefix_kernel, count, team_size(count),...  32.7 us
    ppermute x2, starting transfers between devices, extended(): before = lax.ppermute(last, axis, up)  10.6 us
    slice x6, local copies, waits for them, and re-layouts, roll_slope(): jnp.roll(values, -offset, along_axis) - jnp.roll(values, offset, along_axis)  5.18 us
    add x1, other arithmetic, shards(): forcing = velocity + GAMMA * advection + ZETA * old_advection  5.07 us
    ppermute x2, starting transfers between devices, extended(): after = lax.ppermute(first, axis, down)  4.02 us
  transfers between devices with their start and end apart: 4, of which 0 were waited for; matrix products, arithmetic and copies ran while one was open for 7% of the time, Pallas kernels for 25%

profile of v14, /device:TPU:6, one launch (start us, length us, event | category | flops | bytes accessed | tf_op | source)
XLA Modules:
  0.0 134.0 jit_solution(6969767012397067975)
XLA Ops:
  0.6 1.5 %fusion.33 = (f32[3,12,32,4]{3,2,1,0:T(8,128)S(1)}, f32[3,12,32,4]{3,2,1,0:T(8,128)S(1)}) fusion(f32[3,12,32,128]{3,2,1,0:T(8,128)} %param.4), kind=kLoop, calls=%fused_computation.59 | loop fusion | bytes 73728 | tf_op jit(solution)/shard_map/slice | solution.py:27
  2.1 0.3 copy.10
  2.4 2.7 %collective-permute-start = (f32[3,12,32,4]{2,3,1,0:T(4,128)S(1)}, f32[3,12,32,4]{2,3,1,0:T(4,128)S(1)}, u32[]{:S(2)}, u32[]{:S(2)}) collective-permute-start(f32[3,12,32,4]{2,3,1,0:T(4,128)S(1)} %copy.10), channel_id=1, source_target_pairs={{128,0},{256,128},{384,256},{0,384},{129,1},{257,129},{385,257},{1... | collective-permute-start | bytes 55304 | tf_op jit(solution)/shard_map/ppermute | solution.py:29
  5.1 0.3 copy.11
  5.4 6.9 %collective-permute-start.1 = (f32[3,12,32,4]{2,3,1,0:T(4,128)S(1)}, f32[3,12,32,4]{2,3,1,0:T(4,128)}, u32[]{:S(2)}, u32[]{:S(2)}) collective-permute-start(f32[3,12,32,4]{2,3,1,0:T(4,128)S(1)} %copy.11), channel_id=1, source_target_pairs={{0,128},{128,256},{256,384},{384,0},{1,129},{129,257},{257,385},{3... | collective-permute-start | bytes 55304 | tf_op jit(solution)/shard_map/ppermute | solution.py:28
  12.4 0.6 fusion.34
  13.0 1.3 collective-permute-start.2
  14.3 3.7 %collective-permute-start.3 = (f32[3,1,32,128]{3,2,1,0:T(8,128)}, f32[3,1,32,128]{3,2,1,0:T(8,128)}, u32[]{:S(2)}, u32[]{:S(2)}) collective-permute-start(f32[3,1,32,128]{3,2,1,0:T(8,128)} %get-tuple-element.14), channel_id=1, source_target_pairs={{0,1},{1,2},{2,3},{3,4},{4,5},{5,6},{6,7},{7,8},{8,9},{9,10},{10,1... | collective-permute-start | bytes 147464 | tf_op jit(solution)/shard_map/ppermute | solution.py:28
  18.0 0.8 slice_bitcast_fusion.2
  18.9 0.9 fusion.37
  19.8 1.1 fusion.39
  21.0 1.1 fusion.41
  22.1 0.7 fusion.40
  22.8 0.7 fusion.42
  23.5 0.7 fusion.38
  24.1 0.6 fusion.36
  24.9 0.7 broadcast_in_dim.2.table_ref.given_ref
  25.5 1.4 %shard_map.59.element_ref = f32[8,128]{1,0:T(8,128)} custom-call(f32[48,128]{1,0:T(8,128)} %broadcast_in_dim.2.table_ref.given_ref), custom_call_target="tpu_custom_call" | custom-call | tf_op jit(solution)/shard_map/pallas_call | solution.py:297
  26.9 32.7 %shard_map.60.coef_ref = f32[48,128]{1,0:T(8,128)} custom-call(f32[8,128]{1,0:T(8,128)} %shard_map.59.element_ref, f32[48,128]{1,0:T(8,128)} %broadcast_in_dim.2.table_ref.given_ref), custom_call_target="tpu_custom_call" | custom-call | tf_op jit(solution)/shard_map/pallas_call | solution.py:303
  59.6 0.3 copy.7
  59.9 1.2 copy.9
  61.1 5.1 %multiply_add_fusion = (f32[3,12,32,128]{3,2,1,0:T(8,128)}, f32[3,12,32,128]{3,2,1,0:T(8,128)}) fusion(f32[3,12,32,128]{3,2,1,0:T(8,128)} %param.5, f32[3,12,32,128]{3,2,1,0:T(8,128)S(1)} %copy-done, f32[3,12,28,128]{3,2,1,0:T(8,128)} %get-tuple-element.28, f32[3,12,4,128]{3,2,1,0:T(4,128)} %get-tuple-element.30, f32[3,12,4,128]{3,2,1,0:T(4,128)} %get-tuple-element.29, ...), kind=kLoop, calls=%fused_computation.52 | loop fusion | flops 7667712 | bytes 7802928 | tf_op jit(solution)/shard_map/add | solution.py:486
  66.2 65.9 %shard_map.61 = f32[3,12,32,128]{3,2,1,0:T(8,128)} custom-call(f32[3,12,32,128]{3,2,1,0:T(8,128)} %get-tuple-element.6.rows_ref, f32[48,128]{1,0:T(8,128)} %broadcast_in_dim.2.table_ref.given_ref, f32[48,128]{1,0:T(8,128)} %shard_map.60.coef_ref), custom_call_target="tpu_custom_call" | custom-call | tf_op jit(solution)/shard_map/pallas_call | solution.py:457
  132.1 1.9 %copy.13 = f32[3,12,32,128]{3,2,1,0:T(8,128)} copy(f32[3,12,32,128]{3,2,1,0:T(8,128)} %shard_map.61) | data formatting | bytes 1179648
  (14 shorter events, 0.2 us)
Async XLA Ops:
  2.1 10.3 %copy-start = (f32[3,12,32,128]{3,2,1,0:T(8,128)S(1)}, f32[3,12,32,128]{3,2,1,0:T(8,128)}, u32[]{:S(2)}) copy-start(f32[3,12,32,128]{3,2,1,0:T(8,128)} %param.4) | copy-start | bytes 1769476
  2.4 57.2 %collective-permute-start = (f32[3,12,32,4]{2,3,1,0:T(4,128)S(1)}, f32[3,12,32,4]{2,3,1,0:T(4,128)S(1)}, u32[]{:S(2)}, u32[]{:S(2)}) collective-permute-start(f32[3,12,32,4]{2,3,1,0:T(4,128)S(1)} %copy.10), channel_id=1, source_target_pairs={{128,0},{256,128},{384,256},{0,384},{129,1},{257,129},{385,257},{1... | collective-permute-start | bytes 55304 | tf_op jit(solution)/shard_map/ppermute | solution.py:29
  5.4 54.5 %collective-permute-start.1 = (f32[3,12,32,4]{2,3,1,0:T(4,128)S(1)}, f32[3,12,32,4]{2,3,1,0:T(4,128)}, u32[]{:S(2)}, u32[]{:S(2)}) collective-permute-start(f32[3,12,32,4]{2,3,1,0:T(4,128)S(1)} %copy.11), channel_id=1, source_target_pairs={{0,128},{128,256},{256,384},{384,0},{1,129},{129,257},{257,385},{3... | collective-permute-start | bytes 55304 | tf_op jit(solution)/shard_map/ppermute | solution.py:28
  13.0 48.1 %collective-permute-start.2 = (f32[3,1,32,128]{3,2,1,0:T(8,128)}, f32[3,1,32,128]{3,2,1,0:T(8,128)}, u32[]{:S(2)}, u32[]{:S(2)}) collective-permute-start(f32[3,1,32,128]{3,2,1,0:T(8,128)} %get-tuple-element.13), channel_id=1, source_target_pairs={{1,0},{2,1},{3,2},{4,3},{5,4},{6,5},{7,6},{8,7},{9,8},{10,9},{11,1... | collective-permute-start | bytes 147464 | tf_op jit(solution)/shard_map/ppermute | solution.py:29
  14.3 46.8 %collective-permute-start.3 = (f32[3,1,32,128]{3,2,1,0:T(8,128)}, f32[3,1,32,128]{3,2,1,0:T(8,128)}, u32[]{:S(2)}, u32[]{:S(2)}) collective-permute-start(f32[3,1,32,128]{3,2,1,0:T(8,128)} %get-tuple-element.14), channel_id=1, source_target_pairs={{0,1},{1,2},{2,3},{3,4},{4,5},{5,6},{6,7},{7,8},{8,9},{9,10},{10,1... | collective-permute-start | bytes 147464 | tf_op jit(solution)/shard_map/ppermute | solution.py:28
  22.1 2.7 %copy-start.1 = (f32[12]{0:T(128)S(1)}, f32[12]{0:T(128)}, u32[]{:S(2)}) copy-start(f32[12]{0:T(128)} %param.7) | copy-start | bytes 148
  22.1 2.7 %copy-start.2 = (f32[12]{0:T(128)S(1)}, f32[12]{0:T(128)}, u32[]{:S(2)}) copy-start(f32[12]{0:T(128)} %param.6) | copy-start | bytes 148

commit v15 on v14

--- a/solution.py
+++ b/solution.py
@@ -349,10 +349,10 @@
 
 
 def radix_plan(count):
-    plan = [list(range(1, min(4, count - 1) + 1))]
+    plan = [list(range(1, min(2, count - 1) + 1))]
     span = len(plan[0])
     while span < count - 1:
-        offsets = [span * j for j in range(1, 4) if span * j < count]
+        offsets = [span * j for j in range(1, 2) if span * j < count]
         plan.append(offsets)
         span = span * (1 + len(offsets))
     return plan

time: 135 us -> 137 us (1.015)
  Pallas kernels: 100 us -> 102 us
    pallas_call x1, Pallas kernels: 65.9 us -> 68.4 us  [carry_solve(): pl.pallas_call(functools.partial(carry_kernel, count, rows_here), out_sha...]
where the time goes in v15:
time: 137 us
  Pallas kernels  102 us (74%)
  starting transfers between devices  14.6 us (11%)
  local copies, waits for them, and re-layouts  13.6 us (10%)
  other arithmetic  5.08 us (4%)
    pallas_call x1, Pallas kernels, carry_solve(): pl.pallas_call(functools.partial(carry_kernel, count, rows_here), out_sha...  68.4 us
    pallas_call x1, Pallas kernels, coefficient_table(): pl.pallas_call(functools.partial(prefix_kernel, count, team_size(count),...  32.7 us
    ppermute x2, starting transfers between devices, extended(): before = lax.ppermute(last, axis, up)  10.6 us
    slice x6, local copies, waits for them, and re-layouts, roll_slope(): jnp.roll(values, -offset, along_axis) - jnp.roll(values, offset, along_axis)  5.18 us
    add x1, other arithmetic, shards(): forcing = velocity + GAMMA * advection + ZETA * old_advection  5.07 us
    ppermute x2, starting transfers between devices, extended(): after = lax.ppermute(first, axis, down)  4.02 us
  transfers between devices with their start and end apart: 4, of which 0 were waited for; matrix products, arithmetic and copies ran while one was open for 7% of the time, Pallas kernels for 25%

profile of v15, /device:TPU:6, one launch (start us, length us, event | category | flops | bytes accessed | tf_op | source)
XLA Modules:
  0.0 136.5 jit_solution(11301546853049371094)
XLA Ops:
  0.6 1.5 %fusion.33 = (f32[3,12,32,4]{3,2,1,0:T(8,128)S(1)}, f32[3,12,32,4]{3,2,1,0:T(8,128)S(1)}) fusion(f32[3,12,32,128]{3,2,1,0:T(8,128)} %param.4), kind=kLoop, calls=%fused_computation.59 | loop fusion | bytes 73728 | tf_op jit(solution)/shard_map/slice | solution.py:27
  2.1 0.3 copy.10
  2.4 2.7 %collective-permute-start = (f32[3,12,32,4]{2,3,1,0:T(4,128)S(1)}, f32[3,12,32,4]{2,3,1,0:T(4,128)S(1)}, u32[]{:S(2)}, u32[]{:S(2)}) collective-permute-start(f32[3,12,32,4]{2,3,1,0:T(4,128)S(1)} %copy.10), channel_id=1, source_target_pairs={{128,0},{256,128},{384,256},{0,384},{129,1},{257,129},{385,257},{1... | collective-permute-start | bytes 55304 | tf_op jit(solution)/shard_map/ppermute | solution.py:29
  5.1 0.3 copy.11
  5.4 6.9 %collective-permute-start.1 = (f32[3,12,32,4]{2,3,1,0:T(4,128)S(1)}, f32[3,12,32,4]{2,3,1,0:T(4,128)}, u32[]{:S(2)}, u32[]{:S(2)}) collective-permute-start(f32[3,12,32,4]{2,3,1,0:T(4,128)S(1)} %copy.11), channel_id=1, source_target_pairs={{0,128},{128,256},{256,384},{384,0},{1,129},{129,257},{257,385},{3... | collective-permute-start | bytes 55304 | tf_op jit(solution)/shard_map/ppermute | solution.py:28
  12.4 0.6 fusion.34
  13.0 1.3 collective-permute-start.2
  14.3 3.7 %collective-permute-start.3 = (f32[3,1,32,128]{3,2,1,0:T(8,128)}, f32[3,1,32,128]{3,2,1,0:T(8,128)}, u32[]{:S(2)}, u32[]{:S(2)}) collective-permute-start(f32[3,1,32,128]{3,2,1,0:T(8,128)} %get-tuple-element.14), channel_id=1, source_target_pairs={{0,1},{1,2},{2,3},{3,4},{4,5},{5,6},{6,7},{7,8},{8,9},{9,10},{10,1... | collective-permute-start | bytes 147464 | tf_op jit(solution)/shard_map/ppermute | solution.py:28
  18.0 0.8 slice_bitcast_fusion.2
  18.9 0.9 fusion.37
  19.8 1.1 fusion.39
  21.0 1.1 fusion.41
  22.1 0.7 fusion.40
  22.8 0.7 fusion.42
  23.5 0.7 fusion.38
  24.1 0.6 fusion.36
  24.9 0.7 broadcast_in_dim.2.table_ref.given_ref
  25.5 1.4 %shard_map.59.element_ref = f32[8,128]{1,0:T(8,128)} custom-call(f32[48,128]{1,0:T(8,128)} %broadcast_in_dim.2.table_ref.given_ref), custom_call_target="tpu_custom_call" | custom-call | tf_op jit(solution)/shard_map/pallas_call | solution.py:297
  26.9 32.7 %shard_map.60.coef_ref = f32[48,128]{1,0:T(8,128)} custom-call(f32[8,128]{1,0:T(8,128)} %shard_map.59.element_ref, f32[48,128]{1,0:T(8,128)} %broadcast_in_dim.2.table_ref.given_ref), custom_call_target="tpu_custom_call" | custom-call | tf_op jit(solution)/shard_map/pallas_call | solution.py:303
  59.6 0.3 copy.7
  59.9 1.2 copy.9
  61.1 5.1 %multiply_add_fusion = (f32[3,12,32,128]{3,2,1,0:T(8,128)}, f32[3,12,32,128]{3,2,1,0:T(8,128)}) fusion(f32[3,12,32,128]{3,2,1,0:T(8,128)} %param.5, f32[3,12,32,128]{3,2,1,0:T(8,128)S(1)} %copy-done, f32[3,12,28,128]{3,2,1,0:T(8,128)} %get-tuple-element.28, f32[3,12,4,128]{3,2,1,0:T(4,128)} %get-tuple-element.30, f32[3,12,4,128]{3,2,1,0:T(4,128)} %get-tuple-element.29, ...), kind=kLoop, calls=%fused_computation.52 | loop fusion | flops 7667712 | bytes 7802928 | tf_op jit(solution)/shard_map/add | solution.py:486
  66.2 68.4 %shard_map.61 = f32[3,12,32,128]{3,2,1,0:T(8,128)} custom-call(f32[3,12,32,128]{3,2,1,0:T(8,128)} %get-tuple-element.6.rows_ref, f32[48,128]{1,0:T(8,128)} %broadcast_in_dim.2.table_ref.given_ref, f32[48,128]{1,0:T(8,128)} %shard_map.60.coef_ref), custom_call_target="tpu_custom_call" | custom-call | tf_op jit(solution)/shard_map/pallas_call | solution.py:457
  134.6 1.9 %copy.13 = f32[3,12,32,128]{3,2,1,0:T(8,128)} copy(f32[3,12,32,128]{3,2,1,0:T(8,128)} %shard_map.61) | data formatting | bytes 1179648
  (14 shorter events, 0.2 us)
Async XLA Ops:
  2.1 10.3 %copy-start = (f32[3,12,32,128]{3,2,1,0:T(8,128)S(1)}, f32[3,12,32,128]{3,2,1,0:T(8,128)}, u32[]{:S(2)}) copy-start(f32[3,12,32,128]{3,2,1,0:T(8,128)} %param.4) | copy-start | bytes 1769476
  2.4 57.2 %collective-permute-start = (f32[3,12,32,4]{2,3,1,0:T(4,128)S(1)}, f32[3,12,32,4]{2,3,1,0:T(4,128)S(1)}, u32[]{:S(2)}, u32[]{:S(2)}) collective-permute-start(f32[3,12,32,4]{2,3,1,0:T(4,128)S(1)} %copy.10), channel_id=1, source_target_pairs={{128,0},{256,128},{384,256},{0,384},{129,1},{257,129},{385,257},{1... | collective-permute-start | bytes 55304 | tf_op jit(solution)/shard_map/ppermute | solution.py:29
  5.4 54.5 %collective-permute-start.1 = (f32[3,12,32,4]{2,3,1,0:T(4,128)S(1)}, f32[3,12,32,4]{2,3,1,0:T(4,128)}, u32[]{:S(2)}, u32[]{:S(2)}) collective-permute-start(f32[3,12,32,4]{2,3,1,0:T(4,128)S(1)} %copy.11), channel_id=1, source_target_pairs={{0,128},{128,256},{256,384},{384,0},{1,129},{129,257},{257,385},{3... | collective-permute-start | bytes 55304 | tf_op jit(solution)/shard_map/ppermute | solution.py:28
  13.0 48.1 %collective-permute-start.2 = (f32[3,1,32,128]{3,2,1,0:T(8,128)}, f32[3,1,32,128]{3,2,1,0:T(8,128)}, u32[]{:S(2)}, u32[]{:S(2)}) collective-permute-start(f32[3,1,32,128]{3,2,1,0:T(8,128)} %get-tuple-element.13), channel_id=1, source_target_pairs={{1,0},{2,1},{3,2},{4,3},{5,4},{6,5},{7,6},{8,7},{9,8},{10,9},{11,1... | collective-permute-start | bytes 147464 | tf_op jit(solution)/shard_map/ppermute | solution.py:29
  14.3 46.8 %collective-permute-start.3 = (f32[3,1,32,128]{3,2,1,0:T(8,128)}, f32[3,1,32,128]{3,2,1,0:T(8,128)}, u32[]{:S(2)}, u32[]{:S(2)}) collective-permute-start(f32[3,1,32,128]{3,2,1,0:T(8,128)} %get-tuple-element.14), channel_id=1, source_target_pairs={{0,1},{1,2},{2,3},{3,4},{4,5},{5,6},{6,7},{7,8},{8,9},{9,10},{10,1... | collective-permute-start | bytes 147464 | tf_op jit(solution)/shard_map/ppermute | solution.py:28
  22.1 2.7 %copy-start.1 = (f32[12]{0:T(128)S(1)}, f32[12]{0:T(128)}, u32[]{:S(2)}) copy-start(f32[12]{0:T(128)} %param.7) | copy-start | bytes 148
  22.1 2.7 %copy-start.2 = (f32[12]{0:T(128)S(1)}, f32[12]{0:T(128)}, u32[]{:S(2)}) copy-start(f32[12]{0:T(128)} %param.6) | copy-start | bytes 148

commit v16 on v14

--- a/solution.py
+++ b/solution.py
@@ -262,8 +262,8 @@
 
 
 def team_size(count):
-    if count > 16 and count % 16 == 0:
-        return 16
+    if count > 32 and count % 32 == 0:
+        return 32
     return max(1, count // 2)
 
 

time: 135 us -> 137 us (1.015)
  Pallas kernels: 100 us -> 102 us
    pallas_call x1, Pallas kernels: 65.9 us -> 67.6 us  [carry_solve(): pl.pallas_call(functools.partial(carry_kernel, count, rows_here), out_sha...]
where the time goes in v16:
time: 137 us; the launch traced here: 136 us
  Pallas kernels  102 us (74%)
  starting transfers between devices  14.6 us (11%)
  local copies, waits for them, and re-layouts  13.6 us (10%)
  other arithmetic  5.08 us (4%)
    pallas_call x1, Pallas kernels, carry_solve(): pl.pallas_call(functools.partial(carry_kernel, count, rows_here), out_sha...  67.6 us
    pallas_call x1, Pallas kernels, coefficient_table(): pl.pallas_call(functools.partial(prefix_kernel, count, team_size(count),...  33.4 us
    ppermute x2, starting transfers between devices, extended(): before = lax.ppermute(last, axis, up)  10.6 us
    slice x6, local copies, waits for them, and re-layouts, roll_slope(): jnp.roll(values, -offset, along_axis) - jnp.roll(values, offset, along_axis)  5.18 us
    add x1, other arithmetic, shards(): forcing = velocity + GAMMA * advection + ZETA * old_advection  5.07 us
    ppermute x2, starting transfers between devices, extended(): after = lax.ppermute(first, axis, down)  4.02 us
  transfers between devices with their start and end apart: 4, of which 0 were waited for; matrix products, arithmetic and copies ran while one was open for 7% of the time, Pallas kernels for 25%

profile of v16, /device:TPU:6, one launch (start us, length us, event | category | flops | bytes accessed | tf_op | source)
XLA Modules:
  0.0 136.4 jit_solution(1455262895661604094)
XLA Ops:
  0.6 1.5 %fusion.33 = (f32[3,12,32,4]{3,2,1,0:T(8,128)S(1)}, f32[3,12,32,4]{3,2,1,0:T(8,128)S(1)}) fusion(f32[3,12,32,128]{3,2,1,0:T(8,128)} %param.4), kind=kLoop, calls=%fused_computation.59 | loop fusion | bytes 73728 | tf_op jit(solution)/shard_map/slice | solution.py:27
  2.1 0.3 copy.10
  2.4 2.7 %collective-permute-start = (f32[3,12,32,4]{2,3,1,0:T(4,128)S(1)}, f32[3,12,32,4]{2,3,1,0:T(4,128)S(1)}, u32[]{:S(2)}, u32[]{:S(2)}) collective-permute-start(f32[3,12,32,4]{2,3,1,0:T(4,128)S(1)} %copy.10), channel_id=1, source_target_pairs={{128,0},{256,128},{384,256},{0,384},{129,1},{257,129},{385,257},{1... | collective-permute-start | bytes 55304 | tf_op jit(solution)/shard_map/ppermute | solution.py:29
  5.1 0.3 copy.11
  5.4 6.9 %collective-permute-start.1 = (f32[3,12,32,4]{2,3,1,0:T(4,128)S(1)}, f32[3,12,32,4]{2,3,1,0:T(4,128)}, u32[]{:S(2)}, u32[]{:S(2)}) collective-permute-start(f32[3,12,32,4]{2,3,1,0:T(4,128)S(1)} %copy.11), channel_id=1, source_target_pairs={{0,128},{128,256},{256,384},{384,0},{1,129},{129,257},{257,385},{3... | collective-permute-start | bytes 55304 | tf_op jit(solution)/shard_map/ppermute | solution.py:28
  12.4 0.6 fusion.34
  13.0 1.3 collective-permute-start.2
  14.3 3.7 %collective-permute-start.3 = (f32[3,1,32,128]{3,2,1,0:T(8,128)}, f32[3,1,32,128]{3,2,1,0:T(8,128)}, u32[]{:S(2)}, u32[]{:S(2)}) collective-permute-start(f32[3,1,32,128]{3,2,1,0:T(8,128)} %get-tuple-element.14), channel_id=1, source_target_pairs={{0,1},{1,2},{2,3},{3,4},{4,5},{5,6},{6,7},{7,8},{8,9},{9,10},{10,1... | collective-permute-start | bytes 147464 | tf_op jit(solution)/shard_map/ppermute | solution.py:28
  18.0 0.8 slice_bitcast_fusion.2
  18.9 0.9 fusion.37
  19.8 1.1 fusion.39
  21.0 1.1 fusion.41
  22.1 0.7 fusion.40
  22.8 0.7 fusion.42
  23.5 0.7 fusion.38
  24.1 0.6 fusion.36
  24.9 0.7 broadcast_in_dim.2.table_ref.given_ref
  25.5 1.4 %shard_map.59.element_ref = f32[8,128]{1,0:T(8,128)} custom-call(f32[48,128]{1,0:T(8,128)} %broadcast_in_dim.2.table_ref.given_ref), custom_call_target="tpu_custom_call" | custom-call | tf_op jit(solution)/shard_map/pallas_call | solution.py:297
  26.9 33.4 %shard_map.60.coef_ref = f32[48,128]{1,0:T(8,128)} custom-call(f32[8,128]{1,0:T(8,128)} %shard_map.59.element_ref, f32[48,128]{1,0:T(8,128)} %broadcast_in_dim.2.table_ref.given_ref), custom_call_target="tpu_custom_call" | custom-call | tf_op jit(solution)/shard_map/pallas_call | solution.py:303
  60.3 0.3 copy.7
  60.6 1.2 copy.9
  61.8 5.1 %multiply_add_fusion = (f32[3,12,32,128]{3,2,1,0:T(8,128)}, f32[3,12,32,128]{3,2,1,0:T(8,128)}) fusion(f32[3,12,32,128]{3,2,1,0:T(8,128)} %param.5, f32[3,12,32,128]{3,2,1,0:T(8,128)S(1)} %copy-done, f32[3,12,28,128]{3,2,1,0:T(8,128)} %get-tuple-element.28, f32[3,12,4,128]{3,2,1,0:T(4,128)} %get-tuple-element.30, f32[3,12,4,128]{3,2,1,0:T(4,128)} %get-tuple-element.29, ...), kind=kLoop, calls=%fused_computation.52 | loop fusion | flops 7667712 | bytes 7802928 | tf_op jit(solution)/shard_map/add | solution.py:486
  66.9 67.6 %shard_map.61 = f32[3,12,32,128]{3,2,1,0:T(8,128)} custom-call(f32[3,12,32,128]{3,2,1,0:T(8,128)} %get-tuple-element.6.rows_ref, f32[48,128]{1,0:T(8,128)} %broadcast_in_dim.2.table_ref.given_ref, f32[48,128]{1,0:T(8,128)} %shard_map.60.coef_ref), custom_call_target="tpu_custom_call" | custom-call | tf_op jit(solution)/shard_map/pallas_call | solution.py:457
  134.5 1.9 %copy.13 = f32[3,12,32,128]{3,2,1,0:T(8,128)} copy(f32[3,12,32,128]{3,2,1,0:T(8,128)} %shard_map.61) | data formatting | bytes 1179648
  (14 shorter events, 0.2 us)
Async XLA Ops:
  2.1 10.3 %copy-start = (f32[3,12,32,128]{3,2,1,0:T(8,128)S(1)}, f32[3,12,32,128]{3,2,1,0:T(8,128)}, u32[]{:S(2)}) copy-start(f32[3,12,32,128]{3,2,1,0:T(8,128)} %param.4) | copy-start | bytes 1769476
  2.4 57.9 %collective-permute-start = (f32[3,12,32,4]{2,3,1,0:T(4,128)S(1)}, f32[3,12,32,4]{2,3,1,0:T(4,128)S(1)}, u32[]{:S(2)}, u32[]{:S(2)}) collective-permute-start(f32[3,12,32,4]{2,3,1,0:T(4,128)S(1)} %copy.10), channel_id=1, source_target_pairs={{128,0},{256,128},{384,256},{0,384},{129,1},{257,129},{385,257},{1... | collective-permute-start | bytes 55304 | tf_op jit(solution)/shard_map/ppermute | solution.py:29
  5.4 55.2 %collective-permute-start.1 = (f32[3,12,32,4]{2,3,1,0:T(4,128)S(1)}, f32[3,12,32,4]{2,3,1,0:T(4,128)}, u32[]{:S(2)}, u32[]{:S(2)}) collective-permute-start(f32[3,12,32,4]{2,3,1,0:T(4,128)S(1)} %copy.11), channel_id=1, source_target_pairs={{0,128},{128,256},{256,384},{384,0},{1,129},{129,257},{257,385},{3... | collective-permute-start | bytes 55304 | tf_op jit(solution)/shard_map/ppermute | solution.py:28
  13.0 48.8 %collective-permute-start.2 = (f32[3,1,32,128]{3,2,1,0:T(8,128)}, f32[3,1,32,128]{3,2,1,0:T(8,128)}, u32[]{:S(2)}, u32[]{:S(2)}) collective-permute-start(f32[3,1,32,128]{3,2,1,0:T(8,128)} %get-tuple-element.13), channel_id=1, source_target_pairs={{1,0},{2,1},{3,2},{4,3},{5,4},{6,5},{7,6},{8,7},{9,8},{10,9},{11,1... | collective-permute-start | bytes 147464 | tf_op jit(solution)/shard_map/ppermute | solution.py:29
  14.3 47.5 %collective-permute-start.3 = (f32[3,1,32,128]{3,2,1,0:T(8,128)}, f32[3,1,32,128]{3,2,1,0:T(8,128)}, u32[]{:S(2)}, u32[]{:S(2)}) collective-permute-start(f32[3,1,32,128]{3,2,1,0:T(8,128)} %get-tuple-element.14), channel_id=1, source_target_pairs={{0,1},{1,2},{2,3},{3,4},{4,5},{5,6},{6,7},{7,8},{8,9},{9,10},{10,1... | collective-permute-start | bytes 147464 | tf_op jit(solution)/shard_map/ppermute | solution.py:28
  22.1 2.7 %copy-start.1 = (f32[12]{0:T(128)S(1)}, f32[12]{0:T(128)}, u32[]{:S(2)}) copy-start(f32[12]{0:T(128)} %param.7) | copy-start | bytes 148
  22.1 2.7 %copy-start.2 = (f32[12]{0:T(128)S(1)}, f32[12]{0:T(128)}, u32[]{:S(2)}) copy-start(f32[12]{0:T(128)} %param.6) | copy-start | bytes 148

commit v17 on v16

--- a/solution.py
+++ b/solution.py
@@ -262,8 +262,8 @@
 
 
 def team_size(count):
-    if count > 32 and count % 32 == 0:
-        return 32
+    if count > 8 and count % 8 == 0:
+        return 8
     return max(1, count // 2)
 
 

time: 137 us -> 143 us (1.044)
  Pallas kernels: 102 us -> 108 us
    pallas_call x1, Pallas kernels: 33.4 us -> 37 us  [coefficient_table(): pl.pallas_call(functools.partial(prefix_kernel, count, team_size(count),...]
    pallas_call x1, Pallas kernels: 67.6 us -> 69.7 us  [carry_solve(): pl.pallas_call(functools.partial(carry_kernel, count, rows_here), out_sha...]
  transfers between devices with their start and end apart: 4 -> 4, of which waited for: 0 -> 0; matrix products, arithmetic and copies ran while one was open for 7% -> 7% of each run, Pallas kernels for 25% -> 27%
where the time goes in v17:
time: 143 us; the launch traced here: 142 us
  Pallas kernels  108 us (76%)
  starting transfers between devices  14.6 us (10%)
  local copies, waits for them, and re-layouts  13.6 us (10%)
  other arithmetic  5.08 us (4%)
    pallas_call x1, Pallas kernels, carry_solve(): pl.pallas_call(functools.partial(carry_kernel, count, rows_here), out_sha...  69.7 us
    pallas_call x1, Pallas kernels, coefficient_table(): pl.pallas_call(functools.partial(prefix_kernel, count, team_size(count),...  37 us
    ppermute x2, starting transfers between devices, extended(): before = lax.ppermute(last, axis, up)  10.6 us
    slice x6, local copies, waits for them, and re-layouts, roll_slope(): jnp.roll(values, -offset, along_axis) - jnp.roll(values, offset, along_axis)  5.18 us
    add x1, other arithmetic, shards(): forcing = velocity + GAMMA * advection + ZETA * old_advection  5.07 us
    ppermute x2, starting transfers between devices, extended(): after = lax.ppermute(first, axis, down)  4.02 us
  transfers between devices with their start and end apart: 4, of which 0 were waited for; matrix products, arithmetic and copies ran while one was open for 7% of the time, Pallas kernels for 27%

profile of v17, /device:TPU:6, one launch (start us, length us, event | category | flops | bytes accessed | tf_op | source)
XLA Modules:
  0.0 142.1 jit_solution(496002494818151880)
XLA Ops:
  0.6 1.5 %fusion.33 = (f32[3,12,32,4]{3,2,1,0:T(8,128)S(1)}, f32[3,12,32,4]{3,2,1,0:T(8,128)S(1)}) fusion(f32[3,12,32,128]{3,2,1,0:T(8,128)} %param.4), kind=kLoop, calls=%fused_computation.59 | loop fusion | bytes 73728 | tf_op jit(solution)/shard_map/slice | solution.py:27
  2.1 0.3 copy.10
  2.4 2.7 %collective-permute-start = (f32[3,12,32,4]{2,3,1,0:T(4,128)S(1)}, f32[3,12,32,4]{2,3,1,0:T(4,128)S(1)}, u32[]{:S(2)}, u32[]{:S(2)}) collective-permute-start(f32[3,12,32,4]{2,3,1,0:T(4,128)S(1)} %copy.10), channel_id=1, source_target_pairs={{128,0},{256,128},{384,256},{0,384},{129,1},{257,129},{385,257},{1... | collective-permute-start | bytes 55304 | tf_op jit(solution)/shard_map/ppermute | solution.py:29
  5.1 0.3 copy.11
  5.4 6.9 %collective-permute-start.1 = (f32[3,12,32,4]{2,3,1,0:T(4,128)S(1)}, f32[3,12,32,4]{2,3,1,0:T(4,128)}, u32[]{:S(2)}, u32[]{:S(2)}) collective-permute-start(f32[3,12,32,4]{2,3,1,0:T(4,128)S(1)} %copy.11), channel_id=1, source_target_pairs={{0,128},{128,256},{256,384},{384,0},{1,129},{129,257},{257,385},{3... | collective-permute-start | bytes 55304 | tf_op jit(solution)/shard_map/ppermute | solution.py:28
  12.4 0.6 fusion.34
  13.0 1.3 collective-permute-start.2
  14.3 3.7 %collective-permute-start.3 = (f32[3,1,32,128]{3,2,1,0:T(8,128)}, f32[3,1,32,128]{3,2,1,0:T(8,128)}, u32[]{:S(2)}, u32[]{:S(2)}) collective-permute-start(f32[3,1,32,128]{3,2,1,0:T(8,128)} %get-tuple-element.14), channel_id=1, source_target_pairs={{0,1},{1,2},{2,3},{3,4},{4,5},{5,6},{6,7},{7,8},{8,9},{9,10},{10,1... | collective-permute-start | bytes 147464 | tf_op jit(solution)/shard_map/ppermute | solution.py:28
  18.0 0.8 slice_bitcast_fusion.2
  18.9 0.9 fusion.37
  19.8 1.1 fusion.39
  21.0 1.1 fusion.41
  22.1 0.7 fusion.40
  22.8 0.7 fusion.42
  23.5 0.7 fusion.38
  24.1 0.6 fusion.36
  24.9 0.7 broadcast_in_dim.2.table_ref.given_ref
  25.5 1.4 shard_map.59.element_ref
  26.9 37.0 %shard_map.60.coef_ref = f32[48,128]{1,0:T(8,128)} custom-call(f32[8,128]{1,0:T(8,128)} %shard_map.59.element_ref, f32[48,128]{1,0:T(8,128)} %broadcast_in_dim.2.table_ref.given_ref), custom_call_target="tpu_custom_call" | custom-call | tf_op jit(solution)/shard_map/pallas_call | solution.py:303
  63.9 0.3 copy.7
  64.2 1.2 copy.9
  65.4 5.1 %multiply_add_fusion = (f32[3,12,32,128]{3,2,1,0:T(8,128)}, f32[3,12,32,128]{3,2,1,0:T(8,128)}) fusion(f32[3,12,32,128]{3,2,1,0:T(8,128)} %param.5, f32[3,12,32,128]{3,2,1,0:T(8,128)S(1)} %copy-done, f32[3,12,28,128]{3,2,1,0:T(8,128)} %get-tuple-element.28, f32[3,12,4,128]{3,2,1,0:T(4,128)} %get-tuple-element.30, f32[3,12,4,128]{3,2,1,0:T(4,128)} %get-tuple-element.29, ...), kind=kLoop, calls=%fused_computation.52 | loop fusion | flops 7667712 | bytes 7802928 | tf_op jit(solution)/shard_map/add | solution.py:486
  70.5 69.7 %shard_map.61 = f32[3,12,32,128]{3,2,1,0:T(8,128)} custom-call(f32[3,12,32,128]{3,2,1,0:T(8,128)} %get-tuple-element.6.rows_ref, f32[48,128]{1,0:T(8,128)} %broadcast_in_dim.2.table_ref.given_ref, f32[48,128]{1,0:T(8,128)} %shard_map.60.coef_ref), custom_call_target="tpu_custom_call" | custom-call | tf_op jit(solution)/shard_map/pallas_call | solution.py:457
  140.2 1.9 %copy.13 = f32[3,12,32,128]{3,2,1,0:T(8,128)} copy(f32[3,12,32,128]{3,2,1,0:T(8,128)} %shard_map.61) | data formatting | bytes 1179648
  (14 shorter events, 0.2 us)
Async XLA Ops:
  2.1 10.3 %copy-start = (f32[3,12,32,128]{3,2,1,0:T(8,128)S(1)}, f32[3,12,32,128]{3,2,1,0:T(8,128)}, u32[]{:S(2)}) copy-start(f32[3,12,32,128]{3,2,1,0:T(8,128)} %param.4) | copy-start | bytes 1769476
  2.4 61.5 %collective-permute-start = (f32[3,12,32,4]{2,3,1,0:T(4,128)S(1)}, f32[3,12,32,4]{2,3,1,0:T(4,128)S(1)}, u32[]{:S(2)}, u32[]{:S(2)}) collective-permute-start(f32[3,12,32,4]{2,3,1,0:T(4,128)S(1)} %copy.10), channel_id=1, source_target_pairs={{128,0},{256,128},{384,256},{0,384},{129,1},{257,129},{385,257},{1... | collective-permute-start | bytes 55304 | tf_op jit(solution)/shard_map/ppermute | solution.py:29
  5.4 58.8 %collective-permute-start.1 = (f32[3,12,32,4]{2,3,1,0:T(4,128)S(1)}, f32[3,12,32,4]{2,3,1,0:T(4,128)}, u32[]{:S(2)}, u32[]{:S(2)}) collective-permute-start(f32[3,12,32,4]{2,3,1,0:T(4,128)S(1)} %copy.11), channel_id=1, source_target_pairs={{0,128},{128,256},{256,384},{384,0},{1,129},{129,257},{257,385},{3... | collective-permute-start | bytes 55304 | tf_op jit(solution)/shard_map/ppermute | solution.py:28
  13.0 52.4 %collective-permute-start.2 = (f32[3,1,32,128]{3,2,1,0:T(8,128)}, f32[3,1,32,128]{3,2,1,0:T(8,128)}, u32[]{:S(2)}, u32[]{:S(2)}) collective-permute-start(f32[3,1,32,128]{3,2,1,0:T(8,128)} %get-tuple-element.13), channel_id=1, source_target_pairs={{1,0},{2,1},{3,2},{4,3},{5,4},{6,5},{7,6},{8,7},{9,8},{10,9},{11,1... | collective-permute-start | bytes 147464 | tf_op jit(solution)/shard_map/ppermute | solution.py:29
  14.3 51.1 %collective-permute-start.3 = (f32[3,1,32,128]{3,2,1,0:T(8,128)}, f32[3,1,32,128]{3,2,1,0:T(8,128)}, u32[]{:S(2)}, u32[]{:S(2)}) collective-permute-start(f32[3,1,32,128]{3,2,1,0:T(8,128)} %get-tuple-element.14), channel_id=1, source_target_pairs={{0,1},{1,2},{2,3},{3,4},{4,5},{5,6},{6,7},{7,8},{8,9},{9,10},{10,1... | collective-permute-start | bytes 147464 | tf_op jit(solution)/shard_map/ppermute | solution.py:28
  22.1 2.7 %copy-start.1 = (f32[12]{0:T(128)S(1)}, f32[12]{0:T(128)}, u32[]{:S(2)}) copy-start(f32[12]{0:T(128)} %param.7) | copy-start | bytes 148
  22.1 2.7 %copy-start.2 = (f32[12]{0:T(128)S(1)}, f32[12]{0:T(128)}, u32[]{:S(2)}) copy-start(f32[12]{0:T(128)} %param.6) | copy-start | bytes 148

commit v18 on v15

--- a/solution.py
+++ b/solution.py
@@ -349,10 +349,10 @@
 
 
 def radix_plan(count):
-    plan = [list(range(1, min(2, count - 1) + 1))]
+    plan = [list(range(1, min(3, count - 1) + 1))]
     span = len(plan[0])
     while span < count - 1:
-        offsets = [span * j for j in range(1, 2) if span * j < count]
+        offsets = [span * j for j in range(1, 3) if span * j < count]
         plan.append(offsets)
         span = span * (1 + len(offsets))
     return plan

time: 137 us -> 141 us (1.029); the launches traced: 137 us -> 139 us
  Pallas kernels: 102 us -> 105 us
    pallas_call x1, Pallas kernels: 68.4 us -> 70.9 us  [carry_solve(): pl.pallas_call(functools.partial(carry_kernel, count, rows_here), out_sha...]
where the time goes in v18:
time: 141 us; the launch traced here: 139 us
  Pallas kernels  105 us (74%)
  starting transfers between devices  14.6 us (10%)
  local copies, waits for them, and re-layouts  13.6 us (10%)
  other arithmetic  5.08 us (4%)
    pallas_call x1, Pallas kernels, carry_solve(): pl.pallas_call(functools.partial(carry_kernel, count, rows_here), out_sha...  70.9 us
    pallas_call x1, Pallas kernels, coefficient_table(): pl.pallas_call(functools.partial(prefix_kernel, count, team_size(count),...  32.7 us
    ppermute x2, starting transfers between devices, extended(): before = lax.ppermute(last, axis, up)  10.6 us
    slice x6, local copies, waits for them, and re-layouts, roll_slope(): jnp.roll(values, -offset, along_axis) - jnp.roll(values, offset, along_axis)  5.18 us
    add x1, other arithmetic, shards(): forcing = velocity + GAMMA * advection + ZETA * old_advection  5.07 us
    ppermute x2, starting transfers between devices, extended(): after = lax.ppermute(first, axis, down)  4.02 us
  transfers between devices with their start and end apart: 4, of which 0 were waited for; matrix products, arithmetic and copies ran while one was open for 7% of the time, Pallas kernels for 25%

profile of v18, /device:TPU:6, one launch (start us, length us, event | category | flops | bytes accessed | tf_op | source)
XLA Modules:
  0.0 139.0 jit_solution(9444987415607672794)
XLA Ops:
  0.6 1.5 %fusion.33 = (f32[3,12,32,4]{3,2,1,0:T(8,128)S(1)}, f32[3,12,32,4]{3,2,1,0:T(8,128)S(1)}) fusion(f32[3,12,32,128]{3,2,1,0:T(8,128)} %param.4), kind=kLoop, calls=%fused_computation.59 | loop fusion | bytes 73728 | tf_op jit(solution)/shard_map/slice | solution.py:27
  2.1 0.3 copy.10
  2.4 2.7 %collective-permute-start = (f32[3,12,32,4]{2,3,1,0:T(4,128)S(1)}, f32[3,12,32,4]{2,3,1,0:T(4,128)S(1)}, u32[]{:S(2)}, u32[]{:S(2)}) collective-permute-start(f32[3,12,32,4]{2,3,1,0:T(4,128)S(1)} %copy.10), channel_id=1, source_target_pairs={{128,0},{256,128},{384,256},{0,384},{129,1},{257,129},{385,257},{1... | collective-permute-start | bytes 55304 | tf_op jit(solution)/shard_map/ppermute | solution.py:29
  5.1 0.3 copy.11
  5.4 6.9 %collective-permute-start.1 = (f32[3,12,32,4]{2,3,1,0:T(4,128)S(1)}, f32[3,12,32,4]{2,3,1,0:T(4,128)}, u32[]{:S(2)}, u32[]{:S(2)}) collective-permute-start(f32[3,12,32,4]{2,3,1,0:T(4,128)S(1)} %copy.11), channel_id=1, source_target_pairs={{0,128},{128,256},{256,384},{384,0},{1,129},{129,257},{257,385},{3... | collective-permute-start | bytes 55304 | tf_op jit(solution)/shard_map/ppermute | solution.py:28
  12.4 0.6 fusion.34
  13.0 1.3 collective-permute-start.2
  14.3 3.7 %collective-permute-start.3 = (f32[3,1,32,128]{3,2,1,0:T(8,128)}, f32[3,1,32,128]{3,2,1,0:T(8,128)}, u32[]{:S(2)}, u32[]{:S(2)}) collective-permute-start(f32[3,1,32,128]{3,2,1,0:T(8,128)} %get-tuple-element.14), channel_id=1, source_target_pairs={{0,1},{1,2},{2,3},{3,4},{4,5},{5,6},{6,7},{7,8},{8,9},{9,10},{10,1... | collective-permute-start | bytes 147464 | tf_op jit(solution)/shard_map/ppermute | solution.py:28
  18.0 0.8 slice_bitcast_fusion.2
  18.9 0.9 fusion.37
  19.8 1.1 fusion.39
  21.0 1.1 fusion.41
  22.1 0.7 fusion.40
  22.8 0.7 fusion.42
  23.5 0.7 fusion.38
  24.1 0.6 fusion.36
  24.9 0.7 broadcast_in_dim.2.table_ref.given_ref
  25.5 1.4 shard_map.59.element_ref
  26.9 32.7 %shard_map.60.coef_ref = f32[48,128]{1,0:T(8,128)} custom-call(f32[8,128]{1,0:T(8,128)} %shard_map.59.element_ref, f32[48,128]{1,0:T(8,128)} %broadcast_in_dim.2.table_ref.given_ref), custom_call_target="tpu_custom_call" | custom-call | tf_op jit(solution)/shard_map/pallas_call | solution.py:303
  59.6 0.3 copy.7
  59.9 1.2 copy.9
  61.1 5.1 %multiply_add_fusion = (f32[3,12,32,128]{3,2,1,0:T(8,128)}, f32[3,12,32,128]{3,2,1,0:T(8,128)}) fusion(f32[3,12,32,128]{3,2,1,0:T(8,128)} %param.5, f32[3,12,32,128]{3,2,1,0:T(8,128)S(1)} %copy-done, f32[3,12,28,128]{3,2,1,0:T(8,128)} %get-tuple-element.28, f32[3,12,4,128]{3,2,1,0:T(4,128)} %get-tuple-element.30, f32[3,12,4,128]{3,2,1,0:T(4,128)} %get-tuple-element.29, ...), kind=kLoop, calls=%fused_computation.52 | loop fusion | flops 7667712 | bytes 7802928 | tf_op jit(solution)/shard_map/add | solution.py:486
  66.2 70.9 %shard_map.61 = f32[3,12,32,128]{3,2,1,0:T(8,128)} custom-call(f32[3,12,32,128]{3,2,1,0:T(8,128)} %get-tuple-element.6.rows_ref, f32[48,128]{1,0:T(8,128)} %broadcast_in_dim.2.table_ref.given_ref, f32[48,128]{1,0:T(8,128)} %shard_map.60.coef_ref), custom_call_target="tpu_custom_call" | custom-call | tf_op jit(solution)/shard_map/pallas_call | solution.py:457
  137.1 1.9 %copy.13 = f32[3,12,32,128]{3,2,1,0:T(8,128)} copy(f32[3,12,32,128]{3,2,1,0:T(8,128)} %shard_map.61) | data formatting | bytes 1179648
  (14 shorter events, 0.2 us)
Async XLA Ops:
  2.1 10.3 %copy-start = (f32[3,12,32,128]{3,2,1,0:T(8,128)S(1)}, f32[3,12,32,128]{3,2,1,0:T(8,128)}, u32[]{:S(2)}) copy-start(f32[3,12,32,128]{3,2,1,0:T(8,128)} %param.4) | copy-start | bytes 1769476
  2.4 57.2 %collective-permute-start = (f32[3,12,32,4]{2,3,1,0:T(4,128)S(1)}, f32[3,12,32,4]{2,3,1,0:T(4,128)S(1)}, u32[]{:S(2)}, u32[]{:S(2)}) collective-permute-start(f32[3,12,32,4]{2,3,1,0:T(4,128)S(1)} %copy.10), channel_id=1, source_target_pairs={{128,0},{256,128},{384,256},{0,384},{129,1},{257,129},{385,257},{1... | collective-permute-start | bytes 55304 | tf_op jit(solution)/shard_map/ppermute | solution.py:29
  5.4 54.5 %collective-permute-start.1 = (f32[3,12,32,4]{2,3,1,0:T(4,128)S(1)}, f32[3,12,32,4]{2,3,1,0:T(4,128)}, u32[]{:S(2)}, u32[]{:S(2)}) collective-permute-start(f32[3,12,32,4]{2,3,1,0:T(4,128)S(1)} %copy.11), channel_id=1, source_target_pairs={{0,128},{128,256},{256,384},{384,0},{1,129},{129,257},{257,385},{3... | collective-permute-start | bytes 55304 | tf_op jit(solution)/shard_map/ppermute | solution.py:28
  13.0 48.1 %collective-permute-start.2 = (f32[3,1,32,128]{3,2,1,0:T(8,128)}, f32[3,1,32,128]{3,2,1,0:T(8,128)}, u32[]{:S(2)}, u32[]{:S(2)}) collective-permute-start(f32[3,1,32,128]{3,2,1,0:T(8,128)} %get-tuple-element.13), channel_id=1, source_target_pairs={{1,0},{2,1},{3,2},{4,3},{5,4},{6,5},{7,6},{8,7},{9,8},{10,9},{11,1... | collective-permute-start | bytes 147464 | tf_op jit(solution)/shard_map/ppermute | solution.py:29
  14.3 46.8 %collective-permute-start.3 = (f32[3,1,32,128]{3,2,1,0:T(8,128)}, f32[3,1,32,128]{3,2,1,0:T(8,128)}, u32[]{:S(2)}, u32[]{:S(2)}) collective-permute-start(f32[3,1,32,128]{3,2,1,0:T(8,128)} %get-tuple-element.14), channel_id=1, source_target_pairs={{0,1},{1,2},{2,3},{3,4},{4,5},{5,6},{6,7},{7,8},{8,9},{9,10},{10,1... | collective-permute-start | bytes 147464 | tf_op jit(solution)/shard_map/ppermute | solution.py:28
  22.1 2.7 %copy-start.1 = (f32[12]{0:T(128)S(1)}, f32[12]{0:T(128)}, u32[]{:S(2)}) copy-start(f32[12]{0:T(128)} %param.7) | copy-start | bytes 148
  22.1 2.7 %copy-start.2 = (f32[12]{0:T(128)S(1)}, f32[12]{0:T(128)}, u32[]{:S(2)}) copy-start(f32[12]{0:T(128)} %param.6) | copy-start | bytes 148

commit v19 on v15

--- a/solution.py
+++ b/solution.py
@@ -349,7 +349,7 @@
 
 
 def radix_plan(count):
-    plan = [list(range(1, min(2, count - 1) + 1))]
+    plan = [list(range(1, min(4, count - 1) + 1))]
     span = len(plan[0])
     while span < count - 1:
         offsets = [span * j for j in range(1, 2) if span * j < count]

time: 137 us -> 137 us (level)
  the two profiles are of different devices: /device:TPU:6 before, /device:TPU:22 now
where the time goes in v19:
time: 137 us; the launch traced here: 136 us
  Pallas kernels  105 us (77%)
  local copies, waits for them, and re-layouts  13.6 us (10%)
  starting transfers between devices  11.4 us (8%)
  other arithmetic  5.08 us (4%)
    pallas_call x1, Pallas kernels, carry_solve(): pl.pallas_call(functools.partial(carry_kernel, count, rows_here), out_sha...  69.1 us
    pallas_call x1, Pallas kernels, coefficient_table(): pl.pallas_call(functools.partial(prefix_kernel, count, team_size(count),...  35 us
    ppermute x2, starting transfers between devices, extended(): before = lax.ppermute(last, axis, up)  6.73 us
    slice x6, local copies, waits for them, and re-layouts, roll_slope(): jnp.roll(values, -offset, along_axis) - jnp.roll(values, offset, along_axis)  5.18 us
    add x1, other arithmetic, shards(): forcing = velocity + GAMMA * advection + ZETA * old_advection  5.07 us
    ppermute x2, starting transfers between devices, extended(): after = lax.ppermute(first, axis, down)  4.65 us
  transfers between devices with their start and end apart: 4, of which 0 were waited for; matrix products, arithmetic and copies ran while one was open for 7% of the time, Pallas kernels for 27%

profile of v19, /device:TPU:22, one launch (start us, length us, event | category | flops | bytes accessed | tf_op | source)
XLA Modules:
  0.0 136.3 jit_solution(4661250059168857881)
XLA Ops:
  0.6 1.5 %fusion.33 = (f32[3,12,32,4]{3,2,1,0:T(8,128)S(1)}, f32[3,12,32,4]{3,2,1,0:T(8,128)S(1)}) fusion(f32[3,12,32,128]{3,2,1,0:T(8,128)} %param.4), kind=kLoop, calls=%fused_computation.59 | loop fusion | bytes 73728 | tf_op jit(solution)/shard_map/slice | solution.py:27
  2.1 0.3 copy.10
  2.4 2.7 %collective-permute-start = (f32[3,12,32,4]{2,3,1,0:T(4,128)S(1)}, f32[3,12,32,4]{2,3,1,0:T(4,128)S(1)}, u32[]{:S(2)}, u32[]{:S(2)}) collective-permute-start(f32[3,12,32,4]{2,3,1,0:T(4,128)S(1)} %copy.10), channel_id=1, source_target_pairs={{128,0},{256,128},{384,256},{0,384},{129,1},{257,129},{385,257},{1... | collective-permute-start | bytes 55304 | tf_op jit(solution)/shard_map/ppermute | solution.py:29
  5.1 0.3 copy.11
  5.4 4.3 %collective-permute-start.1 = (f32[3,12,32,4]{2,3,1,0:T(4,128)S(1)}, f32[3,12,32,4]{2,3,1,0:T(4,128)}, u32[]{:S(2)}, u32[]{:S(2)}) collective-permute-start(f32[3,12,32,4]{2,3,1,0:T(4,128)S(1)} %copy.11), channel_id=1, source_target_pairs={{0,128},{128,256},{256,384},{384,0},{1,129},{129,257},{257,385},{3... | collective-permute-start | bytes 55304 | tf_op jit(solution)/shard_map/ppermute | solution.py:28
  9.8 0.6 fusion.34
  10.4 1.9 %collective-permute-start.2 = (f32[3,1,32,128]{3,2,1,0:T(8,128)}, f32[3,1,32,128]{3,2,1,0:T(8,128)}, u32[]{:S(2)}, u32[]{:S(2)}) collective-permute-start(f32[3,1,32,128]{3,2,1,0:T(8,128)} %get-tuple-element.13), channel_id=1, source_target_pairs={{1,0},{2,1},{3,2},{4,3},{5,4},{6,5},{7,6},{8,7},{9,8},{10,9},{11,1... | collective-permute-start | bytes 147464 | tf_op jit(solution)/shard_map/ppermute | solution.py:29
  12.3 2.4 %collective-permute-start.3 = (f32[3,1,32,128]{3,2,1,0:T(8,128)}, f32[3,1,32,128]{3,2,1,0:T(8,128)}, u32[]{:S(2)}, u32[]{:S(2)}) collective-permute-start(f32[3,1,32,128]{3,2,1,0:T(8,128)} %get-tuple-element.14), channel_id=1, source_target_pairs={{0,1},{1,2},{2,3},{3,4},{4,5},{5,6},{6,7},{7,8},{8,9},{9,10},{10,1... | collective-permute-start | bytes 147464 | tf_op jit(solution)/shard_map/ppermute | solution.py:28
  14.7 0.8 slice_bitcast_fusion.2
  15.7 0.9 fusion.37
  16.6 1.1 fusion.39
  17.7 1.1 fusion.41
  18.8 0.7 fusion.40
  19.5 0.7 fusion.42
  20.2 0.7 fusion.38
  20.9 0.6 fusion.36
  21.6 0.7 broadcast_in_dim.2.table_ref.given_ref
  22.3 1.4 %shard_map.59.element_ref = f32[8,128]{1,0:T(8,128)} custom-call(f32[48,128]{1,0:T(8,128)} %broadcast_in_dim.2.table_ref.given_ref), custom_call_target="tpu_custom_call" | custom-call | tf_op jit(solution)/shard_map/pallas_call | solution.py:297
  23.6 35.0 %shard_map.60.coef_ref = f32[48,128]{1,0:T(8,128)} custom-call(f32[8,128]{1,0:T(8,128)} %shard_map.59.element_ref, f32[48,128]{1,0:T(8,128)} %broadcast_in_dim.2.table_ref.given_ref), custom_call_target="tpu_custom_call" | custom-call | tf_op jit(solution)/shard_map/pallas_call | solution.py:303
  58.7 0.3 copy.7
  59.0 1.2 copy.9
  60.1 5.1 %multiply_add_fusion = (f32[3,12,32,128]{3,2,1,0:T(8,128)}, f32[3,12,32,128]{3,2,1,0:T(8,128)}) fusion(f32[3,12,32,128]{3,2,1,0:T(8,128)} %param.5, f32[3,12,32,128]{3,2,1,0:T(8,128)S(1)} %copy-done, f32[3,12,28,128]{3,2,1,0:T(8,128)} %get-tuple-element.28, f32[3,12,4,128]{3,2,1,0:T(4,128)} %get-tuple-element.30, f32[3,12,4,128]{3,2,1,0:T(4,128)} %get-tuple-element.29, ...), kind=kLoop, calls=%fused_computation.52 | loop fusion | flops 7667712 | bytes 7802928 | tf_op jit(solution)/shard_map/add | solution.py:486
  65.2 69.1 %shard_map.61 = f32[3,12,32,128]{3,2,1,0:T(8,128)} custom-call(f32[3,12,32,128]{3,2,1,0:T(8,128)} %get-tuple-element.6.rows_ref, f32[48,128]{1,0:T(8,128)} %broadcast_in_dim.2.table_ref.given_ref, f32[48,128]{1,0:T(8,128)} %shard_map.60.coef_ref), custom_call_target="tpu_custom_call" | custom-call | tf_op jit(solution)/shard_map/pallas_call | solution.py:457
  134.3 1.9 %copy.13 = f32[3,12,32,128]{3,2,1,0:T(8,128)} copy(f32[3,12,32,128]{3,2,1,0:T(8,128)} %shard_map.61) | data formatting | bytes 1179648
  (14 shorter events, 0.2 us)
Async XLA Ops:
  2.1 7.7 %copy-start = (f32[3,12,32,128]{3,2,1,0:T(8,128)S(1)}, f32[3,12,32,128]{3,2,1,0:T(8,128)}, u32[]{:S(2)}) copy-start(f32[3,12,32,128]{3,2,1,0:T(8,128)} %param.4) | copy-start | bytes 1769476
  2.4 56.3 %collective-permute-start = (f32[3,12,32,4]{2,3,1,0:T(4,128)S(1)}, f32[3,12,32,4]{2,3,1,0:T(4,128)S(1)}, u32[]{:S(2)}, u32[]{:S(2)}) collective-permute-start(f32[3,12,32,4]{2,3,1,0:T(4,128)S(1)} %copy.10), channel_id=1, source_target_pairs={{128,0},{256,128},{384,256},{0,384},{129,1},{257,129},{385,257},{1... | collective-permute-start | bytes 55304 | tf_op jit(solution)/shard_map/ppermute | solution.py:29
  5.4 53.5 %collective-permute-start.1 = (f32[3,12,32,4]{2,3,1,0:T(4,128)S(1)}, f32[3,12,32,4]{2,3,1,0:T(4,128)}, u32[]{:S(2)}, u32[]{:S(2)}) collective-permute-start(f32[3,12,32,4]{2,3,1,0:T(4,128)S(1)} %copy.11), channel_id=1, source_target_pairs={{0,128},{128,256},{256,384},{384,0},{1,129},{129,257},{257,385},{3... | collective-permute-start | bytes 55304 | tf_op jit(solution)/shard_map/ppermute | solution.py:28
  10.4 49.7 %collective-permute-start.2 = (f32[3,1,32,128]{3,2,1,0:T(8,128)}, f32[3,1,32,128]{3,2,1,0:T(8,128)}, u32[]{:S(2)}, u32[]{:S(2)}) collective-permute-start(f32[3,1,32,128]{3,2,1,0:T(8,128)} %get-tuple-element.13), channel_id=1, source_target_pairs={{1,0},{2,1},{3,2},{4,3},{5,4},{6,5},{7,6},{8,7},{9,8},{10,9},{11,1... | collective-permute-start | bytes 147464 | tf_op jit(solution)/shard_map/ppermute | solution.py:29
  12.3 47.8 %collective-permute-start.3 = (f32[3,1,32,128]{3,2,1,0:T(8,128)}, f32[3,1,32,128]{3,2,1,0:T(8,128)}, u32[]{:S(2)}, u32[]{:S(2)}) collective-permute-start(f32[3,1,32,128]{3,2,1,0:T(8,128)} %get-tuple-element.14), channel_id=1, source_target_pairs={{0,1},{1,2},{2,3},{3,4},{4,5},{5,6},{6,7},{7,8},{8,9},{9,10},{10,1... | collective-permute-start | bytes 147464 | tf_op jit(solution)/shard_map/ppermute | solution.py:28
  18.8 2.7 %copy-start.1 = (f32[12]{0:T(128)S(1)}, f32[12]{0:T(128)}, u32[]{:S(2)}) copy-start(f32[12]{0:T(128)} %param.7) | copy-start | bytes 148
  18.8 2.7 %copy-start.2 = (f32[12]{0:T(128)S(1)}, f32[12]{0:T(128)}, u32[]{:S(2)}) copy-start(f32[12]{0:T(128)} %param.6) | copy-start | bytes 148
